TPU v7x, 32 devices: a whole 2x2x4 slice. The times are simulated.
32 devices in a mesh: dp: 4 (over y, core), tp: 8 (over z, x).
Axes of the slice: x: 2, y: 2, z: 4, core: 2. Of those that a mesh axis runs over, the one named last changes fastest.
Arguments:
- teacher_partial: bfloat16 [8, 512, 4608], P('tp', 'dp'), may hold values from -5 to 5
- teacher_residual: bfloat16 [512, 4608], P(('dp', 'tp')), may hold values from -120 to 120
- post_gain: float32 [4608], replicated, may hold values from 0.5 to 1.5
- final_gain: float32 [4608], replicated, may hold values from 0.5 to 1.5
- teacher_head: bfloat16 [4608, 32768], P(None, ('dp', 'tp')), may hold values from -40 to 40
- student_hidden: bfloat16 [512, 3584], P(('dp', 'tp')), may hold values from -120 to 120
- student_gain: float32 [3584], replicated, may hold values from 0.5 to 1.5
- student_head: bfloat16 [3584, 32768], P(None, ('dp', 'tp')), may hold values from -40 to 40
- labels: int32 [512], P('dp'), may hold values from 0 to 32767
- lengths: int32 [4, 8], P('dp'), may hold values from 1 to 48, 96 in all within a row
Outputs:
- grad_hidden: float32 [512, 3584], P(('dp', 'tp'))
- token_loss: float32 [512], P(('dp', 'tp'))
Inputs may be any that keep to these rules, and one draw needn't show every extreme that they name: `lengths`: group g's 8 sequences fill, in order, its first 96 rows; its remaining 128 - 96 rows are padding.
All inputs are finite; a program needn't handle non-finite values.
Results may differ from a plain program's by a relative error of at most 0.03.
Values may be sent and summed in bfloat16 or wider, within the bound.
No kernel may reach another device: no remote copies, remote signals or barrier semaphores. Data moves between devices by JAX's collectives and lax.ppermute only.
A program may use at most 128 MiB of HBM per device.

v0:
```python
import functools

import jax
import jax.numpy as jnp
from jax import lax
from jax.experimental import pallas as pl
from jax.experimental.pallas import tpu as pltpu
from jax.sharding import PartitionSpec as P


EPS = 1e-06
BETA = 0.5
LOSS_SCALE = 1024.0
LIVE = 96
F32 = jnp.float32
BF16 = jnp.bfloat16
AXES = ("dp", "tp")


class Grid:
    def __init__(self, dp, tp, share):
        assert dp == 4 and tp % 2 == 0
        self.tp, self.depth = tp, tp // 2
        self.live = LIVE // (2 * share)
        assert self.live * 2 * share == LIVE
        dp_at, tp_at = lax.axis_index("dp"), lax.axis_index("tp")
        self.y, self.c = dp_at // 2, dp_at % 2
        self.z, self.x = tp_at // 2, tp_at % 2
        self.tiled = share % 16 == 0
        self.ids = jnp.stack([self.y, self.c, self.z, self.x, dp_at * tp + tp_at])

    def send(self, value, a=0, b=0, k=0, d=0, source=None, target=None):
        pairs = []
        for dp_at in range(4):
            for tp_at in range(self.tp):
                z = tp_at // 2
                if source is not None and z >= source:
                    continue
                if target is not None and (z ^ k) >= target:
                    continue
                to = (dp_at ^ (2 * a + b)) * self.tp + (tp_at ^ (2 * k + d))
                pairs.append((dp_at * self.tp + tp_at, to))
        return lax.ppermute(value, AXES, pairs)


def pick(pieces, index):
    bit = 0
    while len(pieces) > 1:
        high = (index >> bit) & 1
        pieces = [jnp.where(high == 1, pieces[i + 1], pieces[i]) for i in range(0, len(pieces), 2)]
        bit += 1
    return pieces[0]


def norm_rows(values, gain):
    inverse = lax.rsqrt(jnp.mean(values * values, axis=-1, keepdims=True) + EPS)
    return (values * inverse * gain, inverse)


VMEM = pl.BlockSpec(memory_space=pltpu.VMEM)
SMEM = pl.BlockSpec(memory_space=pltpu.SMEM)
shape_of = pltpu.VMEM
MIB = 1 << 20


def call(kernel, ids, args, outs, scratch, mib):
    args = [pltpu.with_memory_space_constraint(arg, pltpu.VMEM) for arg in args]
    return pl.pallas_call(
        kernel,
        out_shape=outs,
        in_specs=[SMEM] + [VMEM] * len(args),
        out_specs=[VMEM] * len(outs),
        scratch_shapes=scratch,
        compiler_params=pltpu.CompilerParams(vmem_limit_bytes=mib * MIB),
    )(ids, *args)


def pick_kernel(live, ids, *refs):
    pieces, out = refs[:-1], refs[-1]
    share = pieces[0].shape[0]
    for j in range(live):
        for k, piece in enumerate(pieces):

            @pl.when((ids[2] ^ j) == k)
            def _(j=j, piece=piece):
                out[j * share : (j + 1) * share, :] = piece[...]


def pair_kernel(live, ids, partial, other, own, *lows):
    share = own.shape[0]

    def chunk(slot):
        slot = jnp.minimum(slot, live - 1)
        at = pl.multiple_of((2 * slot + ids[3]) * share, share)
        return partial[0, pl.ds(at, share), :].astype(F32) + other[slot].astype(F32)

    own[...] = chunk(ids[2])
    for k, low in enumerate(lows, 1):
        low[...] = chunk(ids[2] ^ k).astype(BF16)


def norm_kernel(ids, *refs):
    own, others = refs[0], refs[1:-4]
    residual, post_gain, final_gain, out = refs[-4:]
    total = own[...]
    for other in others:
        total = total + other[...].astype(F32)
    post, _ = norm_rows(total, post_gain[...])
    final = residual[...].astype(F32) + post
    out[...] = norm_rows(final, final_gain[...])[0].astype(BF16)


def gather_depth(grid, rows):
    pieces = [rows] + [grid.send(rows, k=k, source=grid.live) for k in range(1, grid.depth)]
    if not grid.tiled:
        return jnp.concatenate([pick(pieces, grid.z ^ j) for j in range(grid.live)], axis=0)
    return call(
        functools.partial(pick_kernel, grid.live),
        grid.ids,
        pieces,
        [shape_of((grid.live * rows.shape[0], rows.shape[1]), rows.dtype)],
        [],
        4,
    )[0]


def gather_plane(grid, own):
    by_x = grid.send(own, d=1)
    by_y = grid.send(own, a=1)
    far = grid.send(own, a=1, d=1)
    own_c = grid.send(own, b=1)
    by_x_c = grid.send(by_x, b=1)
    by_y_c = grid.send(by_y, b=1)
    far_c = grid.send(far, b=1)
    return jnp.concatenate([own, by_x, own_c, by_x_c, by_y, far, by_y_c, far_c], axis=0)


def reduce_rows(grid, low, other, share):
    total = low + other.astype(F32)
    low = total.astype(BF16)
    by_x = grid.send(low[0, 1], d=1)
    by_y = grid.send(low[1, 0], a=1)
    far = grid.send(low[1, 1], a=1, d=1)
    mine = total[0, 0] + by_x.astype(F32) + by_y.astype(F32) + far.astype(F32)
    mine = mine.reshape(grid.live, share, total.shape[-1])
    mine_low = mine.astype(BF16)
    summed = lax.dynamic_index_in_dim(
        mine, jnp.minimum(grid.z, grid.live - 1), 0, keepdims=False
    )
    for k in range(1, grid.depth):
        to = jnp.minimum(grid.z ^ k, grid.live - 1)
        chunk = lax.dynamic_index_in_dim(mine_low, to, 0, keepdims=False)
        chunk = grid.send(chunk, k=k, target=grid.live)
        summed = summed + chunk.astype(F32)
    return summed


def row_weights(lengths, tok_rows):
    ends = jnp.cumsum(lengths, axis=1)
    starts = ends - lengths
    places = jnp.arange(tok_rows, dtype=jnp.int32)
    inside = (places[None, :, None] >= starts[:, None, :]) & (
        places[None, :, None] < ends[:, None, :]
    )
    spans = jnp.sum(jnp.where(inside, lengths[:, None, :], 0), axis=2)
    covered = jnp.sum(inside.astype(jnp.int32), axis=2)
    return covered.astype(F32) / jnp.maximum(spans, 1).astype(F32)


def turn(grid, value):
    for axis, at in ((1, grid.y), (2, grid.c), (3, grid.x)):
        value = jnp.where(at == 1, jnp.flip(value, axis), value)
    return value


def exchange(grid, stats):
    devices = 4 * grid.tp
    flat = turn(grid, stats).reshape(-1)
    sent = jnp.broadcast_to(flat[None], (devices, flat.shape[0])).reshape(-1)
    got = lax.all_to_all(sent, AXES, 0, 0, tiled=True)
    return got.reshape((devices,) + stats.shape)


def join_logs(logs):
    top = jnp.max(logs, axis=0)
    return top + jnp.log(jnp.sum(jnp.exp(logs - top[None]), axis=0))


def shards(
    teacher_partial,
    teacher_residual,
    post_gain,
    final_gain,
    teacher_head,
    student_hidden,
    student_gain,
    student_head,
    labels,
    lengths,
):
    share, width_t = teacher_residual.shape
    width_s = student_hidden.shape[1]
    tok_rows = labels.shape[0]
    nseq = lengths.shape[1]
    grid = Grid(lax.axis_size("dp"), lax.axis_size("tp"), share)
    live = grid.live

    parts = teacher_partial[0, :LIVE].reshape(live, 2, share, width_t)
    given = lax.dynamic_index_in_dim(parts, 1 - grid.x, 1, keepdims=False)
    other = grid.send(given, d=1)
    at = jnp.minimum(grid.z, live - 1)
    ks = range(1, grid.depth)
    if grid.tiled:
        own, *lows = call(
            functools.partial(pair_kernel, live),
            grid.ids,
            [teacher_partial, other],
            [shape_of((share, width_t), F32)] + [shape_of((share, width_t), BF16) for k in ks],
            [],
            4,
        )
    else:
        kept = lax.dynamic_index_in_dim(parts, grid.x, 1, keepdims=False)
        pair = kept.astype(F32) + other.astype(F32)
        own = lax.dynamic_index_in_dim(pair, at, 0, keepdims=False)
        lows = [
            lax.dynamic_index_in_dim(
                pair, jnp.minimum(grid.z ^ k, live - 1), 0, keepdims=False
            ).astype(BF16)
            for k in ks
        ]
    others = [grid.send(low, k=k, target=live) for k, low in zip(ks, lows)]

    student_f = student_hidden.astype(F32)
    student_scaled, inverse = norm_rows(student_f, student_gain)
    student_norm = student_scaled.astype(BF16)
    own_s = gather_depth(grid, student_norm)
    whole_s = gather_plane(grid, own_s)

    ints = jnp.concatenate([labels, lengths[0]])[None]
    ints = jnp.concatenate([ints, grid.send(ints, b=1)], axis=0)
    ints = jnp.concatenate([ints, grid.send(ints, a=1)], axis=0)

    def by_row(value):
        value = value[:, :LIVE].reshape(4, live, 2, share)
        value = jnp.moveaxis(value, 2, 1)
        value = jnp.where(grid.x == 1, jnp.flip(value, 1), value)
        return value.reshape(2, 2, 2, live * share)

    label_rows = by_row(ints[:, :tok_rows])
    weight_rows = by_row(row_weights(ints[:, tok_rows : tok_rows + nseq], tok_rows))

    if grid.tiled:
        teacher_norm = call(
            norm_kernel,
            grid.ids,
            [own, *others, teacher_residual, post_gain[None], final_gain[None]],
            [shape_of((share, width_t), BF16)],
            [],
            4,
        )[0]
    else:
        mlp_sum = own
        for other in others:
            mlp_sum = mlp_sum + other.astype(F32)
        post, _ = norm_rows(mlp_sum, post_gain)
        final = teacher_residual.astype(F32) + post
        teacher_norm = norm_rows(final, final_gain)[0].astype(BF16)
    own_t = gather_depth(grid, teacher_norm)
    whole_t = gather_plane(grid, own_t)

    rows = whole_s.shape[0]
    shape = label_rows.shape
    vocab_dev = student_head.shape[1]
    position = lax.axis_index("dp") * lax.axis_size("tp") + lax.axis_index("tp")
    columns = position * vocab_dev + jnp.arange(vocab_dev, dtype=jnp.int32)
    hit = label_rows.reshape(rows)[:, None] == columns[None, :]

    s_logits = jnp.dot(whole_s, student_head, preferred_element_type=F32)
    s_top = jnp.max(s_logits, axis=1)
    s_own = s_top + jnp.log(jnp.sum(jnp.exp(s_logits - s_top[:, None]), axis=1))
    s_label = jnp.sum(jnp.where(hit, s_logits, 0.0), axis=1)

    t_logits = jnp.dot(whole_t, teacher_head, preferred_element_type=F32)
    t_top = jnp.max(t_logits, axis=1)
    t_exp = jnp.exp(t_logits - t_top[:, None])
    t_sum = jnp.sum(t_exp, axis=1)
    t_mix = jnp.sum(t_exp * (t_logits - s_logits), axis=1) / t_sum
    t_own = t_top + jnp.log(t_sum)

    stats = exchange(grid, jnp.stack([t_own, t_mix, s_own, s_label]).reshape((4,) + shape))
    t_log = join_logs(stats[:, 0])
    t_cross = jnp.sum(jnp.exp(stats[:, 0] - t_log[None]) * stats[:, 1], axis=0)
    s_log = join_logs(stats[:, 2])
    label_value = jnp.sum(stats[:, 3], axis=0)
    t_log, t_cross, s_log, label_value = turn(
        grid, jnp.stack([t_log, t_cross, s_log, label_value])
    )
    divergence = t_cross - t_log + s_log
    label_term = s_log - label_value
    row_loss = jnp.where(weight_rows > 0, divergence + BETA * label_term, 0.0)

    def column(value):
        return value.reshape(rows)[:, None]

    t_prob = jnp.exp(t_logits - column(t_log))
    s_prob = jnp.exp(s_logits - column(s_log))
    scale = LOSS_SCALE * column(weight_rows)
    logit_grad = (scale * ((1.0 + BETA) * s_prob - t_prob - BETA * hit.astype(F32))).astype(BF16)
    partial = lax.dot_general(
        logit_grad, student_head, (((1,), (1,)), ((), ())), preferred_element_type=F32
    ).reshape(2, 2, 2, live * share, width_s)

    other = grid.send(partial[:, 1].astype(BF16), b=1)
    summed = reduce_rows(grid, partial[:, 0], other, share)

    scaled = summed * student_gain
    inner = jnp.mean(scaled * student_f, axis=1, keepdims=True)
    grad_hidden = inverse * scaled - student_f * (inverse * inverse * inverse) * inner
    own = grid.z < live
    grad_hidden = jnp.where(own, grad_hidden, 0.0)
    own_loss = lax.dynamic_slice_in_dim(row_loss[0, 0, 0], at * share, share, 0)
    return (grad_hidden, jnp.where(own, own_loss, 0.0))


def solution(mesh):
    placed = (
        P("tp", "dp", None),
        P(("dp", "tp"), None),
        P(),
        P(),
        P(None, ("dp", "tp")),
        P(("dp", "tp"), None),
        P(),
        P(None, ("dp", "tp")),
        P("dp"),
        P("dp", None),
    )
    return jax.shard_map(
        shards,
        mesh=mesh,
        in_specs=placed,
        out_specs=(P(("dp", "tp"), None), P(("dp", "tp"))),
        check_vma=False,
    )
```

profile of v0, /device:TPU:0, one launch (start us, length us, event | category | flops | bytes accessed | tf_op | source)
XLA Modules:
  0.0 161.6 jit_solution(14820466276876435857)
XLA Ops:
  0.6 1.1 fusion.20
  2.3 1.0 fusion.22.refs_0_
  3.3 5.0 %collective-permute-start.2 = (bf16[16,3584]{1,0:T(8,128)(2,1)S(1)}, bf16[16,3584]{1,0:T(8,128)(2,1)S(1)}, u32[]{:S(2)}, u32[]{:S(2)}) collective-permute-start(bf16[16,3584]{1,0:T(8,128)(2,1)S(1)} %fusion.22.refs_0_), channel_id=1, source_target_pairs={{0,2},{1,3},{2,0},{3,1},{4,6},{5,7},{8,10},{9,11},{10,8},{11,9},{1... | collective-permute-start | bytes 344072 | tf_op jit(solution)/shard_map/ppermute | solution.py:43
  8.3 4.5 %collective-permute-start.3 = (bf16[16,3584]{1,0:T(8,128)(2,1)S(1)}, bf16[16,3584]{1,0:T(8,128)(2,1)S(1)}, u32[]{:S(2)}, u32[]{:S(2)}) collective-permute-start(bf16[16,3584]{1,0:T(8,128)(2,1)S(1)} %fusion.22.refs_0_), channel_id=1, source_target_pairs={{0,4},{1,5},{2,6},{3,7},{4,0},{5,1},{8,12},{9,13},{10,14},{11,15},... | collective-permute-start | bytes 344072 | tf_op jit(solution)/shard_map/ppermute | solution.py:43
  12.8 1.3 collective-permute-start.4
  14.1 1.2 slice.51
  15.4 1.6 collective-permute-start.12
  17.0 0.7 pad_add_fusion.2
  17.7 1.1 collective-permute-done
  18.8 1.6 collective-permute-start.1
  20.4 0.7 broadcast_in_dim.58.refs_5_
  21.2 0.7 broadcast_in_dim.59.refs_6_
  23.1 0.7 shard_map.113
  23.7 0.6 collective-permute-start.5
  24.3 1.5 collective-permute-start.8
  25.9 2.1 %collective-permute-done.12.other = bf16[3,16,4608]{2,1,0:T(8,128)(2,1)S(1)} collective-permute-done((bf16[3,16,4608]{2,1,0:T(8,128)(2,1)S(1)}, bf16[3,16,4608]{2,1,0:T(8,128)(2,1)S(1)}, u32[]{:S(2)}, u32[]{:S(2)}) %collective-permute-start.12) | collective-permute-done | bytes 442400 | tf_op jit(solution)/shard_map/ppermute | solution.py:43
  27.9 0.7 shard_map.114
  28.6 2.9 %collective-permute-start.13 = (bf16[16,4608]{1,0:T(8,128)(2,1)S(1)}, bf16[16,4608]{1,0:T(8,128)(2,1)S(1)}, u32[]{:S(2)}, u32[]{:S(2)}) collective-permute-start(bf16[16,4608]{1,0:T(8,128)(2,1)S(1)} %get-tuple-element.7), channel_id=1, source_target_pairs={{0,2},{1,3},{2,0},{3,1},{6,4},{7,5},{8,10},{9,11},{10,8},{11,9},{1... | collective-permute-start | bytes 442376 | tf_op jit(solution)/shard_map/ppermute | solution.py:43
  31.5 1.9 %collective-permute-start.14 = (bf16[16,4608]{1,0:T(8,128)(2,1)S(1)}, bf16[16,4608]{1,0:T(8,128)(2,1)S(1)}, u32[]{:S(2)}, u32[]{:S(2)}) collective-permute-start(bf16[16,4608]{1,0:T(8,128)(2,1)S(1)} %get-tuple-element.8), channel_id=1, source_target_pairs={{0,4},{1,5},{4,0},{5,1},{6,2},{7,3},{8,12},{9,13},{12,8},{13,9},{1... | collective-permute-start | bytes 442376 | tf_op jit(solution)/shard_map/ppermute | solution.py:43
  33.4 0.8 collective-permute-done.5
  34.2 1.3 collective-permute-start.15
  36.0 4.1 %collective-permute-start.9 = (bf16[48,3584]{1,0:T(8,128)(2,1)S(1)}, bf16[48,3584]{1,0:T(8,128)(2,1)S(1)}, u32[]{:S(2)}, u32[]{:S(2)}) collective-permute-start(bf16[48,3584]{1,0:T(8,128)(2,1)S(1)} %shard_map.113), channel_id=1, source_target_pairs={{0,17},{1,16},{2,19},{3,18},{4,21},{5,20},{6,23},{7,22},{8,25},{9,... | collective-permute-start | bytes 1032200 | tf_op jit(solution)/shard_map/ppermute | solution.py:43
  40.1 6.0 %collective-permute-done.14.refs_2_ = bf16[16,4608]{1,0:T(8,128)(2,1)S(1)} collective-permute-done((bf16[16,4608]{1,0:T(8,128)(2,1)S(1)}, bf16[16,4608]{1,0:T(8,128)(2,1)S(1)}, u32[]{:S(2)}, u32[]{:S(2)}) %collective-permute-start.14) | collective-permute-done | bytes 147488 | tf_op jit(solution)/shard_map/ppermute | solution.py:43
  46.0 0.9 shard_map.115.refs_0_
  46.9 4.4 %collective-permute-start.16 = (bf16[16,4608]{1,0:T(8,128)(2,1)S(1)}, bf16[16,4608]{1,0:T(8,128)(2,1)S(1)}, u32[]{:S(2)}, u32[]{:S(2)}) collective-permute-start(bf16[16,4608]{1,0:T(8,128)(2,1)S(1)} %shard_map.115.refs_0_), channel_id=1, source_target_pairs={{0,2},{1,3},{2,0},{3,1},{4,6},{5,7},{8,10},{9,11},{10,8},{11,9},{1... | collective-permute-start | bytes 442376 | tf_op jit(solution)/shard_map/ppermute | solution.py:43
  51.3 1.9 %collective-permute-start.17 = (bf16[16,4608]{1,0:T(8,128)(2,1)S(1)}, bf16[16,4608]{1,0:T(8,128)(2,1)S(1)}, u32[]{:S(2)}, u32[]{:S(2)}) collective-permute-start(bf16[16,4608]{1,0:T(8,128)(2,1)S(1)} %shard_map.115.refs_0_), channel_id=1, source_target_pairs={{0,4},{1,5},{2,6},{3,7},{4,0},{5,1},{8,12},{9,13},{10,14},{11,15},... | collective-permute-start | bytes 442376 | tf_op jit(solution)/shard_map/ppermute | solution.py:43
  53.2 1.3 collective-permute-start.18
  55.5 4.8 %collective-permute-done.17.refs_2_ = bf16[16,4608]{1,0:T(8,128)(2,1)S(1)} collective-permute-done((bf16[16,4608]{1,0:T(8,128)(2,1)S(1)}, bf16[16,4608]{1,0:T(8,128)(2,1)S(1)}, u32[]{:S(2)}, u32[]{:S(2)}) %collective-permute-start.17) | collective-permute-done | bytes 147488 | tf_op jit(solution)/shard_map/ppermute | solution.py:43
  60.4 0.7 shard_map.116
  61.0 0.8 collective-permute-start.19
  61.9 0.6 collective-permute-start.22
  62.7 2.2 %collective-permute-start.23 = (bf16[48,4608]{1,0:T(8,128)(2,1)S(1)}, bf16[48,4608]{1,0:T(8,128)(2,1)S(1)}, u32[]{:S(2)}, u32[]{:S(2)}) collective-permute-start(bf16[48,4608]{1,0:T(8,128)(2,1)S(1)} %shard_map.116), channel_id=1, source_target_pairs={{0,17},{1,16},{2,19},{3,18},{4,21},{5,20},{6,23},{7,22},{8,25},{9,... | collective-permute-start | bytes 1327112 | tf_op jit(solution)/shard_map/ppermute | solution.py:43
  65.0 3.2 %fusion.51 = (f32[384]{0:T(512)S(1)}, f32[384,1024]{1,0:T(8,128)S(1)}) fusion(bf16[384,3584]{1,0:T(8,128)(2,1)S(1)} %constant_dynamic-update-slice_fusion, bf16[3584,1024]{1,0:T(8,128)(2,1)S(1)} %copy-done.9), kind=kOutput, calls=%fused_computation.129 | convolution fusion | flops 2818964992 | bytes 11666944 | tf_op jit(solution)/shard_map/dot_general | solution.py:279
  68.2 6.0 %collective-permute-done.19 = bf16[48,4608]{1,0:T(8,128)(2,1)S(1)} collective-permute-done((bf16[48,4608]{1,0:T(8,128)(2,1)S(1)}, bf16[48,4608]{1,0:T(8,128)(2,1)S(1)}, u32[]{:S(2)}, u32[]{:S(2)}) %collective-permute-start.19) | collective-permute-done | bytes 442400 | tf_op jit(solution)/shard_map/ppermute | solution.py:43
  74.1 9.9 %collective-permute-done.22 = bf16[48,4608]{1,0:T(8,128)(2,1)S(1)} collective-permute-done((bf16[48,4608]{1,0:T(8,128)(2,1)S(1)}, bf16[48,4608]{1,0:T(8,128)(2,1)S(1)}, u32[]{:S(2)}, u32[]{:S(2)}) %collective-permute-start.22) | collective-permute-done | bytes 442400 | tf_op jit(solution)/shard_map/ppermute | solution.py:43
  84.8 1.1 collective-permute-done.24
  85.9 0.6 collective-permute-done.25
  86.5 3.9 %fusion.52 = (f32[384]{0:T(512)S(1)}, f32[384,1024]{1,0:T(8,128)S(1)}) fusion(bf16[384,4608]{1,0:T(8,128)(2,1)S(1)} %constant_dynamic-update-slice_fusion.8, bf16[4608,1024]{1,0:T(8,128)(2,1)S(1)} %bitcast.120), kind=kOutput, calls=%fused_computation.130 | convolution fusion | flops 3624271360 | bytes 14550528 | tf_op jit(solution)/shard_map/dot_general | solution.py:284
  90.4 1.2 copy-done.3
  91.6 1.0 fusion.1
  93.2 0.8 all_to_all.6
  94.0 8.1 %all-to-all-start = ((f32[32,1536,1]{1,2,0:T(1,128)}), f32[32,1536,1]{1,2,0:T(1,128)S(1)}, u32[]{:S(2)}, u32[]{:S(2)}) async-start(f32[32,1536,1]{1,2,0:T(1,128)} %all_to_all.6), calls=%async_computation | async-start | bytes 393216 | tf_op jit(solution)/shard_map/all_to_all | solution.py:180
  102.2 0.6 copy-done.5
  102.9 7.3 %all-to-all-done = f32[32,1536,1]{1,2,0:T(1,128)S(1)} async-done(((f32[32,1536,1]{1,2,0:T(1,128)}), f32[32,1536,1]{1,2,0:T(1,128)S(1)}, u32[]{:S(2)}, u32[]{:S(2)}) %all-to-all-start) | async-done | bytes 196640 | tf_op jit(solution)/shard_map/all_to_all | solution.py:180
  110.6 0.9 reshape.189
  112.2 0.6 fusion.42
  113.0 7.1 %fusion.7 = f32[384,3584]{1,0:T(8,128)S(1)} fusion(bf16[3584,1024]{1,0:T(8,128)(2,1)} %param.17, f32[384,1024]{1,0:T(8,128)} %copy-done.3, f32[384,1024]{1,0:T(8,128)S(1)} %get-tuple-element.38, f32[384]{0:T(512)S(1)} %sub.111, f32[384]{0:T(512)S(1)} %sub.108, s32[1024]{0:T(1024)S(1)} %iota_add_fusion, f32[384]{0:T(512)S(1)} %mul.127, s32[384]{0:T(512)S(1)} %eq.35), kind=kOutput, calls=%fused_computation.14 | convolution fusion | flops 2822111232 | bytes 16001024 | tf_op jit(solution)/shard_map/dot_general | solution.py:310
  120.7 2.8 %collective-permute-done.26 = bf16[2,2,48,3584]{3,2,1,0:T(8,128)(2,1)S(1)} collective-permute-done((bf16[2,2,48,3584]{3,2,1,0:T(8,128)(2,1)S(1)}, bf16[2,2,48,3584]{3,2,1,0:T(8,128)(2,1)S(1)}, u32[]{:S(2)}, u32[]{:S(2)}) %collective-permute-start.26) | collective-permute-done | bytes 1376288 | tf_op jit(solution)/shard_map/ppermute | solution.py:43
  123.9 1.0 slice_bitcast_fusion.4
  124.8 2.0 %collective-permute-start.27 = (bf16[48,3584]{1,0:T(8,128)(2,1)}, bf16[48,3584]{1,0:T(8,128)(2,1)S(1)}, u32[]{:S(2)}, u32[]{:S(2)}) collective-permute-start(bf16[48,3584]{1,0:T(8,128)(2,1)} %get-tuple-element.24), channel_id=1, source_target_pairs={{0,1},{1,0},{2,3},{3,2},{4,5},{5,4},{6,7},{7,6},{8,9},{9,8},{10,11... | collective-permute-start | bytes 1032200 | tf_op jit(solution)/shard_map/ppermute | solution.py:43
  127.3 1.0 collective-permute-start.29
  128.3 0.8 fusion.38
  129.1 0.6 copy.40
  129.7 1.3 gt.13
  131.1 4.9 %collective-permute-done.27 = bf16[48,3584]{1,0:T(8,128)(2,1)S(1)} collective-permute-done((bf16[48,3584]{1,0:T(8,128)(2,1)}, bf16[48,3584]{1,0:T(8,128)(2,1)S(1)}, u32[]{:S(2)}, u32[]{:S(2)}) %collective-permute-start.27) | collective-permute-done | bytes 344096 | tf_op jit(solution)/shard_map/ppermute | solution.py:43
  136.0 8.2 %collective-permute-done.28 = bf16[48,3584]{1,0:T(8,128)(2,1)S(1)} collective-permute-done((bf16[48,3584]{1,0:T(8,128)(2,1)}, bf16[48,3584]{1,0:T(8,128)(2,1)S(1)}, u32[]{:S(2)}, u32[]{:S(2)}) %collective-permute-start.28) | collective-permute-done | bytes 344096 | tf_op jit(solution)/shard_map/ppermute | solution.py:43
  144.2 1.1 fusion.19
  145.4 2.2 %collective-permute-start.30 = (bf16[16,3584]{1,0:T(8,128)(2,1)S(1)}, bf16[16,3584]{1,0:T(8,128)(2,1)S(1)}, u32[]{:S(2)}, u32[]{:S(2)}) collective-permute-start(bf16[16,3584]{1,0:T(8,128)(2,1)S(1)} %get-tuple-element.27), channel_id=1, source_target_pairs={{0,2},{1,3},{2,0},{3,1},{6,4},{7,5},{8,10},{9,11},{10,8},{11,9},{1... | collective-permute-start | bytes 344072 | tf_op jit(solution)/shard_map/ppermute | solution.py:43
  147.7 1.9 %collective-permute-start.31 = (bf16[16,3584]{1,0:T(8,128)(2,1)S(1)}, bf16[16,3584]{1,0:T(8,128)(2,1)S(1)}, u32[]{:S(2)}, u32[]{:S(2)}) collective-permute-start(bf16[16,3584]{1,0:T(8,128)(2,1)S(1)} %get-tuple-element.29), channel_id=1, source_target_pairs={{0,4},{1,5},{4,0},{5,1},{6,2},{7,3},{8,12},{9,13},{12,8},{13,9},{1... | collective-permute-start | bytes 344072 | tf_op jit(solution)/shard_map/ppermute | solution.py:43
  149.6 1.3 collective-permute-start.32
  150.9 0.7 slice_select_fusion
  152.2 1.0 collective-permute-done.30
  153.2 7.3 %collective-permute-done.31 = bf16[16,3584]{1,0:T(8,128)(2,1)S(1)} collective-permute-done((bf16[16,3584]{1,0:T(8,128)(2,1)S(1)}, bf16[16,3584]{1,0:T(8,128)(2,1)S(1)}, u32[]{:S(2)}, u32[]{:S(2)}) %collective-permute-start.31) | collective-permute-done | bytes 114720 | tf_op jit(solution)/shard_map/ppermute | solution.py:43
  160.7 0.8 fusion.25
  (128 shorter events, 8.5 us)
Async XLA Ops:
  0.6 27.3 %copy-start = (bf16[1,128,4608]{2,1,0:T(8,128)(2,1)S(1)}, bf16[1,128,4608]{2,1,0:T(8,128)(2,1)}, u32[]{:S(2)}) copy-start(bf16[1,128,4608]{2,1,0:T(8,128)(2,1)} %partial.1) | copy-start | bytes 3538948
  2.3 6.0 %copy-start.6 = (f32[16]{0:T(128)}, f32[16]{0:T(128)S(1)}, u32[]{:S(2)}) copy-start(f32[16]{0:T(128)S(1)} %get-tuple-element.36) | copy-start | bytes 196
  3.3 19.7 %collective-permute-start.2 = (bf16[16,3584]{1,0:T(8,128)(2,1)S(1)}, bf16[16,3584]{1,0:T(8,128)(2,1)S(1)}, u32[]{:S(2)}, u32[]{:S(2)}) collective-permute-start(bf16[16,3584]{1,0:T(8,128)(2,1)S(1)} %fusion.22.refs_0_), channel_id=1, source_target_pairs={{0,2},{1,3},{2,0},{3,1},{4,6},{5,7},{8,10},{9,11},{10,8},{11,9},{1... | collective-permute-start | bytes 344072 | tf_op jit(solution)/shard_map/ppermute | solution.py:43
  8.3 14.7 %collective-permute-start.3 = (bf16[16,3584]{1,0:T(8,128)(2,1)S(1)}, bf16[16,3584]{1,0:T(8,128)(2,1)S(1)}, u32[]{:S(2)}, u32[]{:S(2)}) collective-permute-start(bf16[16,3584]{1,0:T(8,128)(2,1)S(1)} %fusion.22.refs_0_), channel_id=1, source_target_pairs={{0,4},{1,5},{2,6},{3,7},{4,0},{5,1},{8,12},{9,13},{10,14},{11,15},... | collective-permute-start | bytes 344072 | tf_op jit(solution)/shard_map/ppermute | solution.py:43
  12.8 10.2 %collective-permute-start.4 = (bf16[16,3584]{1,0:T(8,128)(2,1)S(1)}, bf16[16,3584]{1,0:T(8,128)(2,1)S(1)}, u32[]{:S(2)}, u32[]{:S(2)}) collective-permute-start(bf16[16,3584]{1,0:T(8,128)(2,1)S(1)} %fusion.22.refs_0_), channel_id=1, source_target_pairs={{0,6},{1,7},{2,4},{3,5},{4,2},{5,3},{8,14},{9,15},{10,12},{11,13},... | collective-permute-start | bytes 344072 | tf_op jit(solution)/shard_map/ppermute | solution.py:43
  15.4 30.7 %copy-start.1 = (bf16[16,4608]{1,0:T(8,128)(2,1)S(1)}, bf16[16,4608]{1,0:T(8,128)(2,1)}, u32[]{:S(2)}) copy-start(bf16[16,4608]{1,0:T(8,128)(2,1)} %refs_4_.1) | copy-start | bytes 442372
  15.4 12.5 %collective-permute-start.12 = (bf16[3,16,4608]{2,1,0:T(8,128)(2,1)S(1)}, bf16[3,16,4608]{2,1,0:T(8,128)(2,1)S(1)}, u32[]{:S(2)}, u32[]{:S(2)}) collective-permute-start(bf16[3,16,4608]{2,1,0:T(8,128)(2,1)S(1)} %dynamic-slice_bitcast_fusion), channel_id=1, source_target_pairs={{0,1},{1,0},{2,3},{3,2},{4,5},{5,4},{6,7},{7,6},{8,9},{9,8},{10,11... | collective-permute-start | bytes 1327112 | tf_op jit(solution)/shard_map/ppermute | solution.py:43
  17.7 1.2 collective-permute-start
  18.8 3.7 %collective-permute-start.1 = (s32[2,136]{1,0:T(2,128)S(1)}, s32[2,136]{1,0:T(2,128)S(1)}, u32[]{:S(2)}, u32[]{:S(2)}) collective-permute-start(s32[2,136]{1,0:T(2,128)S(1)} %pad_add_fusion.1), channel_id=1, source_target_pairs={{0,16},{1,17},{2,18},{3,19},{4,20},{5,21},{6,22},{7,23},{8,24},{9,... | collective-permute-start | bytes 3272 | tf_op jit(solution)/shard_map/ppermute | solution.py:43
  23.7 10.5 %collective-permute-start.5 = (bf16[48,3584]{1,0:T(8,128)(2,1)S(1)}, bf16[48,3584]{1,0:T(8,128)(2,1)S(1)}, u32[]{:S(2)}, u32[]{:S(2)}) collective-permute-start(bf16[48,3584]{1,0:T(8,128)(2,1)S(1)} %shard_map.113), channel_id=1, source_target_pairs={{0,1},{1,0},{2,3},{3,2},{4,5},{5,4},{6,7},{7,6},{8,9},{9,8},{10,11... | collective-permute-start | bytes 1032200 | tf_op jit(solution)/shard_map/ppermute | solution.py:43
  24.3 28.9 %collective-permute-start.6 = (bf16[48,3584]{1,0:T(8,128)(2,1)S(1)}, bf16[48,3584]{1,0:T(8,128)(2,1)S(1)}, u32[]{:S(2)}, u32[]{:S(2)}) collective-permute-start(bf16[48,3584]{1,0:T(8,128)(2,1)S(1)} %shard_map.113), channel_id=1, source_target_pairs={{0,8},{1,9},{2,10},{3,11},{4,12},{5,13},{6,14},{7,15},{8,0},{9,1},... | collective-permute-start | bytes 1032200 | tf_op jit(solution)/shard_map/ppermute | solution.py:43
  24.3 30.3 %collective-permute-start.8 = (bf16[48,3584]{1,0:T(8,128)(2,1)S(1)}, bf16[48,3584]{1,0:T(8,128)(2,1)S(1)}, u32[]{:S(2)}, u32[]{:S(2)}) collective-permute-start(bf16[48,3584]{1,0:T(8,128)(2,1)S(1)} %shard_map.113), channel_id=1, source_target_pairs={{0,16},{1,17},{2,18},{3,19},{4,20},{5,21},{6,22},{7,23},{8,24},{9,... | collective-permute-start | bytes 1032200 | tf_op jit(solution)/shard_map/ppermute | solution.py:43
  28.6 7.4 %collective-permute-start.13 = (bf16[16,4608]{1,0:T(8,128)(2,1)S(1)}, bf16[16,4608]{1,0:T(8,128)(2,1)S(1)}, u32[]{:S(2)}, u32[]{:S(2)}) collective-permute-start(bf16[16,4608]{1,0:T(8,128)(2,1)S(1)} %get-tuple-element.7), channel_id=1, source_target_pairs={{0,2},{1,3},{2,0},{3,1},{6,4},{7,5},{8,10},{9,11},{10,8},{11,9},{1... | collective-permute-start | bytes 442376 | tf_op jit(solution)/shard_map/ppermute | solution.py:43
  31.5 14.5 %collective-permute-start.14 = (bf16[16,4608]{1,0:T(8,128)(2,1)S(1)}, bf16[16,4608]{1,0:T(8,128)(2,1)S(1)}, u32[]{:S(2)}, u32[]{:S(2)}) collective-permute-start(bf16[16,4608]{1,0:T(8,128)(2,1)S(1)} %get-tuple-element.8), channel_id=1, source_target_pairs={{0,4},{1,5},{4,0},{5,1},{6,2},{7,3},{8,12},{9,13},{12,8},{13,9},{1... | collective-permute-start | bytes 442376 | tf_op jit(solution)/shard_map/ppermute | solution.py:43
  34.2 11.8 %collective-permute-start.15 = (bf16[16,4608]{1,0:T(8,128)(2,1)S(1)}, bf16[16,4608]{1,0:T(8,128)(2,1)S(1)}, u32[]{:S(2)}, u32[]{:S(2)}) collective-permute-start(bf16[16,4608]{1,0:T(8,128)(2,1)S(1)} %get-tuple-element.9), channel_id=1, source_target_pairs={{2,4},{3,5},{4,2},{5,3},{6,0},{7,1},{10,12},{11,13},{12,10},{13,11... | collective-permute-start | bytes 442376 | tf_op jit(solution)/shard_map/ppermute | solution.py:43
  35.5 29.4 %copy-start.9 = (bf16[3584,1024]{1,0:T(8,128)(2,1)S(1)}, bf16[3584,1024]{1,0:T(8,128)(2,1)}, u32[]{:S(2)}) copy-start(bf16[3584,1024]{1,0:T(8,128)(2,1)} %param.17) | copy-start | bytes 22020100
  36.0 18.7 %collective-permute-start.9 = (bf16[48,3584]{1,0:T(8,128)(2,1)S(1)}, bf16[48,3584]{1,0:T(8,128)(2,1)S(1)}, u32[]{:S(2)}, u32[]{:S(2)}) collective-permute-start(bf16[48,3584]{1,0:T(8,128)(2,1)S(1)} %shard_map.113), channel_id=1, source_target_pairs={{0,17},{1,16},{2,19},{3,18},{4,21},{5,20},{6,23},{7,22},{8,25},{9,... | collective-permute-start | bytes 1032200 | tf_op jit(solution)/shard_map/ppermute | solution.py:43
  46.9 8.6 %collective-permute-start.16 = (bf16[16,4608]{1,0:T(8,128)(2,1)S(1)}, bf16[16,4608]{1,0:T(8,128)(2,1)S(1)}, u32[]{:S(2)}, u32[]{:S(2)}) collective-permute-start(bf16[16,4608]{1,0:T(8,128)(2,1)S(1)} %shard_map.115.refs_0_), channel_id=1, source_target_pairs={{0,2},{1,3},{2,0},{3,1},{4,6},{5,7},{8,10},{9,11},{10,8},{11,9},{1... | collective-permute-start | bytes 442376 | tf_op jit(solution)/shard_map/ppermute | solution.py:43
  51.3 9.1 %collective-permute-start.17 = (bf16[16,4608]{1,0:T(8,128)(2,1)S(1)}, bf16[16,4608]{1,0:T(8,128)(2,1)S(1)}, u32[]{:S(2)}, u32[]{:S(2)}) collective-permute-start(bf16[16,4608]{1,0:T(8,128)(2,1)S(1)} %shard_map.115.refs_0_), channel_id=1, source_target_pairs={{0,4},{1,5},{2,6},{3,7},{4,0},{5,1},{8,12},{9,13},{10,14},{11,15},... | collective-permute-start | bytes 442376 | tf_op jit(solution)/shard_map/ppermute | solution.py:43
  53.2 7.1 %collective-permute-start.18 = (bf16[16,4608]{1,0:T(8,128)(2,1)S(1)}, bf16[16,4608]{1,0:T(8,128)(2,1)S(1)}, u32[]{:S(2)}, u32[]{:S(2)}) collective-permute-start(bf16[16,4608]{1,0:T(8,128)(2,1)S(1)} %shard_map.115.refs_0_), channel_id=1, source_target_pairs={{0,6},{1,7},{2,4},{3,5},{4,2},{5,3},{8,14},{9,15},{10,12},{11,13},... | collective-permute-start | bytes 442376 | tf_op jit(solution)/shard_map/ppermute | solution.py:43
  54.6 7.3 %collective-permute-start.7 = (bf16[48,3584]{1,0:T(8,128)(2,1)S(1)}, bf16[48,3584]{1,0:T(8,128)(2,1)S(1)}, u32[]{:S(2)}, u32[]{:S(2)}) collective-permute-start(bf16[48,3584]{1,0:T(8,128)(2,1)S(1)} %collective-permute-done.5), channel_id=1, source_target_pairs={{0,8},{1,9},{2,10},{3,11},{4,12},{5,13},{6,14},{7,15},{8,0},{9,1},... | collective-permute-start | bytes 1032200 | tf_op jit(solution)/shard_map/ppermute | solution.py:43
  54.7 8.0 %collective-permute-start.10 = (bf16[48,3584]{1,0:T(8,128)(2,1)S(1)}, bf16[48,3584]{1,0:T(8,128)(2,1)S(1)}, u32[]{:S(2)}, u32[]{:S(2)}) collective-permute-start(bf16[48,3584]{1,0:T(8,128)(2,1)S(1)} %collective-permute-done.8), channel_id=1, source_target_pairs={{0,8},{1,9},{2,10},{3,11},{4,12},{5,13},{6,14},{7,15},{8,0},{9,1},... | collective-permute-start | bytes 1032200 | tf_op jit(solution)/shard_map/ppermute | solution.py:43
  55.5 9.4 %collective-permute-start.11 = (bf16[48,3584]{1,0:T(8,128)(2,1)S(1)}, bf16[48,3584]{1,0:T(8,128)(2,1)S(1)}, u32[]{:S(2)}, u32[]{:S(2)}) collective-permute-start(bf16[48,3584]{1,0:T(8,128)(2,1)S(1)} %collective-permute-done.9), channel_id=1, source_target_pairs={{0,8},{1,9},{2,10},{3,11},{4,12},{5,13},{6,14},{7,15},{8,0},{9,1},... | collective-permute-start | bytes 1032200 | tf_op jit(solution)/shard_map/ppermute | solution.py:43
  61.0 13.1 %collective-permute-start.19 = (bf16[48,4608]{1,0:T(8,128)(2,1)S(1)}, bf16[48,4608]{1,0:T(8,128)(2,1)S(1)}, u32[]{:S(2)}, u32[]{:S(2)}) collective-permute-start(bf16[48,4608]{1,0:T(8,128)(2,1)S(1)} %shard_map.116), channel_id=1, source_target_pairs={{0,1},{1,0},{2,3},{3,2},{4,5},{5,4},{6,7},{7,6},{8,9},{9,8},{10,11... | collective-permute-start | bytes 1327112 | tf_op jit(solution)/shard_map/ppermute | solution.py:43
  61.9 22.7 %collective-permute-start.20 = (bf16[48,4608]{1,0:T(8,128)(2,1)S(1)}, bf16[48,4608]{1,0:T(8,128)(2,1)S(1)}, u32[]{:S(2)}, u32[]{:S(2)}) collective-permute-start(bf16[48,4608]{1,0:T(8,128)(2,1)S(1)} %shard_map.116), channel_id=1, source_target_pairs={{0,8},{1,9},{2,10},{3,11},{4,12},{5,13},{6,14},{7,15},{8,0},{9,1},... | collective-permute-start | bytes 1327112 | tf_op jit(solution)/shard_map/ppermute | solution.py:43
  61.9 22.1 %collective-permute-start.22 = (bf16[48,4608]{1,0:T(8,128)(2,1)S(1)}, bf16[48,4608]{1,0:T(8,128)(2,1)S(1)}, u32[]{:S(2)}, u32[]{:S(2)}) collective-permute-start(bf16[48,4608]{1,0:T(8,128)(2,1)S(1)} %shard_map.116), channel_id=1, source_target_pairs={{0,16},{1,17},{2,18},{3,19},{4,20},{5,21},{6,22},{7,23},{8,24},{9,... | collective-permute-start | bytes 1327112 | tf_op jit(solution)/shard_map/ppermute | solution.py:43
  62.7 21.4 %collective-permute-start.23 = (bf16[48,4608]{1,0:T(8,128)(2,1)S(1)}, bf16[48,4608]{1,0:T(8,128)(2,1)S(1)}, u32[]{:S(2)}, u32[]{:S(2)}) collective-permute-start(bf16[48,4608]{1,0:T(8,128)(2,1)S(1)} %shard_map.116), channel_id=1, source_target_pairs={{0,17},{1,16},{2,19},{3,18},{4,21},{5,20},{6,23},{7,22},{8,25},{9,... | collective-permute-start | bytes 1327112 | tf_op jit(solution)/shard_map/ppermute | solution.py:43
  64.9 21.6 %slice-start = ((s8[9437184]{0:T(1024)(128)(4,1)}), s8[4194304]{0:T(1024)(128)(4,1)S(1)}, s32[]{:S(2)}) async-start(s8[9437184]{0:T(1024)(128)(4,1)} %bitcast.119), calls=%async_computation.1 | async-start | bytes 8388608
  64.9 21.6 %slice-start.1 = ((s8[9437184]{0:T(1024)(128)(4,1)}), s8[4194304]{0:T(1024)(128)(4,1)S(1)}, s32[]{:S(2)}) async-start(s8[9437184]{0:T(1024)(128)(4,1)} %bitcast.119), calls=%async_computation.2 | async-start | bytes 8388608
  65.0 21.6 %slice-start.2 = ((s8[9437184]{0:T(1024)(128)(4,1)}), s8[1048576]{0:T(1024)(128)(4,1)S(1)}, s32[]{:S(2)}) async-start(s8[9437184]{0:T(1024)(128)(4,1)} %bitcast.119), calls=%async_computation.3 | async-start | bytes 2097152
  74.1 10.5 %collective-permute-start.21 = (bf16[48,4608]{1,0:T(8,128)(2,1)S(1)}, bf16[48,4608]{1,0:T(8,128)(2,1)S(1)}, u32[]{:S(2)}, u32[]{:S(2)}) collective-permute-start(bf16[48,4608]{1,0:T(8,128)(2,1)S(1)} %collective-permute-done.19), channel_id=1, source_target_pairs={{0,8},{1,9},{2,10},{3,11},{4,12},{5,13},{6,14},{7,15},{8,0},{9,1},... | collective-permute-start | bytes 1327112 | tf_op jit(solution)/shard_map/ppermute | solution.py:43
  84.0 1.8 %collective-permute-start.24 = (bf16[48,4608]{1,0:T(8,128)(2,1)S(1)}, bf16[48,4608]{1,0:T(8,128)(2,1)S(1)}, u32[]{:S(2)}, u32[]{:S(2)}) collective-permute-start(bf16[48,4608]{1,0:T(8,128)(2,1)S(1)} %collective-permute-done.22), channel_id=1, source_target_pairs={{0,8},{1,9},{2,10},{3,11},{4,12},{5,13},{6,14},{7,15},{8,0},{9,1},... | collective-permute-start | bytes 1327112 | tf_op jit(solution)/shard_map/ppermute | solution.py:43
  84.0 2.4 %collective-permute-start.25 = (bf16[48,4608]{1,0:T(8,128)(2,1)S(1)}, bf16[48,4608]{1,0:T(8,128)(2,1)S(1)}, u32[]{:S(2)}, u32[]{:S(2)}) collective-permute-start(bf16[48,4608]{1,0:T(8,128)(2,1)S(1)} %collective-permute-done.23), channel_id=1, source_target_pairs={{0,8},{1,9},{2,10},{3,11},{4,12},{5,13},{6,14},{7,15},{8,0},{9,1},... | collective-permute-start | bytes 1327112 | tf_op jit(solution)/shard_map/ppermute | solution.py:43
  90.4 1.2 copy-start.3
  94.0 16.2 %all-to-all-start = ((f32[32,1536,1]{1,2,0:T(1,128)}), f32[32,1536,1]{1,2,0:T(1,128)S(1)}, u32[]{:S(2)}, u32[]{:S(2)}) async-start(f32[32,1536,1]{1,2,0:T(1,128)} %all_to_all.6), calls=%async_computation | async-start | bytes 393216 | tf_op jit(solution)/shard_map/all_to_all | solution.py:180
  102.2 0.6 copy-start.5
  120.2 3.2 %collective-permute-start.26 = (bf16[2,2,48,3584]{3,2,1,0:T(8,128)(2,1)S(1)}, bf16[2,2,48,3584]{3,2,1,0:T(8,128)(2,1)S(1)}, u32[]{:S(2)}, u32[]{:S(2)}) collective-permute-start(bf16[2,2,48,3584]{3,2,1,0:T(8,128)(2,1)S(1)} %fusion.6), channel_id=1, source_target_pairs={{0,8},{1,9},{2,10},{3,11},{4,12},{5,13},{6,14},{7,15},{8,0},{9,1},... | collective-permute-start | bytes 4128776 | tf_op jit(solution)/shard_map/ppermute | solution.py:43
  123.8 36.7 %copy-start.2 = (bf16[16,3584]{1,0:T(8,128)(2,1)S(1)}, bf16[16,3584]{1,0:T(8,128)(2,1)}, u32[]{:S(2)}) copy-start(bf16[16,3584]{1,0:T(8,128)(2,1)} %param.15) | copy-start | bytes 344068
  124.8 11.1 %collective-permute-start.27 = (bf16[48,3584]{1,0:T(8,128)(2,1)}, bf16[48,3584]{1,0:T(8,128)(2,1)S(1)}, u32[]{:S(2)}, u32[]{:S(2)}) collective-permute-start(bf16[48,3584]{1,0:T(8,128)(2,1)} %get-tuple-element.24), channel_id=1, source_target_pairs={{0,1},{1,0},{2,3},{3,2},{4,5},{5,4},{6,7},{7,6},{8,9},{9,8},{10,11... | collective-permute-start | bytes 1032200 | tf_op jit(solution)/shard_map/ppermute | solution.py:43
  126.8 17.4 %collective-permute-start.28 = (bf16[48,3584]{1,0:T(8,128)(2,1)}, bf16[48,3584]{1,0:T(8,128)(2,1)S(1)}, u32[]{:S(2)}, u32[]{:S(2)}) collective-permute-start(bf16[48,3584]{1,0:T(8,128)(2,1)} %get-tuple-element.26), channel_id=1, source_target_pairs={{0,16},{1,17},{2,18},{3,19},{4,20},{5,21},{6,22},{7,23},{8,24},{9,... | collective-permute-start | bytes 1032200 | tf_op jit(solution)/shard_map/ppermute | solution.py:43
  127.3 16.9 %collective-permute-start.29 = (bf16[48,3584]{1,0:T(8,128)(2,1)}, bf16[48,3584]{1,0:T(8,128)(2,1)}, u32[]{:S(2)}, u32[]{:S(2)}) collective-permute-start(bf16[48,3584]{1,0:T(8,128)(2,1)} %get-tuple-element.25), channel_id=1, source_target_pairs={{0,17},{1,16},{2,19},{3,18},{4,21},{5,20},{6,23},{7,22},{8,25},{9,... | collective-permute-start | bytes 1032200 | tf_op jit(solution)/shard_map/ppermute | solution.py:43
  131.1 29.5 %copy-start.4 = (f32[3584]{0:T(1024)S(1)}, f32[3584]{0:T(1024)}, u32[]{:S(2)}) copy-start(f32[3584]{0:T(1024)} %param.16) | copy-start | bytes 43012
  131.1 29.7 %copy-start.7 = (f32[16]{0:T(128)S(1)}, f32[16]{0:T(128)}, u32[]{:S(2)}) copy-start(f32[16]{0:T(128)} %copy-done.6) | copy-start | bytes 196
  131.1 29.7 %copy-start.8 = (f32[16]{0:T(128)S(1)}, f32[16]{0:T(128)}, u32[]{:S(2)}) copy-start(f32[16]{0:T(128)} %get-tuple-element.35) | copy-start | bytes 196
  145.4 7.8 %collective-permute-start.30 = (bf16[16,3584]{1,0:T(8,128)(2,1)S(1)}, bf16[16,3584]{1,0:T(8,128)(2,1)S(1)}, u32[]{:S(2)}, u32[]{:S(2)}) collective-permute-start(bf16[16,3584]{1,0:T(8,128)(2,1)S(1)} %get-tuple-element.27), channel_id=1, source_target_pairs={{0,2},{1,3},{2,0},{3,1},{6,4},{7,5},{8,10},{9,11},{10,8},{11,9},{1... | collective-permute-start | bytes 344072 | tf_op jit(solution)/shard_map/ppermute | solution.py:43
  147.7 12.8 %collective-permute-start.31 = (bf16[16,3584]{1,0:T(8,128)(2,1)S(1)}, bf16[16,3584]{1,0:T(8,128)(2,1)S(1)}, u32[]{:S(2)}, u32[]{:S(2)}) collective-permute-start(bf16[16,3584]{1,0:T(8,128)(2,1)S(1)} %get-tuple-element.29), channel_id=1, source_target_pairs={{0,4},{1,5},{4,0},{5,1},{6,2},{7,3},{8,12},{9,13},{12,8},{13,9},{1... | collective-permute-start | bytes 344072 | tf_op jit(solution)/shard_map/ppermute | solution.py:43
  149.6 10.9 %collective-permute-start.32 = (bf16[16,3584]{1,0:T(8,128)(2,1)S(1)}, bf16[16,3584]{1,0:T(8,128)(2,1)S(1)}, u32[]{:S(2)}, u32[]{:S(2)}) collective-permute-start(bf16[16,3584]{1,0:T(8,128)(2,1)S(1)} %get-tuple-element.28), channel_id=1, source_target_pairs={{2,4},{3,5},{4,2},{5,3},{6,0},{7,1},{10,12},{11,13},{12,10},{13,11... | collective-permute-start | bytes 344072 | tf_op jit(solution)/shard_map/ppermute | solution.py:43
where the time goes:
time: 162 us
  waiting for transfers between devices  65.1 us (40%)
  starting transfers between devices  56.1 us (35%)
  matrix products  14.2 us (9%)
  other arithmetic  11 us (7%)
  local copies, waits for them, and re-layouts  10.9 us (7%)
  Pallas kernels  2.84 us (2%)
    ppermute x33, waiting for transfers between devices, send(): return lax.ppermute(value, AXES, pairs)  57.9 us
    ppermute x33, starting transfers between devices, send(): return lax.ppermute(value, AXES, pairs)  47.9 us
    all_to_all x1, starting transfers between devices, exchange(): got = lax.all_to_all(sent, AXES, 0, 0, tiled=True)  8.11 us
    all_to_all x1, waiting for transfers between devices, exchange(): got = lax.all_to_all(sent, AXES, 0, 0, tiled=True)  7.27 us
    dot_general x1, matrix products, shards(): lax.dot_general(logit_grad, student_head, (((1,), (1,)), ((), ())), prefe...  7.06 us
    dot_general x1, matrix products, shards(): t_logits = jnp.dot(whole_t, teacher_head, preferred_element_type=F32)  3.89 us
  transfers between devices with their start and end apart: 34, of which 18 were waited for; matrix products, arithmetic and copies ran while one was open for 7% of the time, Pallas kernels for 2%

commit v1 on v0

--- a/solution.py
+++ b/solution.py
@@ -63,16 +63,17 @@
 MIB = 1 << 20
 
 
-def call(kernel, ids, args, outs, scratch, mib):
+def call(kernel, ids, args, outs, scratch, mib, far=()):
     args = [pltpu.with_memory_space_constraint(arg, pltpu.VMEM) for arg in args]
+    far = [pltpu.with_memory_space_constraint(arg, pltpu.HBM) for arg in far]
     return pl.pallas_call(
         kernel,
         out_shape=outs,
-        in_specs=[SMEM] + [VMEM] * len(args),
+        in_specs=[SMEM] + [VMEM] * len(args) + [pl.BlockSpec(memory_space=pltpu.HBM)] * len(far),
         out_specs=[VMEM] * len(outs),
         scratch_shapes=scratch,
         compiler_params=pltpu.CompilerParams(vmem_limit_bytes=mib * MIB),
-    )(ids, *args)
+    )(ids, *args, *far)
 
 
 def pick_kernel(live, ids, *refs):
@@ -135,24 +136,250 @@
     return jnp.concatenate([own, by_x, own_c, by_x_c, by_y, far, by_y_c, far_c], axis=0)
 
 
-def reduce_rows(grid, low, other, share):
-    total = low + other.astype(F32)
-    low = total.astype(BF16)
-    by_x = grid.send(low[0, 1], d=1)
-    by_y = grid.send(low[1, 0], a=1)
-    far = grid.send(low[1, 1], a=1, d=1)
-    mine = total[0, 0] + by_x.astype(F32) + by_y.astype(F32) + far.astype(F32)
-    mine = mine.reshape(grid.live, share, total.shape[-1])
-    mine_low = mine.astype(BF16)
-    summed = lax.dynamic_index_in_dim(
-        mine, jnp.minimum(grid.z, grid.live - 1), 0, keepdims=False
+def lane(shape):
+    return lax.broadcasted_iota(jnp.int32, shape, 1)
+
+
+def own_place(ids):
+    return ids[0] * 4 + ids[1] * 2 + ids[3]
+
+
+def block_rows(number, rows):
+    return pl.ds(pl.multiple_of(number * rows, rows), rows)
+
+
+def student_kernel(ids, logits, labels, cols):
+    vocab = logits.shape[1]
+    rows = logits.shape[0] // 8
+    mine = own_place(ids)
+
+    def step(r, carry):
+        here = block_rows(r, rows)
+        block = logits[here, :]
+        top = jnp.max(block, axis=1, keepdims=True)
+        log = top + jnp.log(jnp.sum(jnp.exp(block - top), axis=1, keepdims=True))
+        hit = labels[here, :] - ids[4] * vocab == lane(block.shape)
+        value = jnp.sum(jnp.where(hit, block, 0.0), axis=1, keepdims=True)
+        places = lane((rows, 128))
+        cols[block_rows(mine ^ r, rows), :] = jnp.where(
+            places == 1, log, jnp.where(places == 3, value, 0.0)
+        )
+        return carry
+
+    lax.fori_loop(0, 8, step, 0)
+
+
+def teacher_kernel(ids, logits, s_logits, s_cols, sent, cols):
+    rows = logits.shape[0] // 8
+    mine = own_place(ids)
+
+    def step(r, carry):
+        here = block_rows(r, rows)
+        block = logits[here, :]
+        top = jnp.max(block, axis=1, keepdims=True)
+        weights = jnp.exp(block - top)
+        total = jnp.sum(weights, axis=1, keepdims=True)
+        mix = jnp.sum(weights * (block - s_logits[here, :]), axis=1, keepdims=True) / total
+        places = lane((rows, 128))
+        log = top + jnp.log(total)
+        there = block_rows(mine ^ r, rows)
+        cols[there, :] = jnp.where(
+            places == 0, log, jnp.where(places == 2, mix, s_cols[there, :])
+        )
+        return carry
+
+    lax.fori_loop(0, 8, step, 0, unroll=4)
+    turned = cols[...].T
+    message = jnp.concatenate([turned[n : n + 1, :] for n in range(4)], axis=1)
+    for d in range(sent.shape[0]):
+        sent[d] = message
+
+
+def joined(got, rows):
+    every = [got[d][:, : 2 * rows] for d in range(got.shape[0])]
+    top = functools.reduce(jnp.maximum, every)
+    return top + jnp.log(sum([jnp.exp(part - top) for part in every[1:]], jnp.exp(every[0] - top)))
+
+
+def product_into(out, grads, head):
+    height = head.shape[0] // 4
+
+    def step(n, carry):
+        here = block_rows(n, height)
+        value = lax.dot_general(
+            grads[...], head[here, :], (((1,), (1,)), ((), ())), preferred_element_type=F32
+        )
+        out[:, here] = value.astype(out.dtype)
+        return carry
+
+    lax.fori_loop(0, 4, step, 0)
+
+
+def given_kernel(
+    ids, got, labels, scale, t_logits, s_logits, head, given, kept, near, lines, columns, grads, sems
+):
+    vocab = t_logits.shape[1]
+    rows = t_logits.shape[0] // 8
+    part = head.shape[0] // 4
+    heads = [
+        pltpu.make_async_copy(
+            head.at[n * part : (n + 1) * part, :],
+            near.at[n * part : (n + 1) * part, :],
+            sems.at[n],
+        )
+        for n in range(4)
+    ]
+    for copy in heads:
+        copy.start()
+    total = joined(got, 8 * rows)
+    lines[...] = jnp.zeros_like(lines)
+    lines[0:1, :] = total[:, : 8 * rows]
+    lines[1:2, :] = total[:, 8 * rows :]
+    columns[...] = lines[...].T
+    mine = own_place(ids)
+    for r in range(8):
+        here = slice(r * rows, (r + 1) * rows)
+        logs = columns[block_rows(mine ^ r, rows), :]
+        t_prob = jnp.exp(t_logits[here, :] - logs[:, 0:1])
+        s_prob = jnp.exp(s_logits[here, :] - logs[:, 1:2])
+        hit = labels[here, :] - ids[4] * vocab == lane(t_prob.shape)
+        grad = scale[here, :] * ((1.0 + BETA) * s_prob - t_prob - BETA * hit.astype(F32))
+        place = (r // 4) * 2 + r % 2
+        into = grads if (r // 2) % 2 else kept
+        into[place * rows : (place + 1) * rows, :] = grad.astype(BF16)
+    for n, copy in enumerate(heads):
+        copy.wait()
+        here = slice(n * part, (n + 1) * part)
+        given[:, here] = lax.dot_general(
+            grads[...], near[here, :], (((1,), (1,)), ((), ())), preferred_element_type=F32
+        ).astype(BF16)
+
+
+def kept_kernel(ids, grads, head, out):
+    product_into(out, grads, head)
+
+
+def prep_kernel(live, share, nseq, ids, *refs):
+    packed, (labels, scale, weights, turned) = refs[:4], refs[4:]
+    tok = turned.shape[0]
+    places = lane((1, tok))
+    turned[...] = jnp.zeros_like(turned)
+    for g, ref in enumerate(packed):
+        start = jnp.zeros((1, 1), jnp.int32)
+        covered = jnp.zeros((1, tok), jnp.int32)
+        spans = jnp.zeros((1, tok), jnp.int32)
+        for n in range(nseq):
+            length = ref[:, tok + n : tok + n + 1]
+            inside = ((places >= start) & (places < start + length)).astype(jnp.int32)
+            covered = covered + inside
+            spans = spans + inside * length
+            start = start + length
+        weight = covered.astype(F32) / jnp.maximum(spans, 1).astype(F32)
+        if g == 0:
+            weights[...] = weight
+        turned[g : g + 1, :] = ref[:, :tok].astype(F32)
+        turned[4 + g : 5 + g, :] = LOSS_SCALE * weight
+    turned[...] = turned[...].T
+    for i in range(8):
+        g, d = i // 2, i % 2
+        for z in range(live):
+            there = slice((i * live + z) * share, (i * live + z + 1) * share)
+            here = block_rows(2 * z + (ids[3] ^ d), share)
+            block = turned[here, :]
+            labels[there, :] = block[:, g : g + 1].astype(jnp.int32)
+            scale[there, :] = block[:, 4 + g : 5 + g]
+
+
+def loss_kernel(live, share, ids, got, weights, loss):
+    tok = weights.shape[1]
+    rows = 8 * live * share
+    total = joined(got, rows)
+    t_log = total[:, :rows]
+    s_log = total[:, rows:]
+    cross, value = 0.0, 0.0
+    for d in range(got.shape[0]):
+        part = got[d]
+        cross = cross + jnp.exp(part[:, :rows] - t_log) * part[:, 2 * rows : 3 * rows]
+        value = value + part[:, 3 * rows :]
+    line = cross - t_log + s_log + BETA * (s_log - value)
+    slot = jnp.minimum(ids[2], live - 1)
+    at = (own_place(ids) * live + slot) * share
+    own = pltpu.roll(line, rows - at, 1)[:, :128]
+    weight = pltpu.roll(weights[...], tok - (2 * slot + ids[3]) * share, 1)[:, :128]
+    keep = (weight > 0) & (ids[2] < live)
+    loss[...] = jnp.where(keep, own, 0.0)
+
+
+def add_kernel(ids, kept, other, own, to_x, to_y, to_far):
+    rows = own.shape[0]
+    own[...] = kept[:rows, :] + other[:rows, :].astype(F32)
+    for i, out in ((1, to_x), (2, to_y), (3, to_far)):
+        here = slice(i * rows, (i + 1) * rows)
+        out[...] = (kept[here, :] + other[here, :].astype(F32)).astype(BF16)
+
+
+def chunk_kernel(live, ids, base, by_x, by_y, far, own, *lows):
+    share = own.shape[0]
+
+    def chunk(slot):
+        here = block_rows(jnp.minimum(slot, live - 1), share)
+        total = base[here, :] + by_x[here, :].astype(F32)
+        return total + by_y[here, :].astype(F32) + far[here, :].astype(F32)
+
+    own[...] = chunk(ids[2])
+    for k, low in enumerate(lows, 1):
+        low[...] = chunk(ids[2] ^ k).astype(BF16)
+
+
+def final_kernel(live, ids, own, *refs):
+    chunks, (hidden, gain, out) = refs[:-3], refs[-3:]
+    summed = own[...]
+    for chunk in chunks:
+        summed = summed + chunk[...].astype(F32)
+    out[...] = hidden_gradient(summed, hidden[...].astype(F32), gain[...])
+
+    @pl.when(ids[2] >= live)
+    def _():
+        out[...] = jnp.zeros_like(out)
+
+
+def hidden_gradient(summed, hidden, gain):
+    inverse = lax.rsqrt(jnp.mean(hidden * hidden, axis=-1, keepdims=True) + EPS)
+    scaled = summed * gain
+    inner = jnp.mean(scaled * hidden, axis=1, keepdims=True)
+    return inverse * scaled - hidden * (inverse * inverse * inverse) * inner
+
+
+def reduce_rows(grid, kept, other, share):
+    rows, width = kept.shape[0] // 4, kept.shape[1]
+    own, to_x, to_y, to_far = call(
+        add_kernel,
+        grid.ids,
+        [kept, other],
+        [shape_of((rows, width), F32)] + [shape_of((rows, width), BF16)] * 3,
+        [],
+        4,
     )
-    for k in range(1, grid.depth):
-        to = jnp.minimum(grid.z ^ k, grid.live - 1)
-        chunk = lax.dynamic_index_in_dim(mine_low, to, 0, keepdims=False)
-        chunk = grid.send(chunk, k=k, target=grid.live)
-        summed = summed + chunk.astype(F32)
-    return summed
+    by_x = grid.send(to_x, d=1)
+    by_y = grid.send(to_y, a=1)
+    far = grid.send(to_far, a=1, d=1)
+    ks = range(1, grid.depth)
+    if grid.tiled:
+        summed, *lows = call(
+            functools.partial(chunk_kernel, grid.live),
+            grid.ids,
+            [own, by_x, by_y, far],
+            [shape_of((share, width), F32)] + [shape_of((share, width), BF16) for k in ks],
+            [],
+            4,
+        )
+    else:
+        mine = own + by_x.astype(F32) + by_y.astype(F32) + far.astype(F32)
+        mine = mine.reshape(grid.live, share, width)
+        slots = [jnp.minimum(grid.z ^ k, grid.live - 1) for k in range(grid.depth)]
+        summed, *lows = [lax.dynamic_index_in_dim(mine, k, 0, keepdims=False) for k in slots]
+        lows = [low.astype(BF16) for low in lows]
+    return summed, [grid.send(low, k=k, target=grid.live) for k, low in zip(ks, lows)]
 
 
 def row_weights(lengths, tok_rows):
@@ -165,25 +392,6 @@
     spans = jnp.sum(jnp.where(inside, lengths[:, None, :], 0), axis=2)
     covered = jnp.sum(inside.astype(jnp.int32), axis=2)
     return covered.astype(F32) / jnp.maximum(spans, 1).astype(F32)
-
-
-def turn(grid, value):
-    for axis, at in ((1, grid.y), (2, grid.c), (3, grid.x)):
-        value = jnp.where(at == 1, jnp.flip(value, axis), value)
-    return value
-
-
-def exchange(grid, stats):
-    devices = 4 * grid.tp
-    flat = turn(grid, stats).reshape(-1)
-    sent = jnp.broadcast_to(flat[None], (devices, flat.shape[0])).reshape(-1)
-    got = lax.all_to_all(sent, AXES, 0, 0, tiled=True)
-    return got.reshape((devices,) + stats.shape)
-
-
-def join_logs(logs):
-    top = jnp.max(logs, axis=0)
-    return top + jnp.log(jnp.sum(jnp.exp(logs - top[None]), axis=0))
 
 
 def shards(
@@ -232,23 +440,39 @@
     others = [grid.send(low, k=k, target=live) for k, low in zip(ks, lows)]
 
     student_f = student_hidden.astype(F32)
-    student_scaled, inverse = norm_rows(student_f, student_gain)
-    student_norm = student_scaled.astype(BF16)
+    student_norm = norm_rows(student_f, student_gain)[0].astype(BF16)
     own_s = gather_depth(grid, student_norm)
     whole_s = gather_plane(grid, own_s)
 
     ints = jnp.concatenate([labels, lengths[0]])[None]
-    ints = jnp.concatenate([ints, grid.send(ints, b=1)], axis=0)
-    ints = jnp.concatenate([ints, grid.send(ints, a=1)], axis=0)
+    packed = [ints] + [grid.send(ints, a=a, b=b) for a, b in ((0, 1), (1, 0), (1, 1))]
 
     def by_row(value):
         value = value[:, :LIVE].reshape(4, live, 2, share)
         value = jnp.moveaxis(value, 2, 1)
         value = jnp.where(grid.x == 1, jnp.flip(value, 1), value)
-        return value.reshape(2, 2, 2, live * share)
-
-    label_rows = by_row(ints[:, :tok_rows])
-    weight_rows = by_row(row_weights(ints[:, tok_rows : tok_rows + nseq], tok_rows))
+        return value.reshape(-1)[:, None]
+
+    rows = 8 * live * share
+    if grid.tiled:
+        label_column, scale_column, weight_line = call(
+            functools.partial(prep_kernel, live, share, nseq),
+            grid.ids,
+            packed,
+            [
+                shape_of((rows, 1), jnp.int32),
+                shape_of((rows, 1), F32),
+                shape_of((1, tok_rows), F32),
+            ],
+            [pltpu.VMEM((tok_rows, 128), F32)],
+            4,
+        )
+    else:
+        whole = jnp.concatenate(packed, axis=0)
+        weight_rows = row_weights(whole[:, tok_rows : tok_rows + nseq], tok_rows)
+        label_column = by_row(whole[:, :tok_rows])
+        scale_column = by_row(LOSS_SCALE * weight_rows)
+        weight_line = weight_rows[:1]
 
     if grid.tiled:
         teacher_norm = call(
@@ -269,58 +493,70 @@
     own_t = gather_depth(grid, teacher_norm)
     whole_t = gather_plane(grid, own_t)
 
-    rows = whole_s.shape[0]
-    shape = label_rows.shape
     vocab_dev = student_head.shape[1]
-    position = lax.axis_index("dp") * lax.axis_size("tp") + lax.axis_index("tp")
-    columns = position * vocab_dev + jnp.arange(vocab_dev, dtype=jnp.int32)
-    hit = label_rows.reshape(rows)[:, None] == columns[None, :]
 
     s_logits = jnp.dot(whole_s, student_head, preferred_element_type=F32)
-    s_top = jnp.max(s_logits, axis=1)
-    s_own = s_top + jnp.log(jnp.sum(jnp.exp(s_logits - s_top[:, None]), axis=1))
-    s_label = jnp.sum(jnp.where(hit, s_logits, 0.0), axis=1)
-
+    s_cols = call(
+        student_kernel, grid.ids, [s_logits, label_column], [shape_of((rows, 128), F32)], [], 4
+    )[0]
     t_logits = jnp.dot(whole_t, teacher_head, preferred_element_type=F32)
-    t_top = jnp.max(t_logits, axis=1)
-    t_exp = jnp.exp(t_logits - t_top[:, None])
-    t_sum = jnp.sum(t_exp, axis=1)
-    t_mix = jnp.sum(t_exp * (t_logits - s_logits), axis=1) / t_sum
-    t_own = t_top + jnp.log(t_sum)
-
-    stats = exchange(grid, jnp.stack([t_own, t_mix, s_own, s_label]).reshape((4,) + shape))
-    t_log = join_logs(stats[:, 0])
-    t_cross = jnp.sum(jnp.exp(stats[:, 0] - t_log[None]) * stats[:, 1], axis=0)
-    s_log = join_logs(stats[:, 2])
-    label_value = jnp.sum(stats[:, 3], axis=0)
-    t_log, t_cross, s_log, label_value = turn(
-        grid, jnp.stack([t_log, t_cross, s_log, label_value])
+    devices = 4 * grid.tp
+    sent = call(
+        teacher_kernel,
+        grid.ids,
+        [t_logits, s_logits, s_cols],
+        [shape_of((devices, 1, 4 * rows), F32)],
+        [pltpu.VMEM((rows, 128), F32)],
+        8,
+    )[0]
+    got = lax.all_to_all(sent, AXES, 0, 0, tiled=True)
+
+    half = rows // 2
+    given, grads, near = call(
+        given_kernel,
+        grid.ids,
+        [got, label_column, scale_column, t_logits, s_logits],
+        [
+            shape_of((half, width_s), BF16),
+            shape_of((half, vocab_dev), BF16),
+            shape_of(student_head.shape, BF16),
+        ],
+        [
+            pltpu.VMEM((128, rows), F32),
+            pltpu.VMEM((rows, 128), F32),
+            pltpu.VMEM((half, vocab_dev), BF16),
+            pltpu.SemaphoreType.DMA((4,)),
+        ],
+        10,
+        [student_head],
     )
-    divergence = t_cross - t_log + s_log
-    label_term = s_log - label_value
-    row_loss = jnp.where(weight_rows > 0, divergence + BETA * label_term, 0.0)
-
-    def column(value):
-        return value.reshape(rows)[:, None]
-
-    t_prob = jnp.exp(t_logits - column(t_log))
-    s_prob = jnp.exp(s_logits - column(s_log))
-    scale = LOSS_SCALE * column(weight_rows)
-    logit_grad = (scale * ((1.0 + BETA) * s_prob - t_prob - BETA * hit.astype(F32))).astype(BF16)
-    partial = lax.dot_general(
-        logit_grad, student_head, (((1,), (1,)), ((), ())), preferred_element_type=F32
-    ).reshape(2, 2, 2, live * share, width_s)
-
-    other = grid.send(partial[:, 1].astype(BF16), b=1)
-    summed = reduce_rows(grid, partial[:, 0], other, share)
-
-    scaled = summed * student_gain
-    inner = jnp.mean(scaled * student_f, axis=1, keepdims=True)
-    grad_hidden = inverse * scaled - student_f * (inverse * inverse * inverse) * inner
-    own = grid.z < live
-    grad_hidden = jnp.where(own, grad_hidden, 0.0)
-    own_loss = lax.dynamic_slice_in_dim(row_loss[0, 0, 0], at * share, share, 0)
-    return (grad_hidden, jnp.where(own, own_loss, 0.0))
+    other = grid.send(given, b=1)
+    kept = call(kept_kernel, grid.ids, [grads, near], [shape_of((half, width_s), F32)], [], 4)[0]
+    summed, chunks = reduce_rows(grid, kept, other, share)
+    row_loss = call(
+        functools.partial(loss_kernel, live, share),
+        grid.ids,
+        [got, weight_line],
+        [shape_of((1, 128), F32)],
+        [],
+        4,
+    )[0]
+    if grid.tiled:
+        grad_hidden = call(
+            functools.partial(final_kernel, live),
+            grid.ids,
+            [summed, *chunks, student_hidden, student_gain[None]],
+            [jax.ShapeDtypeStruct((share, width_s), F32)],
+            [],
+            4,
+        )[0]
+    else:
+        for chunk in chunks:
+            summed = summed + chunk.astype(F32)
+        grad_hidden = jnp.where(
+            grid.z < live, hidden_gradient(summed, student_f, student_gain), 0.0
+        )
+    return (grad_hidden, row_loss[0, :share])
 
 
 def solution(mesh):

time: 162 us -> 161 us (level)
  Pallas kernels: 2.84 us -> 21 us
  blocking collectives: 0 us -> 15.5 us
  starting transfers between devices: 56.1 us -> 47.7 us
  other arithmetic: 11 us -> 2.83 us
  matrix products: 14.2 us -> 6.8 us
  local copies, waits for them, and re-layouts: 10.9 us -> 3.84 us
  waiting for transfers between devices: 65.1 us -> 61.5 us
    pallas_call x4 -> x13, Pallas kernels: 2.84 us -> 21 us  [call(): pl.pallas_call(kernel, out_shape=outs, in_specs=[SMEM] + [VMEM] * len(arg...]
    all_to_all x0 -> x1, blocking collectives: none -> 15.5 us  [shards(): got = lax.all_to_all(sent, AXES, 0, 0, tiled=True)]
    all_to_all x1 -> x0, starting transfers between devices: 8.11 us -> none  [exchange(): got = lax.all_to_all(sent, AXES, 0, 0, tiled=True)]
    all_to_all x1 -> x0, waiting for transfers between devices: 7.27 us -> none  [exchange(): got = lax.all_to_all(sent, AXES, 0, 0, tiled=True)]
    dot_general x1 -> x0, matrix products: 7.06 us -> none  [shards(): lax.dot_general(logit_grad, student_head, (((1,), (1,)), ((), ())), prefe...]
    ppermute x33 -> x34, waiting for transfers between devices: 57.9 us -> 61.5 us  [send(): return lax.ppermute(value, AXES, pairs)]
    select_n x10 -> x0, other arithmetic: 2.15 us -> none  [the longest x1 0.81 us: shards(): grad_hidden = jnp.where(own, grad_hidden, 0.0)]
    gt x2 -> x0, local copies, waits for them, and re-layouts: 1.94 us -> none  [shards(): row_loss = jnp.where(weight_rows > 0, divergence + BETA * label_term, 0.0)]
  transfers between devices with their start and end apart: 34 -> 34, of which waited for: 18 -> 15; matrix products, arithmetic and copies ran while one was open for 7% -> 5% of each run, Pallas kernels for 2% -> 7%
where the time goes in v1:
time: 161 us; the launch traced here: 160 us
  waiting for transfers between devices  61.5 us (38%)
  starting transfers between devices  47.7 us (30%)
  Pallas kernels  21 us (13%)
  blocking collectives  15.5 us (10%)
  matrix products  6.8 us (4%)
  local copies, waits for them, and re-layouts  3.84 us (2%)
  other arithmetic  2.83 us (2%)
    ppermute x34, waiting for transfers between devices, send(): return lax.ppermute(value, AXES, pairs)  61.5 us
    ppermute x34, starting transfers between devices, send(): return lax.ppermute(value, AXES, pairs)  47.7 us
    pallas_call x13, Pallas kernels, call(): pl.pallas_call(kernel, out_shape=outs, in_specs=[SMEM] + [VMEM] * len(arg...  21 us
    all_to_all x1, blocking collectives, shards(): got = lax.all_to_all(sent, AXES, 0, 0, tiled=True)  15.5 us
    dot_general x1, matrix products, shards(): t_logits = jnp.dot(whole_t, teacher_head, preferred_element_type=F32)  3.8 us
  transfers between devices with their start and end apart: 34, of which 15 were waited for; matrix products, arithmetic and copies ran while one was open for 5% of the time, Pallas kernels for 7%

profile of v1, /device:TPU:0, one launch (start us, length us, event | category | flops | bytes accessed | tf_op | source)
XLA Modules:
  0.0 160.3 jit_solution(14880359719505121388)
XLA Ops:
  0.7 1.1 fusion
  1.8 1.0 fusion.2.refs_0_
  2.8 5.0 %collective-permute-start.14 = (bf16[16,3584]{1,0:T(8,128)(2,1)S(1)}, bf16[16,3584]{1,0:T(8,128)(2,1)S(1)}, u32[]{:S(2)}, u32[]{:S(2)}) collective-permute-start(bf16[16,3584]{1,0:T(8,128)(2,1)S(1)} %fusion.2.refs_0_), channel_id=1, source_target_pairs={{0,2},{1,3},{2,0},{3,1},{4,6},{5,7},{8,10},{9,11},{10,8},{11,9},{1... | collective-permute-start | bytes 344072 | tf_op jit(solution)/shard_map/ppermute | solution.py:43
  7.8 4.5 %collective-permute-start.15 = (bf16[16,3584]{1,0:T(8,128)(2,1)S(1)}, bf16[16,3584]{1,0:T(8,128)(2,1)S(1)}, u32[]{:S(2)}, u32[]{:S(2)}) collective-permute-start(bf16[16,3584]{1,0:T(8,128)(2,1)S(1)} %fusion.2.refs_0_), channel_id=1, source_target_pairs={{0,4},{1,5},{2,6},{3,7},{4,0},{5,1},{8,12},{9,13},{10,14},{11,15},... | collective-permute-start | bytes 344072 | tf_op jit(solution)/shard_map/ppermute | solution.py:43
  12.3 1.3 collective-permute-start.16
  13.6 0.7 pad_add_fusion
  14.3 1.6 collective-permute-start.25
  15.9 1.2 slice.6
  17.2 0.7 broadcast_in_dim.14.refs_5_
  17.9 0.7 broadcast_in_dim.15.refs_6_
  18.7 0.3 collective-permute-start.26
  19.1 1.5 collective-permute-start
  20.6 1.1 collective-permute-done.26.refs_3_
  21.7 1.1 shard_map.117
  22.9 0.7 shard_map.116
  23.6 1.6 collective-permute-start.17
  25.1 0.5 collective-permute-start.20
  25.7 6.5 %collective-permute-done.other = bf16[3,16,4608]{2,1,0:T(8,128)(2,1)S(1)} collective-permute-done((bf16[3,16,4608]{2,1,0:T(8,128)(2,1)S(1)}, bf16[3,16,4608]{2,1,0:T(8,128)(2,1)S(1)}, u32[]{:S(2)}, u32[]{:S(2)}) %collective-permute-start) | collective-permute-done | bytes 442400 | tf_op jit(solution)/shard_map/ppermute | solution.py:43
  32.1 0.7 shard_map.113
  32.8 3.4 %collective-permute-start.1 = (bf16[16,4608]{1,0:T(8,128)(2,1)S(1)}, bf16[16,4608]{1,0:T(8,128)(2,1)S(1)}, u32[]{:S(2)}, u32[]{:S(2)}) collective-permute-start(bf16[16,4608]{1,0:T(8,128)(2,1)S(1)} %get-tuple-element.21), channel_id=1, source_target_pairs={{0,2},{1,3},{2,0},{3,1},{6,4},{7,5},{8,10},{9,11},{10,8},{11,9},{1... | collective-permute-start | bytes 442376 | tf_op jit(solution)/shard_map/ppermute | solution.py:43
  36.3 1.9 %collective-permute-start.2 = (bf16[16,4608]{1,0:T(8,128)(2,1)S(1)}, bf16[16,4608]{1,0:T(8,128)(2,1)S(1)}, u32[]{:S(2)}, u32[]{:S(2)}) collective-permute-start(bf16[16,4608]{1,0:T(8,128)(2,1)S(1)} %get-tuple-element.22), channel_id=1, source_target_pairs={{0,4},{1,5},{4,0},{5,1},{6,2},{7,3},{8,12},{9,13},{12,8},{13,9},{1... | collective-permute-start | bytes 442376 | tf_op jit(solution)/shard_map/ppermute | solution.py:43
  38.2 0.7 collective-permute-done.17
  38.9 1.3 collective-permute-start.3
  40.2 0.1 collective-permute-done.1.refs_1_
  40.3 2.4 %collective-permute-start.21 = (bf16[48,3584]{1,0:T(8,128)(2,1)S(1)}, bf16[48,3584]{1,0:T(8,128)(2,1)S(1)}, u32[]{:S(2)}, u32[]{:S(2)}) collective-permute-start(bf16[48,3584]{1,0:T(8,128)(2,1)S(1)} %shard_map.116), channel_id=1, source_target_pairs={{0,17},{1,16},{2,19},{3,18},{4,21},{5,20},{6,23},{7,22},{8,25},{9,... | collective-permute-start | bytes 1032200 | tf_op jit(solution)/shard_map/ppermute | solution.py:43
  42.8 7.7 %collective-permute-done.2.refs_2_ = bf16[16,4608]{1,0:T(8,128)(2,1)S(1)} collective-permute-done((bf16[16,4608]{1,0:T(8,128)(2,1)S(1)}, bf16[16,4608]{1,0:T(8,128)(2,1)S(1)}, u32[]{:S(2)}, u32[]{:S(2)}) %collective-permute-start.2) | collective-permute-done | bytes 147488 | tf_op jit(solution)/shard_map/ppermute | solution.py:43
  50.5 0.9 shard_map.114.refs_0_
  51.3 4.9 %collective-permute-start.4 = (bf16[16,4608]{1,0:T(8,128)(2,1)S(1)}, bf16[16,4608]{1,0:T(8,128)(2,1)S(1)}, u32[]{:S(2)}, u32[]{:S(2)}) collective-permute-start(bf16[16,4608]{1,0:T(8,128)(2,1)S(1)} %shard_map.114.refs_0_), channel_id=1, source_target_pairs={{0,2},{1,3},{2,0},{3,1},{4,6},{5,7},{8,10},{9,11},{10,8},{11,9},{1... | collective-permute-start | bytes 442376 | tf_op jit(solution)/shard_map/ppermute | solution.py:43
  56.2 1.9 %collective-permute-start.5 = (bf16[16,4608]{1,0:T(8,128)(2,1)S(1)}, bf16[16,4608]{1,0:T(8,128)(2,1)S(1)}, u32[]{:S(2)}, u32[]{:S(2)}) collective-permute-start(bf16[16,4608]{1,0:T(8,128)(2,1)S(1)} %shard_map.114.refs_0_), channel_id=1, source_target_pairs={{0,4},{1,5},{2,6},{3,7},{4,0},{5,1},{8,12},{9,13},{10,14},{11,15},... | collective-permute-start | bytes 442376 | tf_op jit(solution)/shard_map/ppermute | solution.py:43
  58.1 1.3 collective-permute-start.6
  59.6 0.5 collective-permute-start.22
  60.2 5.5 %collective-permute-done.5.refs_2_ = bf16[16,4608]{1,0:T(8,128)(2,1)S(1)} collective-permute-done((bf16[16,4608]{1,0:T(8,128)(2,1)S(1)}, bf16[16,4608]{1,0:T(8,128)(2,1)S(1)}, u32[]{:S(2)}, u32[]{:S(2)}) %collective-permute-start.5) | collective-permute-done | bytes 147488 | tf_op jit(solution)/shard_map/ppermute | solution.py:43
  65.7 0.7 shard_map.115
  66.4 1.6 collective-permute-start.7
  68.0 1.6 collective-permute-start.10
  69.7 0.5 collective-permute-start.11
  70.3 3.0 %fusion.4.logits.s_logits = f32[384,1024]{1,0:T(8,128)S(1)} fusion(bf16[384,3584]{1,0:T(8,128)(2,1)S(1)} %constant_dynamic-update-slice_fusion.8, bf16[3584,1024]{1,0:T(8,128)(2,1)S(1)} %copy-done.3), kind=kOutput, calls=%fused_computation.26 | convolution fusion | flops 2818572288 | bytes 11665408 | tf_op jit(solution)/shard_map/dot_general | solution.py:498
  73.3 2.3 %shard_map.118.s_cols = f32[384,128]{1,0:T(8,128)S(1)} custom-call(s32[5]{0:T(128)S(1)} %stack.23.ids, f32[384,1024]{1,0:T(8,128)S(1)} %fusion.4.logits.s_logits, s32[384,1]{1,0:T(8,128)S(1)} %get-tuple-element.24.labels), custom_call_target="tpu_custom_call" | custom-call | tf_op jit(solution)/shard_map/pallas_call | solution.py:69
  75.7 3.8 %collective-permute-done.7 = bf16[48,4608]{1,0:T(8,128)(2,1)S(1)} collective-permute-done((bf16[48,4608]{1,0:T(8,128)(2,1)S(1)}, bf16[48,4608]{1,0:T(8,128)(2,1)S(1)}, u32[]{:S(2)}, u32[]{:S(2)}) %collective-permute-start.7) | collective-permute-done | bytes 442400 | tf_op jit(solution)/shard_map/ppermute | solution.py:43
  79.5 10.6 %collective-permute-done.10 = bf16[48,4608]{1,0:T(8,128)(2,1)S(1)} collective-permute-done((bf16[48,4608]{1,0:T(8,128)(2,1)S(1)}, bf16[48,4608]{1,0:T(8,128)(2,1)S(1)}, u32[]{:S(2)}, u32[]{:S(2)}) %collective-permute-start.10) | collective-permute-done | bytes 442400 | tf_op jit(solution)/shard_map/ppermute | solution.py:43
  90.1 0.5 collective-permute-start.13
  90.8 1.1 collective-permute-done.12
  91.9 0.6 collective-permute-done.13
  92.6 3.8 %fusion.3.logits.t_logits = f32[384,1024]{1,0:T(8,128)S(1)} fusion(bf16[384,4608]{1,0:T(8,128)(2,1)S(1)} %constant_dynamic-update-slice_fusion, bf16[4608,1024]{1,0:T(8,128)(2,1)S(1)} %bitcast.25), kind=kOutput, calls=%fused_computation.25 | convolution fusion | flops 3623878656 | bytes 14548992 | tf_op jit(solution)/shard_map/dot_general | solution.py:502
  96.4 1.4 shard_map.119
  97.8 15.5 %all_to_all.5.got = f32[32,1,1536]{2,1,0:T(1,128)S(1)} all-to-all(f32[32,1,1536]{2,1,0:T(1,128)S(1)} %shard_map.119), channel_id=1, replica_groups=mesh['dp'=4,'tp'=8] {'dp','tp'}, dimensions={0} | all-to-all | bytes 393216 | tf_op jit(solution)/shard_map/all_to_all | solution.py:512
  113.3 5.9 %shard_map.120 = (bf16[192,3584]{1,0:T(8,128)(2,1)S(1)}, bf16[192,1024]{1,0:T(8,128)(2,1)S(1)}, bf16[3584,1024]{1,0:T(8,128)(2,1)S(1)}) custom-call(s32[5]{0:T(128)S(1)} %stack.23.ids, f32[32,1,1536]{2,1,0:T(1,128)S(1)} %all_to_all.5.got, s32[384,1]{1,0:T(8,128)S(1)} %get-tuple-element.24.labels, f32[384,1]{1,0:T(8,128)S(1)} %get-tuple-element.25.scale, ...), custom_call_target="tpu_custom_call" | custom-call | tf_op jit(solution)/shard_map/pallas_call | solution.py:69
  119.2 0.5 collective-permute-start.27
  119.7 3.7 %shard_map.121.kept = f32[192,3584]{1,0:T(8,128)S(1)} custom-call(s32[5]{0:T(128)S(1)} %stack.23.ids, bf16[192,1024]{1,0:T(8,128)(2,1)S(1)} %get-tuple-element.26.grads, bf16[3584,1024]{1,0:T(8,128)(2,1)S(1)} %get-tuple-element.27.head), custom_call_target="tpu_custom_call" | custom-call | tf_op jit(solution)/shard_map/pallas_call | solution.py:69
  123.4 0.8 shard_map.122
  124.2 1.8 %collective-permute-start.28 = (bf16[48,3584]{1,0:T(8,128)(2,1)S(1)}, bf16[48,3584]{1,0:T(8,128)(2,1)S(1)}, u32[]{:S(2)}, u32[]{:S(2)}) collective-permute-start(bf16[48,3584]{1,0:T(8,128)(2,1)S(1)} %get-tuple-element.30), channel_id=1, source_target_pairs={{0,1},{1,0},{2,3},{3,2},{4,5},{5,4},{6,7},{7,6},{8,9},{9,8},{10,11... | collective-permute-start | bytes 1032200 | tf_op jit(solution)/shard_map/ppermute | solution.py:43
  125.9 0.5 collective-permute-start.29
  126.5 1.2 collective-permute-start.30
  127.7 0.7 shard_map.125
  128.5 6.7 %collective-permute-done.28.by_x = bf16[48,3584]{1,0:T(8,128)(2,1)S(1)} collective-permute-done((bf16[48,3584]{1,0:T(8,128)(2,1)S(1)}, bf16[48,3584]{1,0:T(8,128)(2,1)S(1)}, u32[]{:S(2)}, u32[]{:S(2)}) %collective-permute-start.28) | collective-permute-done | bytes 344096 | tf_op jit(solution)/shard_map/ppermute | solution.py:43
  135.2 8.2 %collective-permute-done.29.by_y = bf16[48,3584]{1,0:T(8,128)(2,1)S(1)} collective-permute-done((bf16[48,3584]{1,0:T(8,128)(2,1)S(1)}, bf16[48,3584]{1,0:T(8,128)(2,1)S(1)}, u32[]{:S(2)}, u32[]{:S(2)}) %collective-permute-start.29) | collective-permute-done | bytes 344096 | tf_op jit(solution)/shard_map/ppermute | solution.py:43
  143.4 0.7 shard_map.123
  144.1 2.3 %collective-permute-start.31 = (bf16[16,3584]{1,0:T(8,128)(2,1)S(1)}, bf16[16,3584]{1,0:T(8,128)(2,1)S(1)}, u32[]{:S(2)}, u32[]{:S(2)}) collective-permute-start(bf16[16,3584]{1,0:T(8,128)(2,1)S(1)} %get-tuple-element.34), channel_id=1, source_target_pairs={{0,2},{1,3},{2,0},{3,1},{6,4},{7,5},{8,10},{9,11},{10,8},{11,9},{1... | collective-permute-start | bytes 344072 | tf_op jit(solution)/shard_map/ppermute | solution.py:43
  146.4 1.9 %collective-permute-start.32 = (bf16[16,3584]{1,0:T(8,128)(2,1)S(1)}, bf16[16,3584]{1,0:T(8,128)(2,1)S(1)}, u32[]{:S(2)}, u32[]{:S(2)}) collective-permute-start(bf16[16,3584]{1,0:T(8,128)(2,1)S(1)} %get-tuple-element.35), channel_id=1, source_target_pairs={{0,4},{1,5},{4,0},{5,1},{6,2},{7,3},{8,12},{9,13},{12,8},{13,9},{1... | collective-permute-start | bytes 344072 | tf_op jit(solution)/shard_map/ppermute | solution.py:43
  148.3 1.3 collective-permute-start.33
  149.6 0.5 slice_bitcast_fusion
  150.1 0.7 collective-permute-done.31.refs_0_
  150.8 8.1 %collective-permute-done.32.refs_1_ = bf16[16,3584]{1,0:T(8,128)(2,1)S(1)} collective-permute-done((bf16[16,3584]{1,0:T(8,128)(2,1)S(1)}, bf16[16,3584]{1,0:T(8,128)(2,1)S(1)}, u32[]{:S(2)}, u32[]{:S(2)}) %collective-permute-start.32) | collective-permute-done | bytes 114720 | tf_op jit(solution)/shard_map/ppermute | solution.py:43
  158.9 1.4 shard_map.124
  (64 shorter events, 0.8 us)
Async XLA Ops:
  0.6 31.5 %copy-start = (bf16[1,128,4608]{2,1,0:T(8,128)(2,1)S(1)}, bf16[1,128,4608]{2,1,0:T(8,128)(2,1)}, u32[]{:S(2)}) copy-start(bf16[1,128,4608]{2,1,0:T(8,128)(2,1)} %partial.1) | copy-start | bytes 3538948
  0.6 49.8 %copy-start.2 = (bf16[16,4608]{1,0:T(8,128)(2,1)S(1)}, bf16[16,4608]{1,0:T(8,128)(2,1)}, u32[]{:S(2)}) copy-start(bf16[16,4608]{1,0:T(8,128)(2,1)} %refs_4_.1) | copy-start | bytes 442372
  2.8 20.1 %collective-permute-start.14 = (bf16[16,3584]{1,0:T(8,128)(2,1)S(1)}, bf16[16,3584]{1,0:T(8,128)(2,1)S(1)}, u32[]{:S(2)}, u32[]{:S(2)}) collective-permute-start(bf16[16,3584]{1,0:T(8,128)(2,1)S(1)} %fusion.2.refs_0_), channel_id=1, source_target_pairs={{0,2},{1,3},{2,0},{3,1},{4,6},{5,7},{8,10},{9,11},{10,8},{11,9},{1... | collective-permute-start | bytes 344072 | tf_op jit(solution)/shard_map/ppermute | solution.py:43
  7.8 15.1 %collective-permute-start.15 = (bf16[16,3584]{1,0:T(8,128)(2,1)S(1)}, bf16[16,3584]{1,0:T(8,128)(2,1)S(1)}, u32[]{:S(2)}, u32[]{:S(2)}) collective-permute-start(bf16[16,3584]{1,0:T(8,128)(2,1)S(1)} %fusion.2.refs_0_), channel_id=1, source_target_pairs={{0,4},{1,5},{2,6},{3,7},{4,0},{5,1},{8,12},{9,13},{10,14},{11,15},... | collective-permute-start | bytes 344072 | tf_op jit(solution)/shard_map/ppermute | solution.py:43
  12.3 10.6 %collective-permute-start.16 = (bf16[16,3584]{1,0:T(8,128)(2,1)S(1)}, bf16[16,3584]{1,0:T(8,128)(2,1)S(1)}, u32[]{:S(2)}, u32[]{:S(2)}) collective-permute-start(bf16[16,3584]{1,0:T(8,128)(2,1)S(1)} %fusion.2.refs_0_), channel_id=1, source_target_pairs={{0,6},{1,7},{2,4},{3,5},{4,2},{5,3},{8,14},{9,15},{10,12},{11,13},... | collective-permute-start | bytes 344072 | tf_op jit(solution)/shard_map/ppermute | solution.py:43
  14.3 4.4 %collective-permute-start.24 = (s32[1,136]{1,0:T(1,128)S(1)}, s32[1,136]{1,0:T(1,128)S(1)}, u32[]{:S(2)}, u32[]{:S(2)}) collective-permute-start(s32[1,136]{1,0:T(1,128)S(1)} %bitcast.18), channel_id=1, source_target_pairs={{0,8},{1,9},{2,10},{3,11},{4,12},{5,13},{6,14},{7,15},{8,0},{9,1},... | collective-permute-start | bytes 1640 | tf_op jit(solution)/shard_map/ppermute | solution.py:43
  14.3 4.8 %collective-permute-start.25 = (s32[1,136]{1,0:T(1,128)S(1)}, s32[1,136]{1,0:T(1,128)S(1)}, u32[]{:S(2)}, u32[]{:S(2)}) collective-permute-start(s32[1,136]{1,0:T(1,128)S(1)} %bitcast.19), channel_id=1, source_target_pairs={{0,16},{1,17},{2,18},{3,19},{4,20},{5,21},{6,22},{7,23},{8,24},{9,... | collective-permute-start | bytes 1640 | tf_op jit(solution)/shard_map/ppermute | solution.py:43
  18.7 3.1 %collective-permute-start.26 = (s32[1,136]{1,0:T(1,128)S(1)}, s32[1,136]{1,0:T(1,128)S(1)}, u32[]{:S(2)}, u32[]{:S(2)}) collective-permute-start(s32[1,136]{1,0:T(1,128)S(1)} %bitcast.20), channel_id=1, source_target_pairs={{0,24},{1,25},{2,26},{3,27},{4,28},{5,29},{6,30},{7,31},{8,16},{9,... | collective-permute-start | bytes 1640 | tf_op jit(solution)/shard_map/ppermute | solution.py:43
  19.1 13.0 %collective-permute-start = (bf16[3,16,4608]{2,1,0:T(8,128)(2,1)S(1)}, bf16[3,16,4608]{2,1,0:T(8,128)(2,1)S(1)}, u32[]{:S(2)}, u32[]{:S(2)}) collective-permute-start(bf16[3,16,4608]{2,1,0:T(8,128)(2,1)S(1)} %dynamic-slice_bitcast_fusion), channel_id=1, source_target_pairs={{0,1},{1,0},{2,3},{3,2},{4,5},{5,4},{6,7},{7,6},{8,9},{9,8},{10,11... | collective-permute-start | bytes 1327112 | tf_op jit(solution)/shard_map/ppermute | solution.py:43
  23.6 15.3 %collective-permute-start.17 = (bf16[48,3584]{1,0:T(8,128)(2,1)S(1)}, bf16[48,3584]{1,0:T(8,128)(2,1)S(1)}, u32[]{:S(2)}, u32[]{:S(2)}) collective-permute-start(bf16[48,3584]{1,0:T(8,128)(2,1)S(1)} %shard_map.116), channel_id=1, source_target_pairs={{0,1},{1,0},{2,3},{3,2},{4,5},{5,4},{6,7},{7,6},{8,9},{9,8},{10,11... | collective-permute-start | bytes 1032200 | tf_op jit(solution)/shard_map/ppermute | solution.py:43
  25.1 33.0 %collective-permute-start.18 = (bf16[48,3584]{1,0:T(8,128)(2,1)S(1)}, bf16[48,3584]{1,0:T(8,128)(2,1)S(1)}, u32[]{:S(2)}, u32[]{:S(2)}) collective-permute-start(bf16[48,3584]{1,0:T(8,128)(2,1)S(1)} %shard_map.116), channel_id=1, source_target_pairs={{0,8},{1,9},{2,10},{3,11},{4,12},{5,13},{6,14},{7,15},{8,0},{9,1},... | collective-permute-start | bytes 1032200 | tf_op jit(solution)/shard_map/ppermute | solution.py:43
  25.1 34.4 %collective-permute-start.20 = (bf16[48,3584]{1,0:T(8,128)(2,1)S(1)}, bf16[48,3584]{1,0:T(8,128)(2,1)S(1)}, u32[]{:S(2)}, u32[]{:S(2)}) collective-permute-start(bf16[48,3584]{1,0:T(8,128)(2,1)S(1)} %shard_map.116), channel_id=1, source_target_pairs={{0,16},{1,17},{2,18},{3,19},{4,20},{5,21},{6,22},{7,23},{8,24},{9,... | collective-permute-start | bytes 1032200 | tf_op jit(solution)/shard_map/ppermute | solution.py:43
  32.8 7.5 %collective-permute-start.1 = (bf16[16,4608]{1,0:T(8,128)(2,1)S(1)}, bf16[16,4608]{1,0:T(8,128)(2,1)S(1)}, u32[]{:S(2)}, u32[]{:S(2)}) collective-permute-start(bf16[16,4608]{1,0:T(8,128)(2,1)S(1)} %get-tuple-element.21), channel_id=1, source_target_pairs={{0,2},{1,3},{2,0},{3,1},{6,4},{7,5},{8,10},{9,11},{10,8},{11,9},{1... | collective-permute-start | bytes 442376 | tf_op jit(solution)/shard_map/ppermute | solution.py:43
  36.3 14.2 %collective-permute-start.2 = (bf16[16,4608]{1,0:T(8,128)(2,1)S(1)}, bf16[16,4608]{1,0:T(8,128)(2,1)S(1)}, u32[]{:S(2)}, u32[]{:S(2)}) collective-permute-start(bf16[16,4608]{1,0:T(8,128)(2,1)S(1)} %get-tuple-element.22), channel_id=1, source_target_pairs={{0,4},{1,5},{4,0},{5,1},{6,2},{7,3},{8,12},{9,13},{12,8},{13,9},{1... | collective-permute-start | bytes 442376 | tf_op jit(solution)/shard_map/ppermute | solution.py:43
  38.9 11.6 %collective-permute-start.3 = (bf16[16,4608]{1,0:T(8,128)(2,1)S(1)}, bf16[16,4608]{1,0:T(8,128)(2,1)S(1)}, u32[]{:S(2)}, u32[]{:S(2)}) collective-permute-start(bf16[16,4608]{1,0:T(8,128)(2,1)S(1)} %get-tuple-element.23), channel_id=1, source_target_pairs={{2,4},{3,5},{4,2},{5,3},{6,0},{7,1},{10,12},{11,13},{12,10},{13,11... | collective-permute-start | bytes 442376 | tf_op jit(solution)/shard_map/ppermute | solution.py:43
  40.2 30.1 %copy-start.3 = (bf16[3584,1024]{1,0:T(8,128)(2,1)S(1)}, bf16[3584,1024]{1,0:T(8,128)(2,1)}, u32[]{:S(2)}) copy-start(bf16[3584,1024]{1,0:T(8,128)(2,1)} %head.1) | copy-start | bytes 22020100
  40.3 19.3 %collective-permute-start.21 = (bf16[48,3584]{1,0:T(8,128)(2,1)S(1)}, bf16[48,3584]{1,0:T(8,128)(2,1)S(1)}, u32[]{:S(2)}, u32[]{:S(2)}) collective-permute-start(bf16[48,3584]{1,0:T(8,128)(2,1)S(1)} %shard_map.116), channel_id=1, source_target_pairs={{0,17},{1,16},{2,19},{3,18},{4,21},{5,20},{6,23},{7,22},{8,25},{9,... | collective-permute-start | bytes 1032200 | tf_op jit(solution)/shard_map/ppermute | solution.py:43
  51.3 8.8 %collective-permute-start.4 = (bf16[16,4608]{1,0:T(8,128)(2,1)S(1)}, bf16[16,4608]{1,0:T(8,128)(2,1)S(1)}, u32[]{:S(2)}, u32[]{:S(2)}) collective-permute-start(bf16[16,4608]{1,0:T(8,128)(2,1)S(1)} %shard_map.114.refs_0_), channel_id=1, source_target_pairs={{0,2},{1,3},{2,0},{3,1},{4,6},{5,7},{8,10},{9,11},{10,8},{11,9},{1... | collective-permute-start | bytes 442376 | tf_op jit(solution)/shard_map/ppermute | solution.py:43
  56.2 9.5 %collective-permute-start.5 = (bf16[16,4608]{1,0:T(8,128)(2,1)S(1)}, bf16[16,4608]{1,0:T(8,128)(2,1)S(1)}, u32[]{:S(2)}, u32[]{:S(2)}) collective-permute-start(bf16[16,4608]{1,0:T(8,128)(2,1)S(1)} %shard_map.114.refs_0_), channel_id=1, source_target_pairs={{0,4},{1,5},{2,6},{3,7},{4,0},{5,1},{8,12},{9,13},{10,14},{11,15},... | collective-permute-start | bytes 442376 | tf_op jit(solution)/shard_map/ppermute | solution.py:43
  58.1 7.6 %collective-permute-start.6 = (bf16[16,4608]{1,0:T(8,128)(2,1)S(1)}, bf16[16,4608]{1,0:T(8,128)(2,1)S(1)}, u32[]{:S(2)}, u32[]{:S(2)}) collective-permute-start(bf16[16,4608]{1,0:T(8,128)(2,1)S(1)} %shard_map.114.refs_0_), channel_id=1, source_target_pairs={{0,6},{1,7},{2,4},{3,5},{4,2},{5,3},{8,14},{9,15},{10,12},{11,13},... | collective-permute-start | bytes 442376 | tf_op jit(solution)/shard_map/ppermute | solution.py:43
  59.5 8.5 %collective-permute-start.19 = (bf16[48,3584]{1,0:T(8,128)(2,1)S(1)}, bf16[48,3584]{1,0:T(8,128)(2,1)S(1)}, u32[]{:S(2)}, u32[]{:S(2)}) collective-permute-start(bf16[48,3584]{1,0:T(8,128)(2,1)S(1)} %collective-permute-done.17), channel_id=1, source_target_pairs={{0,8},{1,9},{2,10},{3,11},{4,12},{5,13},{6,14},{7,15},{8,0},{9,1},... | collective-permute-start | bytes 1032200 | tf_op jit(solution)/shard_map/ppermute | solution.py:43
  59.6 10.1 %collective-permute-start.22 = (bf16[48,3584]{1,0:T(8,128)(2,1)S(1)}, bf16[48,3584]{1,0:T(8,128)(2,1)S(1)}, u32[]{:S(2)}, u32[]{:S(2)}) collective-permute-start(bf16[48,3584]{1,0:T(8,128)(2,1)S(1)} %collective-permute-done.20), channel_id=1, source_target_pairs={{0,8},{1,9},{2,10},{3,11},{4,12},{5,13},{6,14},{7,15},{8,0},{9,1},... | collective-permute-start | bytes 1032200 | tf_op jit(solution)/shard_map/ppermute | solution.py:43
  60.1 10.1 %collective-permute-start.23 = (bf16[48,3584]{1,0:T(8,128)(2,1)S(1)}, bf16[48,3584]{1,0:T(8,128)(2,1)S(1)}, u32[]{:S(2)}, u32[]{:S(2)}) collective-permute-start(bf16[48,3584]{1,0:T(8,128)(2,1)S(1)} %collective-permute-done.21), channel_id=1, source_target_pairs={{0,8},{1,9},{2,10},{3,11},{4,12},{5,13},{6,14},{7,15},{8,0},{9,1},... | collective-permute-start | bytes 1032200 | tf_op jit(solution)/shard_map/ppermute | solution.py:43
  66.4 13.1 %collective-permute-start.7 = (bf16[48,4608]{1,0:T(8,128)(2,1)S(1)}, bf16[48,4608]{1,0:T(8,128)(2,1)S(1)}, u32[]{:S(2)}, u32[]{:S(2)}) collective-permute-start(bf16[48,4608]{1,0:T(8,128)(2,1)S(1)} %shard_map.115), channel_id=1, source_target_pairs={{0,1},{1,0},{2,3},{3,2},{4,5},{5,4},{6,7},{7,6},{8,9},{9,8},{10,11... | collective-permute-start | bytes 1327112 | tf_op jit(solution)/shard_map/ppermute | solution.py:43
  67.9 22.7 %collective-permute-start.8 = (bf16[48,4608]{1,0:T(8,128)(2,1)S(1)}, bf16[48,4608]{1,0:T(8,128)(2,1)S(1)}, u32[]{:S(2)}, u32[]{:S(2)}) collective-permute-start(bf16[48,4608]{1,0:T(8,128)(2,1)S(1)} %shard_map.115), channel_id=1, source_target_pairs={{0,8},{1,9},{2,10},{3,11},{4,12},{5,13},{6,14},{7,15},{8,0},{9,1},... | collective-permute-start | bytes 1327112 | tf_op jit(solution)/shard_map/ppermute | solution.py:43
  68.0 22.1 %collective-permute-start.10 = (bf16[48,4608]{1,0:T(8,128)(2,1)S(1)}, bf16[48,4608]{1,0:T(8,128)(2,1)S(1)}, u32[]{:S(2)}, u32[]{:S(2)}) collective-permute-start(bf16[48,4608]{1,0:T(8,128)(2,1)S(1)} %shard_map.115), channel_id=1, source_target_pairs={{0,16},{1,17},{2,18},{3,19},{4,20},{5,21},{6,22},{7,23},{8,24},{9,... | collective-permute-start | bytes 1327112 | tf_op jit(solution)/shard_map/ppermute | solution.py:43
  69.7 20.4 %collective-permute-start.11 = (bf16[48,4608]{1,0:T(8,128)(2,1)S(1)}, bf16[48,4608]{1,0:T(8,128)(2,1)S(1)}, u32[]{:S(2)}, u32[]{:S(2)}) collective-permute-start(bf16[48,4608]{1,0:T(8,128)(2,1)S(1)} %shard_map.115), channel_id=1, source_target_pairs={{0,17},{1,16},{2,19},{3,18},{4,21},{5,20},{6,23},{7,22},{8,25},{9,... | collective-permute-start | bytes 1327112 | tf_op jit(solution)/shard_map/ppermute | solution.py:43
  70.2 22.3 %slice-start = ((s8[9437184]{0:T(1024)(128)(4,1)}), s8[4194304]{0:T(1024)(128)(4,1)S(1)}, s32[]{:S(2)}) async-start(s8[9437184]{0:T(1024)(128)(4,1)} %bitcast.24), calls=%async_computation.1 | async-start | bytes 8388608
  70.3 22.3 %slice-start.1 = ((s8[9437184]{0:T(1024)(128)(4,1)}), s8[4194304]{0:T(1024)(128)(4,1)S(1)}, s32[]{:S(2)}) async-start(s8[9437184]{0:T(1024)(128)(4,1)} %bitcast.24), calls=%async_computation.2 | async-start | bytes 8388608
  70.3 22.3 %slice-start.2 = ((s8[9437184]{0:T(1024)(128)(4,1)}), s8[1048576]{0:T(1024)(128)(4,1)S(1)}, s32[]{:S(2)}) async-start(s8[9437184]{0:T(1024)(128)(4,1)} %bitcast.24), calls=%async_computation.3 | async-start | bytes 2097152
  79.5 11.2 %collective-permute-start.9 = (bf16[48,4608]{1,0:T(8,128)(2,1)S(1)}, bf16[48,4608]{1,0:T(8,128)(2,1)S(1)}, u32[]{:S(2)}, u32[]{:S(2)}) collective-permute-start(bf16[48,4608]{1,0:T(8,128)(2,1)S(1)} %collective-permute-done.7), channel_id=1, source_target_pairs={{0,8},{1,9},{2,10},{3,11},{4,12},{5,13},{6,14},{7,15},{8,0},{9,1},... | collective-permute-start | bytes 1327112 | tf_op jit(solution)/shard_map/ppermute | solution.py:43
  90.1 1.8 %collective-permute-start.12 = (bf16[48,4608]{1,0:T(8,128)(2,1)S(1)}, bf16[48,4608]{1,0:T(8,128)(2,1)S(1)}, u32[]{:S(2)}, u32[]{:S(2)}) collective-permute-start(bf16[48,4608]{1,0:T(8,128)(2,1)S(1)} %collective-permute-done.10), channel_id=1, source_target_pairs={{0,8},{1,9},{2,10},{3,11},{4,12},{5,13},{6,14},{7,15},{8,0},{9,1},... | collective-permute-start | bytes 1327112 | tf_op jit(solution)/shard_map/ppermute | solution.py:43
  90.1 2.4 %collective-permute-start.13 = (bf16[48,4608]{1,0:T(8,128)(2,1)S(1)}, bf16[48,4608]{1,0:T(8,128)(2,1)S(1)}, u32[]{:S(2)}, u32[]{:S(2)}) collective-permute-start(bf16[48,4608]{1,0:T(8,128)(2,1)S(1)} %collective-permute-done.11), channel_id=1, source_target_pairs={{0,8},{1,9},{2,10},{3,11},{4,12},{5,13},{6,14},{7,15},{8,0},{9,1},... | collective-permute-start | bytes 1327112 | tf_op jit(solution)/shard_map/ppermute | solution.py:43
  119.2 4.2 %collective-permute-start.27 = (bf16[192,3584]{1,0:T(8,128)(2,1)S(1)}, bf16[192,3584]{1,0:T(8,128)(2,1)S(1)}, u32[]{:S(2)}, u32[]{:S(2)}) collective-permute-start(bf16[192,3584]{1,0:T(8,128)(2,1)S(1)} %get-tuple-element.28), channel_id=1, source_target_pairs={{0,8},{1,9},{2,10},{3,11},{4,12},{5,13},{6,14},{7,15},{8,0},{9,1},... | collective-permute-start | bytes 4128776 | tf_op jit(solution)/shard_map/ppermute | solution.py:43
  123.3 4.4 %copy-start.4 = (f32[3584]{0:T(1024)S(1)}, f32[3584]{0:T(1024)}, u32[]{:S(2)}) copy-start(f32[3584]{0:T(1024)} %param.16) | copy-start | bytes 43012
  123.4 35.5 %copy-start.1 = (bf16[16,3584]{1,0:T(8,128)(2,1)S(1)}, bf16[16,3584]{1,0:T(8,128)(2,1)}, u32[]{:S(2)}) copy-start(bf16[16,3584]{1,0:T(8,128)(2,1)} %refs_3_.1) | copy-start | bytes 344068
  124.2 11.0 %collective-permute-start.28 = (bf16[48,3584]{1,0:T(8,128)(2,1)S(1)}, bf16[48,3584]{1,0:T(8,128)(2,1)S(1)}, u32[]{:S(2)}, u32[]{:S(2)}) collective-permute-start(bf16[48,3584]{1,0:T(8,128)(2,1)S(1)} %get-tuple-element.30), channel_id=1, source_target_pairs={{0,1},{1,0},{2,3},{3,2},{4,5},{5,4},{6,7},{7,6},{8,9},{9,8},{10,11... | collective-permute-start | bytes 1032200 | tf_op jit(solution)/shard_map/ppermute | solution.py:43
  125.9 17.5 %collective-permute-start.29 = (bf16[48,3584]{1,0:T(8,128)(2,1)S(1)}, bf16[48,3584]{1,0:T(8,128)(2,1)S(1)}, u32[]{:S(2)}, u32[]{:S(2)}) collective-permute-start(bf16[48,3584]{1,0:T(8,128)(2,1)S(1)} %get-tuple-element.31), channel_id=1, source_target_pairs={{0,16},{1,17},{2,18},{3,19},{4,20},{5,21},{6,22},{7,23},{8,24},{9,... | collective-permute-start | bytes 1032200 | tf_op jit(solution)/shard_map/ppermute | solution.py:43
  126.5 16.9 %collective-permute-start.30 = (bf16[48,3584]{1,0:T(8,128)(2,1)S(1)}, bf16[48,3584]{1,0:T(8,128)(2,1)S(1)}, u32[]{:S(2)}, u32[]{:S(2)}) collective-permute-start(bf16[48,3584]{1,0:T(8,128)(2,1)S(1)} %get-tuple-element.32), channel_id=1, source_target_pairs={{0,17},{1,16},{2,19},{3,18},{4,21},{5,20},{6,23},{7,22},{8,25},{9,... | collective-permute-start | bytes 1032200 | tf_op jit(solution)/shard_map/ppermute | solution.py:43
  144.1 6.7 %collective-permute-start.31 = (bf16[16,3584]{1,0:T(8,128)(2,1)S(1)}, bf16[16,3584]{1,0:T(8,128)(2,1)S(1)}, u32[]{:S(2)}, u32[]{:S(2)}) collective-permute-start(bf16[16,3584]{1,0:T(8,128)(2,1)S(1)} %get-tuple-element.34), channel_id=1, source_target_pairs={{0,2},{1,3},{2,0},{3,1},{6,4},{7,5},{8,10},{9,11},{10,8},{11,9},{1... | collective-permute-start | bytes 344072 | tf_op jit(solution)/shard_map/ppermute | solution.py:43
  146.4 12.5 %collective-permute-start.32 = (bf16[16,3584]{1,0:T(8,128)(2,1)S(1)}, bf16[16,3584]{1,0:T(8,128)(2,1)S(1)}, u32[]{:S(2)}, u32[]{:S(2)}) collective-permute-start(bf16[16,3584]{1,0:T(8,128)(2,1)S(1)} %get-tuple-element.35), channel_id=1, source_target_pairs={{0,4},{1,5},{4,0},{5,1},{6,2},{7,3},{8,12},{9,13},{12,8},{13,9},{1... | collective-permute-start | bytes 344072 | tf_op jit(solution)/shard_map/ppermute | solution.py:43
  148.3 10.6 %collective-permute-start.33 = (bf16[16,3584]{1,0:T(8,128)(2,1)S(1)}, bf16[16,3584]{1,0:T(8,128)(2,1)S(1)}, u32[]{:S(2)}, u32[]{:S(2)}) collective-permute-start(bf16[16,3584]{1,0:T(8,128)(2,1)S(1)} %get-tuple-element.36), channel_id=1, source_target_pairs={{2,4},{3,5},{4,2},{5,3},{6,0},{7,1},{10,12},{11,13},{12,10},{13,11... | collective-permute-start | bytes 344072 | tf_op jit(solution)/shard_map/ppermute | solution.py:43

commit v2 on v1

--- a/solution.py
+++ b/solution.py
@@ -12,6 +12,7 @@
 BETA = 0.5
 LOSS_SCALE = 1024.0
 LIVE = 96
+PARTS = 2
 F32 = jnp.float32
 BF16 = jnp.bfloat16
 AXES = ("dp", "tp")
@@ -42,6 +43,12 @@
                 pairs.append((dp_at * self.tp + tp_at, to))
         return lax.ppermute(value, AXES, pairs)
 
+    def send_depth(self, values, source=None, target=None):
+        got = []
+        for k, value in enumerate(values, 1):
+            got.append(self.send(value, k=k, source=source, target=target))
+        return got
+
 
 def pick(pieces, index):
     bit = 0
@@ -112,7 +119,7 @@
 
 
 def gather_depth(grid, rows):
-    pieces = [rows] + [grid.send(rows, k=k, source=grid.live) for k in range(1, grid.depth)]
+    pieces = [rows] + grid.send_depth([rows] * (grid.depth - 1), source=grid.live)
     if not grid.tiled:
         return jnp.concatenate([pick(pieces, grid.z ^ j) for j in range(grid.live)], axis=0)
     return call(
@@ -201,22 +208,18 @@
     return top + jnp.log(sum([jnp.exp(part - top) for part in every[1:]], jnp.exp(every[0] - top)))
 
 
-def product_into(out, grads, head):
-    height = head.shape[0] // 4
-
-    def step(n, carry):
-        here = block_rows(n, height)
+def product_kernel(part, ids, grads, head, out):
+    height = out.shape[1] // 2
+    for n in range(2):
+        here = slice(part * out.shape[1] + n * height, part * out.shape[1] + (n + 1) * height)
         value = lax.dot_general(
             grads[...], head[here, :], (((1,), (1,)), ((), ())), preferred_element_type=F32
         )
-        out[:, here] = value.astype(out.dtype)
-        return carry
-
-    lax.fori_loop(0, 4, step, 0)
+        out[:, n * height : (n + 1) * height] = value.astype(out.dtype)
 
 
 def given_kernel(
-    ids, got, labels, scale, t_logits, s_logits, head, given, kept, near, lines, columns, grads, sems
+    ids, got, labels, scale, t_logits, s_logits, head, given, kept, grads, near, lines, columns, sems
 ):
     vocab = t_logits.shape[1]
     rows = t_logits.shape[0] // 8
@@ -249,14 +252,11 @@
         into[place * rows : (place + 1) * rows, :] = grad.astype(BF16)
     for n, copy in enumerate(heads):
         copy.wait()
-        here = slice(n * part, (n + 1) * part)
-        given[:, here] = lax.dot_general(
-            grads[...], near[here, :], (((1,), (1,)), ((), ())), preferred_element_type=F32
-        ).astype(BF16)
-
-
-def kept_kernel(ids, grads, head, out):
-    product_into(out, grads, head)
+        if n < 4 // PARTS:
+            here = slice(n * part, (n + 1) * part)
+            given[:, here] = lax.dot_general(
+                grads[...], near[here, :], (((1,), (1,)), ((), ())), preferred_element_type=F32
+            ).astype(BF16)
 
 
 def prep_kernel(live, share, nseq, ids, *refs):
@@ -310,25 +310,29 @@
     loss[...] = jnp.where(keep, own, 0.0)
 
 
-def add_kernel(ids, kept, other, own, to_x, to_y, to_far):
+def add_kernel(ids, kept, other, own, *outs):
     rows = own.shape[0]
     own[...] = kept[:rows, :] + other[:rows, :].astype(F32)
-    for i, out in ((1, to_x), (2, to_y), (3, to_far)):
+    for i, out in enumerate(outs, 1):
         here = slice(i * rows, (i + 1) * rows)
         out[...] = (kept[here, :] + other[here, :].astype(F32)).astype(BF16)
 
 
-def chunk_kernel(live, ids, base, by_x, by_y, far, own, *lows):
-    share = own.shape[0]
-
-    def chunk(slot):
+def chunk_kernel(live, ids, *refs):
+    parts, (own, *lows) = refs[: 4 * PARTS], refs[4 * PARTS :]
+    share, width = own.shape[0], own.shape[1] // PARTS
+
+    def chunk(out, slot):
         here = block_rows(jnp.minimum(slot, live - 1), share)
-        total = base[here, :] + by_x[here, :].astype(F32)
-        return total + by_y[here, :].astype(F32) + far[here, :].astype(F32)
-
-    own[...] = chunk(ids[2])
+        for part in range(PARTS):
+            base, by_x, by_y, far = parts[4 * part : 4 * part + 4]
+            total = base[here, :] + by_x[here, :].astype(F32)
+            total = total + by_y[here, :].astype(F32) + far[here, :].astype(F32)
+            out[:, part * width : (part + 1) * width] = total.astype(out.dtype)
+
+    chunk(own, ids[2])
     for k, low in enumerate(lows, 1):
-        low[...] = chunk(ids[2] ^ k).astype(BF16)
+        chunk(low, ids[2] ^ k)
 
 
 def final_kernel(live, ids, own, *refs):
@@ -350,7 +354,18 @@
     return inverse * scaled - hidden * (inverse * inverse * inverse) * inner
 
 
-def reduce_rows(grid, kept, other, share):
+def product(grid, grads, head, part, dtype):
+    return call(
+        functools.partial(product_kernel, part),
+        grid.ids,
+        [grads, head],
+        [shape_of((grads.shape[0], head.shape[0] // PARTS), dtype)],
+        [],
+        6,
+    )[0]
+
+
+def reduce_plane(grid, kept, other):
     rows, width = kept.shape[0] // 4, kept.shape[1]
     own, to_x, to_y, to_far = call(
         add_kernel,
@@ -360,26 +375,27 @@
         [],
         4,
     )
-    by_x = grid.send(to_x, d=1)
-    by_y = grid.send(to_y, a=1)
-    far = grid.send(to_far, a=1, d=1)
-    ks = range(1, grid.depth)
+    return own, grid.send(to_x, d=1), grid.send(to_y, a=1), grid.send(to_far, a=1, d=1)
+
+
+def reduce_depth(grid, parts, share):
+    width = PARTS * parts[0][0].shape[1]
     if grid.tiled:
         summed, *lows = call(
             functools.partial(chunk_kernel, grid.live),
             grid.ids,
-            [own, by_x, by_y, far],
-            [shape_of((share, width), F32)] + [shape_of((share, width), BF16) for k in ks],
+            [value for part in parts for value in part],
+            [shape_of((share, width), F32)] + [shape_of((share, width), BF16)] * (grid.depth - 1),
             [],
             4,
         )
     else:
-        mine = own + by_x.astype(F32) + by_y.astype(F32) + far.astype(F32)
+        mine = jnp.concatenate([sum([value.astype(F32) for value in part]) for part in parts], axis=1)
         mine = mine.reshape(grid.live, share, width)
         slots = [jnp.minimum(grid.z ^ k, grid.live - 1) for k in range(grid.depth)]
         summed, *lows = [lax.dynamic_index_in_dim(mine, k, 0, keepdims=False) for k in slots]
         lows = [low.astype(BF16) for low in lows]
-    return summed, [grid.send(low, k=k, target=grid.live) for k, low in zip(ks, lows)]
+    return [summed] + grid.send_depth(lows, target=grid.live)
 
 
 def row_weights(lengths, tok_rows):
@@ -437,7 +453,7 @@
             ).astype(BF16)
             for k in ks
         ]
-    others = [grid.send(low, k=k, target=live) for k, low in zip(ks, lows)]
+    others = grid.send_depth(lows, target=live)
 
     student_f = student_hidden.astype(F32)
     student_norm = norm_rows(student_f, student_gain)[0].astype(BF16)
@@ -512,27 +528,30 @@
     got = lax.all_to_all(sent, AXES, 0, 0, tiled=True)
 
     half = rows // 2
-    given, grads, near = call(
+    given, keeps, gives, near = call(
         given_kernel,
         grid.ids,
         [got, label_column, scale_column, t_logits, s_logits],
         [
-            shape_of((half, width_s), BF16),
+            shape_of((half, width_s // PARTS), BF16),
+            shape_of((half, vocab_dev), BF16),
             shape_of((half, vocab_dev), BF16),
             shape_of(student_head.shape, BF16),
         ],
-        [
-            pltpu.VMEM((128, rows), F32),
-            pltpu.VMEM((rows, 128), F32),
-            pltpu.VMEM((half, vocab_dev), BF16),
-            pltpu.SemaphoreType.DMA((4,)),
-        ],
+        [pltpu.VMEM((128, rows), F32), pltpu.VMEM((rows, 128), F32), pltpu.SemaphoreType.DMA((4,))],
         10,
         [student_head],
     )
-    other = grid.send(given, b=1)
-    kept = call(kept_kernel, grid.ids, [grads, near], [shape_of((half, width_s), F32)], [], 4)[0]
-    summed, chunks = reduce_rows(grid, kept, other, share)
+    others = []
+    for part in range(PARTS):
+        if part:
+            given = product(grid, gives, near, part, BF16)
+        others.append(grid.send(given, b=1))
+    parts = []
+    for part in range(PARTS):
+        kept = product(grid, keeps, near, part, F32)
+        parts.append(reduce_plane(grid, kept, others[part]))
+    sums = reduce_depth(grid, parts, share)
     row_loss = call(
         functools.partial(loss_kernel, live, share),
         grid.ids,
@@ -545,14 +564,13 @@
         grad_hidden = call(
             functools.partial(final_kernel, live),
             grid.ids,
-            [summed, *chunks, student_hidden, student_gain[None]],
+            [*sums, student_hidden, student_gain[None]],
             [jax.ShapeDtypeStruct((share, width_s), F32)],
             [],
             4,
         )[0]
     else:
-        for chunk in chunks:
-            summed = summed + chunk.astype(F32)
+        summed = sum([value.astype(F32) for value in sums])
         grad_hidden = jnp.where(
             grid.z < live, hidden_gradient(summed, student_f, student_gain), 0.0
         )

time: 161 us -> 162 us (level)
  waiting for transfers between devices: 61.5 us -> 57.5 us
  starting transfers between devices: 47.7 us -> 51.4 us
    ppermute x34 -> x38, waiting for transfers between devices: 61.5 us -> 57.5 us  [send(): return lax.ppermute(value, AXES, pairs)]
    ppermute x34 -> x38, starting transfers between devices: 47.7 us -> 51.4 us  [send(): return lax.ppermute(value, AXES, pairs)]
    pallas_call x13 -> x16, Pallas kernels: 21 us -> 21.9 us  [call(): pl.pallas_call(kernel, out_shape=outs, in_specs=[SMEM] + [VMEM] * len(arg...]
  transfers between devices with their start and end apart: 34 -> 38, of which waited for: 15 -> 16; matrix products, arithmetic and copies ran while one was open for 5% -> 5% of each run, Pallas kernels for 7% -> 8%
where the time goes in v2:
time: 162 us; the launch traced here: 161 us
  waiting for transfers between devices  57.5 us (35%)
  starting transfers between devices  51.4 us (32%)
  Pallas kernels  21.9 us (14%)
  blocking collectives  15.5 us (10%)
  matrix products  6.8 us (4%)
  local copies, waits for them, and re-layouts  3.84 us (2%)
  other arithmetic  2.83 us (2%)
    ppermute x38, waiting for transfers between devices, send(): return lax.ppermute(value, AXES, pairs)  57.5 us
    ppermute x38, starting transfers between devices, send(): return lax.ppermute(value, AXES, pairs)  51.4 us
    pallas_call x16, Pallas kernels, call(): pl.pallas_call(kernel, out_shape=outs, in_specs=[SMEM] + [VMEM] * len(arg...  21.9 us
    all_to_all x1, blocking collectives, shards(): got = lax.all_to_all(sent, AXES, 0, 0, tiled=True)  15.5 us
    dot_general x1, matrix products, shards(): t_logits = jnp.dot(whole_t, teacher_head, preferred_element_type=F32)  3.81 us
  transfers between devices with their start and end apart: 38, of which 16 were waited for; matrix products, arithmetic and copies ran while one was open for 5% of the time, Pallas kernels for 8%

profile of v2, /device:TPU:0, one launch (start us, length us, event | category | flops | bytes accessed | tf_op | source)
XLA Modules:
  0.0 161.0 jit_solution(16966561775830874861)
XLA Ops:
  0.7 1.1 fusion
  1.8 1.0 fusion.2.refs_0_
  2.8 5.0 %collective-permute-start.14 = (bf16[16,3584]{1,0:T(8,128)(2,1)S(1)}, bf16[16,3584]{1,0:T(8,128)(2,1)S(1)}, u32[]{:S(2)}, u32[]{:S(2)}) collective-permute-start(bf16[16,3584]{1,0:T(8,128)(2,1)S(1)} %fusion.2.refs_0_), channel_id=1, source_target_pairs={{0,2},{1,3},{2,0},{3,1},{4,6},{5,7},{8,10},{9,11},{10,8},{11,9},{1... | collective-permute-start | bytes 344072 | tf_op jit(solution)/shard_map/ppermute | solution.py:44
  7.8 4.5 %collective-permute-start.15 = (bf16[16,3584]{1,0:T(8,128)(2,1)S(1)}, bf16[16,3584]{1,0:T(8,128)(2,1)S(1)}, u32[]{:S(2)}, u32[]{:S(2)}) collective-permute-start(bf16[16,3584]{1,0:T(8,128)(2,1)S(1)} %fusion.2.refs_0_), channel_id=1, source_target_pairs={{0,4},{1,5},{2,6},{3,7},{4,0},{5,1},{8,12},{9,13},{10,14},{11,15},... | collective-permute-start | bytes 344072 | tf_op jit(solution)/shard_map/ppermute | solution.py:44
  12.3 1.3 collective-permute-start.16
  13.6 0.7 pad_add_fusion
  14.3 1.6 collective-permute-start.25
  15.9 1.2 slice.6
  17.2 0.7 broadcast_in_dim.14.refs_5_
  17.9 0.7 broadcast_in_dim.15.refs_6_
  19.1 1.5 collective-permute-start
  20.6 1.1 collective-permute-done.26.refs_3_
  21.7 1.1 shard_map.117
  22.9 0.7 shard_map.116
  23.6 1.6 collective-permute-start.17
  25.7 6.5 %collective-permute-done.other = bf16[3,16,4608]{2,1,0:T(8,128)(2,1)S(1)} collective-permute-done((bf16[3,16,4608]{2,1,0:T(8,128)(2,1)S(1)}, bf16[3,16,4608]{2,1,0:T(8,128)(2,1)S(1)}, u32[]{:S(2)}, u32[]{:S(2)}) %collective-permute-start) | collective-permute-done | bytes 442400 | tf_op jit(solution)/shard_map/ppermute | solution.py:44
  32.1 0.7 shard_map.113
  32.8 3.4 %collective-permute-start.1 = (bf16[16,4608]{1,0:T(8,128)(2,1)S(1)}, bf16[16,4608]{1,0:T(8,128)(2,1)S(1)}, u32[]{:S(2)}, u32[]{:S(2)}) collective-permute-start(bf16[16,4608]{1,0:T(8,128)(2,1)S(1)} %get-tuple-element.26), channel_id=1, source_target_pairs={{0,2},{1,3},{2,0},{3,1},{6,4},{7,5},{8,10},{9,11},{10,8},{11,9},{1... | collective-permute-start | bytes 442376 | tf_op jit(solution)/shard_map/ppermute | solution.py:44
  36.3 1.9 %collective-permute-start.2 = (bf16[16,4608]{1,0:T(8,128)(2,1)S(1)}, bf16[16,4608]{1,0:T(8,128)(2,1)S(1)}, u32[]{:S(2)}, u32[]{:S(2)}) collective-permute-start(bf16[16,4608]{1,0:T(8,128)(2,1)S(1)} %get-tuple-element.27), channel_id=1, source_target_pairs={{0,4},{1,5},{4,0},{5,1},{6,2},{7,3},{8,12},{9,13},{12,8},{13,9},{1... | collective-permute-start | bytes 442376 | tf_op jit(solution)/shard_map/ppermute | solution.py:44
  38.2 0.7 collective-permute-done.17
  38.9 1.3 collective-permute-start.3
  40.3 2.4 %collective-permute-start.21 = (bf16[48,3584]{1,0:T(8,128)(2,1)S(1)}, bf16[48,3584]{1,0:T(8,128)(2,1)S(1)}, u32[]{:S(2)}, u32[]{:S(2)}) collective-permute-start(bf16[48,3584]{1,0:T(8,128)(2,1)S(1)} %shard_map.116), channel_id=1, source_target_pairs={{0,17},{1,16},{2,19},{3,18},{4,21},{5,20},{6,23},{7,22},{8,25},{9,... | collective-permute-start | bytes 1032200 | tf_op jit(solution)/shard_map/ppermute | solution.py:44
  42.8 7.7 %collective-permute-done.2.refs_2_ = bf16[16,4608]{1,0:T(8,128)(2,1)S(1)} collective-permute-done((bf16[16,4608]{1,0:T(8,128)(2,1)S(1)}, bf16[16,4608]{1,0:T(8,128)(2,1)S(1)}, u32[]{:S(2)}, u32[]{:S(2)}) %collective-permute-start.2) | collective-permute-done | bytes 147488 | tf_op jit(solution)/shard_map/ppermute | solution.py:44
  50.5 0.9 shard_map.114.refs_0_
  51.3 4.9 %collective-permute-start.4 = (bf16[16,4608]{1,0:T(8,128)(2,1)S(1)}, bf16[16,4608]{1,0:T(8,128)(2,1)S(1)}, u32[]{:S(2)}, u32[]{:S(2)}) collective-permute-start(bf16[16,4608]{1,0:T(8,128)(2,1)S(1)} %shard_map.114.refs_0_), channel_id=1, source_target_pairs={{0,2},{1,3},{2,0},{3,1},{4,6},{5,7},{8,10},{9,11},{10,8},{11,9},{1... | collective-permute-start | bytes 442376 | tf_op jit(solution)/shard_map/ppermute | solution.py:44
  56.2 1.9 %collective-permute-start.5 = (bf16[16,4608]{1,0:T(8,128)(2,1)S(1)}, bf16[16,4608]{1,0:T(8,128)(2,1)S(1)}, u32[]{:S(2)}, u32[]{:S(2)}) collective-permute-start(bf16[16,4608]{1,0:T(8,128)(2,1)S(1)} %shard_map.114.refs_0_), channel_id=1, source_target_pairs={{0,4},{1,5},{2,6},{3,7},{4,0},{5,1},{8,12},{9,13},{10,14},{11,15},... | collective-permute-start | bytes 442376 | tf_op jit(solution)/shard_map/ppermute | solution.py:44
  58.1 1.3 collective-permute-start.6
  60.2 5.5 %collective-permute-done.5.refs_2_ = bf16[16,4608]{1,0:T(8,128)(2,1)S(1)} collective-permute-done((bf16[16,4608]{1,0:T(8,128)(2,1)S(1)}, bf16[16,4608]{1,0:T(8,128)(2,1)S(1)}, u32[]{:S(2)}, u32[]{:S(2)}) %collective-permute-start.5) | collective-permute-done | bytes 147488 | tf_op jit(solution)/shard_map/ppermute | solution.py:44
  65.7 0.7 shard_map.115
  66.4 1.6 collective-permute-start.7
  68.0 1.6 collective-permute-start.10
  69.7 0.5 collective-permute-start.11
  70.3 3.0 %fusion.4.logits.s_logits = f32[384,1024]{1,0:T(8,128)S(1)} fusion(bf16[384,3584]{1,0:T(8,128)(2,1)S(1)} %constant_dynamic-update-slice_fusion.8, bf16[3584,1024]{1,0:T(8,128)(2,1)S(1)} %copy-done.3), kind=kOutput, calls=%fused_computation.26 | convolution fusion | flops 2818572288 | bytes 11665408 | tf_op jit(solution)/shard_map/dot_general | solution.py:514
  73.3 2.3 %shard_map.118.s_cols = f32[384,128]{1,0:T(8,128)S(1)} custom-call(s32[5]{0:T(128)S(1)} %stack.23.ids, f32[384,1024]{1,0:T(8,128)S(1)} %fusion.4.logits.s_logits, s32[384,1]{1,0:T(8,128)S(1)} %get-tuple-element.29.labels), custom_call_target="tpu_custom_call" | custom-call | tf_op jit(solution)/shard_map/pallas_call | solution.py:76
  75.7 3.8 %collective-permute-done.7 = bf16[48,4608]{1,0:T(8,128)(2,1)S(1)} collective-permute-done((bf16[48,4608]{1,0:T(8,128)(2,1)S(1)}, bf16[48,4608]{1,0:T(8,128)(2,1)S(1)}, u32[]{:S(2)}, u32[]{:S(2)}) %collective-permute-start.7) | collective-permute-done | bytes 442400 | tf_op jit(solution)/shard_map/ppermute | solution.py:44
  79.5 10.6 %collective-permute-done.10 = bf16[48,4608]{1,0:T(8,128)(2,1)S(1)} collective-permute-done((bf16[48,4608]{1,0:T(8,128)(2,1)S(1)}, bf16[48,4608]{1,0:T(8,128)(2,1)S(1)}, u32[]{:S(2)}, u32[]{:S(2)}) %collective-permute-start.10) | collective-permute-done | bytes 442400 | tf_op jit(solution)/shard_map/ppermute | solution.py:44
  90.8 1.1 collective-permute-done.12
  91.9 0.6 collective-permute-done.13
  92.6 3.8 %fusion.3.logits.t_logits = f32[384,1024]{1,0:T(8,128)S(1)} fusion(bf16[384,4608]{1,0:T(8,128)(2,1)S(1)} %constant_dynamic-update-slice_fusion, bf16[4608,1024]{1,0:T(8,128)(2,1)S(1)} %bitcast.25), kind=kOutput, calls=%fused_computation.25 | convolution fusion | flops 3623878656 | bytes 14548992 | tf_op jit(solution)/shard_map/dot_general | solution.py:518
  96.4 1.4 shard_map.119
  97.8 15.5 %all_to_all.5.got = f32[32,1,1536]{2,1,0:T(1,128)S(1)} all-to-all(f32[32,1,1536]{2,1,0:T(1,128)S(1)} %shard_map.119), channel_id=1, replica_groups=mesh['dp'=4,'tp'=8] {'dp','tp'}, dimensions={0} | all-to-all | bytes 393216 | tf_op jit(solution)/shard_map/all_to_all | solution.py:528
  113.3 4.3 %shard_map.120 = (bf16[192,1792]{1,0:T(8,128)(2,1)S(1)}, bf16[192,1024]{1,0:T(8,128)(2,1)S(1)}, bf16[192,1024]{1,0:T(8,128)(2,1)S(1)}, bf16[3584,1024]{1,0:T(8,128)(2,1)S(1)}) custom-call(s32[5]{0:T(128)S(1)} %stack.23.ids, f32[32,1,1536]{2,1,0:T(1,128)S(1)} %all_to_all.5.got, s32[384,1]{1,0:T(8,128)S(1)} %get-tuple-element.29.labels, ...), custom_call_target="tpu_custom_call" | custom-call | tf_op jit(solution)/shard_map/pallas_call | solution.py:76
  117.6 1.9 %shard_map.124 = bf16[192,1792]{1,0:T(8,128)(2,1)S(1)} custom-call(s32[5]{0:T(128)S(1)} %stack.23.ids, bf16[192,1024]{1,0:T(8,128)(2,1)S(1)} %get-tuple-element.38.grads, bf16[3584,1024]{1,0:T(8,128)(2,1)S(1)} %get-tuple-element.32.head), custom_call_target="tpu_custom_call" | custom-call | tf_op jit(solution)/shard_map/pallas_call | solution.py:76
  120.1 1.9 %shard_map.123.kept = f32[192,1792]{1,0:T(8,128)S(1)} custom-call(s32[5]{0:T(128)S(1)} %stack.23.ids, bf16[192,1024]{1,0:T(8,128)(2,1)S(1)} %get-tuple-element.31.grads, bf16[3584,1024]{1,0:T(8,128)(2,1)S(1)} %get-tuple-element.32.head), custom_call_target="tpu_custom_call" | custom-call | tf_op jit(solution)/shard_map/pallas_call | solution.py:76
  122.0 0.7 shard_map.125
  122.7 2.1 %collective-permute-start.32 = (bf16[48,1792]{1,0:T(8,128)(2,1)S(1)}, bf16[48,1792]{1,0:T(8,128)(2,1)S(1)}, u32[]{:S(2)}, u32[]{:S(2)}) collective-permute-start(bf16[48,1792]{1,0:T(8,128)(2,1)S(1)} %get-tuple-element.40), channel_id=1, source_target_pairs={{0,1},{1,0},{2,3},{3,2},{4,5},{5,4},{6,7},{7,6},{8,9},{9,8},{10,11... | collective-permute-start | bytes 516104 | tf_op jit(solution)/shard_map/ppermute | solution.py:44
  124.7 1.9 %shard_map.121.kept = f32[192,1792]{1,0:T(8,128)S(1)} custom-call(s32[5]{0:T(128)S(1)} %stack.23.ids, bf16[192,1024]{1,0:T(8,128)(2,1)S(1)} %get-tuple-element.31.grads, bf16[3584,1024]{1,0:T(8,128)(2,1)S(1)} %get-tuple-element.32.head), custom_call_target="tpu_custom_call" | custom-call | tf_op jit(solution)/shard_map/pallas_call | solution.py:76
  126.6 0.6 collective-permute-start.33
  127.2 0.9 collective-permute-start.34
  128.2 0.7 shard_map.122
  128.8 2.1 %collective-permute-start.28 = (bf16[48,1792]{1,0:T(8,128)(2,1)S(1)}, bf16[48,1792]{1,0:T(8,128)(2,1)S(1)}, u32[]{:S(2)}, u32[]{:S(2)}) collective-permute-start(bf16[48,1792]{1,0:T(8,128)(2,1)S(1)} %get-tuple-element.35), channel_id=1, source_target_pairs={{0,1},{1,0},{2,3},{3,2},{4,5},{5,4},{6,7},{7,6},{8,9},{9,8},{10,11... | collective-permute-start | bytes 516104 | tf_op jit(solution)/shard_map/ppermute | solution.py:44
  130.9 0.5 collective-permute-start.29
  131.5 1.0 collective-permute-start.30
  132.5 0.7 shard_map.128
  133.2 5.6 %collective-permute-done.33.refs_6_ = bf16[48,1792]{1,0:T(8,128)(2,1)S(1)} collective-permute-done((bf16[48,1792]{1,0:T(8,128)(2,1)S(1)}, bf16[48,1792]{1,0:T(8,128)(2,1)S(1)}, u32[]{:S(2)}, u32[]{:S(2)}) %collective-permute-start.33) | collective-permute-done | bytes 172064 | tf_op jit(solution)/shard_map/ppermute | solution.py:44
  139.1 4.8 %collective-permute-done.29.refs_2_ = bf16[48,1792]{1,0:T(8,128)(2,1)S(1)} collective-permute-done((bf16[48,1792]{1,0:T(8,128)(2,1)S(1)}, bf16[48,1792]{1,0:T(8,128)(2,1)S(1)}, u32[]{:S(2)}, u32[]{:S(2)}) %collective-permute-start.29) | collective-permute-done | bytes 172064 | tf_op jit(solution)/shard_map/ppermute | solution.py:44
  143.9 0.7 shard_map.126
  144.6 2.2 %collective-permute-start.35 = (bf16[16,3584]{1,0:T(8,128)(2,1)S(1)}, bf16[16,3584]{1,0:T(8,128)(2,1)S(1)}, u32[]{:S(2)}, u32[]{:S(2)}) collective-permute-start(bf16[16,3584]{1,0:T(8,128)(2,1)S(1)} %get-tuple-element.44), channel_id=1, source_target_pairs={{0,2},{1,3},{2,0},{3,1},{6,4},{7,5},{8,10},{9,11},{10,8},{11,9},{1... | collective-permute-start | bytes 344072 | tf_op jit(solution)/shard_map/ppermute | solution.py:44
  146.9 1.9 %collective-permute-start.36 = (bf16[16,3584]{1,0:T(8,128)(2,1)S(1)}, bf16[16,3584]{1,0:T(8,128)(2,1)S(1)}, u32[]{:S(2)}, u32[]{:S(2)}) collective-permute-start(bf16[16,3584]{1,0:T(8,128)(2,1)S(1)} %get-tuple-element.45), channel_id=1, source_target_pairs={{0,4},{1,5},{4,0},{5,1},{6,2},{7,3},{8,12},{9,13},{12,8},{13,9},{1... | collective-permute-start | bytes 344072 | tf_op jit(solution)/shard_map/ppermute | solution.py:44
  148.8 1.3 collective-permute-start.37
  150.1 0.5 slice_bitcast_fusion
  150.6 1.9 %collective-permute-done.35.refs_0_ = bf16[16,3584]{1,0:T(8,128)(2,1)S(1)} collective-permute-done((bf16[16,3584]{1,0:T(8,128)(2,1)S(1)}, bf16[16,3584]{1,0:T(8,128)(2,1)S(1)}, u32[]{:S(2)}, u32[]{:S(2)}) %collective-permute-start.35) | collective-permute-done | bytes 114720 | tf_op jit(solution)/shard_map/ppermute | solution.py:44
  152.5 7.1 %collective-permute-done.36.refs_1_ = bf16[16,3584]{1,0:T(8,128)(2,1)S(1)} collective-permute-done((bf16[16,3584]{1,0:T(8,128)(2,1)S(1)}, bf16[16,3584]{1,0:T(8,128)(2,1)S(1)}, u32[]{:S(2)}, u32[]{:S(2)}) %collective-permute-start.36) | collective-permute-done | bytes 114720 | tf_op jit(solution)/shard_map/ppermute | solution.py:44
  159.6 1.4 shard_map.127
  (75 shorter events, 3.7 us)
Async XLA Ops:
  0.6 31.5 %copy-start = (bf16[1,128,4608]{2,1,0:T(8,128)(2,1)S(1)}, bf16[1,128,4608]{2,1,0:T(8,128)(2,1)}, u32[]{:S(2)}) copy-start(bf16[1,128,4608]{2,1,0:T(8,128)(2,1)} %partial.1) | copy-start | bytes 3538948
  0.6 49.8 %copy-start.2 = (bf16[16,4608]{1,0:T(8,128)(2,1)S(1)}, bf16[16,4608]{1,0:T(8,128)(2,1)}, u32[]{:S(2)}) copy-start(bf16[16,4608]{1,0:T(8,128)(2,1)} %refs_4_.1) | copy-start | bytes 442372
  2.8 20.1 %collective-permute-start.14 = (bf16[16,3584]{1,0:T(8,128)(2,1)S(1)}, bf16[16,3584]{1,0:T(8,128)(2,1)S(1)}, u32[]{:S(2)}, u32[]{:S(2)}) collective-permute-start(bf16[16,3584]{1,0:T(8,128)(2,1)S(1)} %fusion.2.refs_0_), channel_id=1, source_target_pairs={{0,2},{1,3},{2,0},{3,1},{4,6},{5,7},{8,10},{9,11},{10,8},{11,9},{1... | collective-permute-start | bytes 344072 | tf_op jit(solution)/shard_map/ppermute | solution.py:44
  7.8 15.1 %collective-permute-start.15 = (bf16[16,3584]{1,0:T(8,128)(2,1)S(1)}, bf16[16,3584]{1,0:T(8,128)(2,1)S(1)}, u32[]{:S(2)}, u32[]{:S(2)}) collective-permute-start(bf16[16,3584]{1,0:T(8,128)(2,1)S(1)} %fusion.2.refs_0_), channel_id=1, source_target_pairs={{0,4},{1,5},{2,6},{3,7},{4,0},{5,1},{8,12},{9,13},{10,14},{11,15},... | collective-permute-start | bytes 344072 | tf_op jit(solution)/shard_map/ppermute | solution.py:44
  12.3 10.6 %collective-permute-start.16 = (bf16[16,3584]{1,0:T(8,128)(2,1)S(1)}, bf16[16,3584]{1,0:T(8,128)(2,1)S(1)}, u32[]{:S(2)}, u32[]{:S(2)}) collective-permute-start(bf16[16,3584]{1,0:T(8,128)(2,1)S(1)} %fusion.2.refs_0_), channel_id=1, source_target_pairs={{0,6},{1,7},{2,4},{3,5},{4,2},{5,3},{8,14},{9,15},{10,12},{11,13},... | collective-permute-start | bytes 344072 | tf_op jit(solution)/shard_map/ppermute | solution.py:44
  14.3 4.4 %collective-permute-start.24 = (s32[1,136]{1,0:T(1,128)S(1)}, s32[1,136]{1,0:T(1,128)S(1)}, u32[]{:S(2)}, u32[]{:S(2)}) collective-permute-start(s32[1,136]{1,0:T(1,128)S(1)} %bitcast.18), channel_id=1, source_target_pairs={{0,8},{1,9},{2,10},{3,11},{4,12},{5,13},{6,14},{7,15},{8,0},{9,1},... | collective-permute-start | bytes 1640 | tf_op jit(solution)/shard_map/ppermute | solution.py:44
  14.3 4.8 %collective-permute-start.25 = (s32[1,136]{1,0:T(1,128)S(1)}, s32[1,136]{1,0:T(1,128)S(1)}, u32[]{:S(2)}, u32[]{:S(2)}) collective-permute-start(s32[1,136]{1,0:T(1,128)S(1)} %bitcast.19), channel_id=1, source_target_pairs={{0,16},{1,17},{2,18},{3,19},{4,20},{5,21},{6,22},{7,23},{8,24},{9,... | collective-permute-start | bytes 1640 | tf_op jit(solution)/shard_map/ppermute | solution.py:44
  18.7 3.1 %collective-permute-start.26 = (s32[1,136]{1,0:T(1,128)S(1)}, s32[1,136]{1,0:T(1,128)S(1)}, u32[]{:S(2)}, u32[]{:S(2)}) collective-permute-start(s32[1,136]{1,0:T(1,128)S(1)} %bitcast.20), channel_id=1, source_target_pairs={{0,24},{1,25},{2,26},{3,27},{4,28},{5,29},{6,30},{7,31},{8,16},{9,... | collective-permute-start | bytes 1640 | tf_op jit(solution)/shard_map/ppermute | solution.py:44
  19.1 13.0 %collective-permute-start = (bf16[3,16,4608]{2,1,0:T(8,128)(2,1)S(1)}, bf16[3,16,4608]{2,1,0:T(8,128)(2,1)S(1)}, u32[]{:S(2)}, u32[]{:S(2)}) collective-permute-start(bf16[3,16,4608]{2,1,0:T(8,128)(2,1)S(1)} %dynamic-slice_bitcast_fusion), channel_id=1, source_target_pairs={{0,1},{1,0},{2,3},{3,2},{4,5},{5,4},{6,7},{7,6},{8,9},{9,8},{10,11... | collective-permute-start | bytes 1327112 | tf_op jit(solution)/shard_map/ppermute | solution.py:44
  23.6 15.3 %collective-permute-start.17 = (bf16[48,3584]{1,0:T(8,128)(2,1)S(1)}, bf16[48,3584]{1,0:T(8,128)(2,1)S(1)}, u32[]{:S(2)}, u32[]{:S(2)}) collective-permute-start(bf16[48,3584]{1,0:T(8,128)(2,1)S(1)} %shard_map.116), channel_id=1, source_target_pairs={{0,1},{1,0},{2,3},{3,2},{4,5},{5,4},{6,7},{7,6},{8,9},{9,8},{10,11... | collective-permute-start | bytes 1032200 | tf_op jit(solution)/shard_map/ppermute | solution.py:44
  25.1 33.0 %collective-permute-start.18 = (bf16[48,3584]{1,0:T(8,128)(2,1)S(1)}, bf16[48,3584]{1,0:T(8,128)(2,1)S(1)}, u32[]{:S(2)}, u32[]{:S(2)}) collective-permute-start(bf16[48,3584]{1,0:T(8,128)(2,1)S(1)} %shard_map.116), channel_id=1, source_target_pairs={{0,8},{1,9},{2,10},{3,11},{4,12},{5,13},{6,14},{7,15},{8,0},{9,1},... | collective-permute-start | bytes 1032200 | tf_op jit(solution)/shard_map/ppermute | solution.py:44
  25.1 34.4 %collective-permute-start.20 = (bf16[48,3584]{1,0:T(8,128)(2,1)S(1)}, bf16[48,3584]{1,0:T(8,128)(2,1)S(1)}, u32[]{:S(2)}, u32[]{:S(2)}) collective-permute-start(bf16[48,3584]{1,0:T(8,128)(2,1)S(1)} %shard_map.116), channel_id=1, source_target_pairs={{0,16},{1,17},{2,18},{3,19},{4,20},{5,21},{6,22},{7,23},{8,24},{9,... | collective-permute-start | bytes 1032200 | tf_op jit(solution)/shard_map/ppermute | solution.py:44
  32.8 7.5 %collective-permute-start.1 = (bf16[16,4608]{1,0:T(8,128)(2,1)S(1)}, bf16[16,4608]{1,0:T(8,128)(2,1)S(1)}, u32[]{:S(2)}, u32[]{:S(2)}) collective-permute-start(bf16[16,4608]{1,0:T(8,128)(2,1)S(1)} %get-tuple-element.26), channel_id=1, source_target_pairs={{0,2},{1,3},{2,0},{3,1},{6,4},{7,5},{8,10},{9,11},{10,8},{11,9},{1... | collective-permute-start | bytes 442376 | tf_op jit(solution)/shard_map/ppermute | solution.py:44
  36.3 14.2 %collective-permute-start.2 = (bf16[16,4608]{1,0:T(8,128)(2,1)S(1)}, bf16[16,4608]{1,0:T(8,128)(2,1)S(1)}, u32[]{:S(2)}, u32[]{:S(2)}) collective-permute-start(bf16[16,4608]{1,0:T(8,128)(2,1)S(1)} %get-tuple-element.27), channel_id=1, source_target_pairs={{0,4},{1,5},{4,0},{5,1},{6,2},{7,3},{8,12},{9,13},{12,8},{13,9},{1... | collective-permute-start | bytes 442376 | tf_op jit(solution)/shard_map/ppermute | solution.py:44
  38.9 11.6 %collective-permute-start.3 = (bf16[16,4608]{1,0:T(8,128)(2,1)S(1)}, bf16[16,4608]{1,0:T(8,128)(2,1)S(1)}, u32[]{:S(2)}, u32[]{:S(2)}) collective-permute-start(bf16[16,4608]{1,0:T(8,128)(2,1)S(1)} %get-tuple-element.28), channel_id=1, source_target_pairs={{2,4},{3,5},{4,2},{5,3},{6,0},{7,1},{10,12},{11,13},{12,10},{13,11... | collective-permute-start | bytes 442376 | tf_op jit(solution)/shard_map/ppermute | solution.py:44
  40.2 30.1 %copy-start.3 = (bf16[3584,1024]{1,0:T(8,128)(2,1)S(1)}, bf16[3584,1024]{1,0:T(8,128)(2,1)}, u32[]{:S(2)}) copy-start(bf16[3584,1024]{1,0:T(8,128)(2,1)} %head.1) | copy-start | bytes 22020100
  40.3 19.3 %collective-permute-start.21 = (bf16[48,3584]{1,0:T(8,128)(2,1)S(1)}, bf16[48,3584]{1,0:T(8,128)(2,1)S(1)}, u32[]{:S(2)}, u32[]{:S(2)}) collective-permute-start(bf16[48,3584]{1,0:T(8,128)(2,1)S(1)} %shard_map.116), channel_id=1, source_target_pairs={{0,17},{1,16},{2,19},{3,18},{4,21},{5,20},{6,23},{7,22},{8,25},{9,... | collective-permute-start | bytes 1032200 | tf_op jit(solution)/shard_map/ppermute | solution.py:44
  51.3 8.8 %collective-permute-start.4 = (bf16[16,4608]{1,0:T(8,128)(2,1)S(1)}, bf16[16,4608]{1,0:T(8,128)(2,1)S(1)}, u32[]{:S(2)}, u32[]{:S(2)}) collective-permute-start(bf16[16,4608]{1,0:T(8,128)(2,1)S(1)} %shard_map.114.refs_0_), channel_id=1, source_target_pairs={{0,2},{1,3},{2,0},{3,1},{4,6},{5,7},{8,10},{9,11},{10,8},{11,9},{1... | collective-permute-start | bytes 442376 | tf_op jit(solution)/shard_map/ppermute | solution.py:44
  56.2 9.5 %collective-permute-start.5 = (bf16[16,4608]{1,0:T(8,128)(2,1)S(1)}, bf16[16,4608]{1,0:T(8,128)(2,1)S(1)}, u32[]{:S(2)}, u32[]{:S(2)}) collective-permute-start(bf16[16,4608]{1,0:T(8,128)(2,1)S(1)} %shard_map.114.refs_0_), channel_id=1, source_target_pairs={{0,4},{1,5},{2,6},{3,7},{4,0},{5,1},{8,12},{9,13},{10,14},{11,15},... | collective-permute-start | bytes 442376 | tf_op jit(solution)/shard_map/ppermute | solution.py:44
  58.1 7.6 %collective-permute-start.6 = (bf16[16,4608]{1,0:T(8,128)(2,1)S(1)}, bf16[16,4608]{1,0:T(8,128)(2,1)S(1)}, u32[]{:S(2)}, u32[]{:S(2)}) collective-permute-start(bf16[16,4608]{1,0:T(8,128)(2,1)S(1)} %shard_map.114.refs_0_), channel_id=1, source_target_pairs={{0,6},{1,7},{2,4},{3,5},{4,2},{5,3},{8,14},{9,15},{10,12},{11,13},... | collective-permute-start | bytes 442376 | tf_op jit(solution)/shard_map/ppermute | solution.py:44
  59.5 8.5 %collective-permute-start.19 = (bf16[48,3584]{1,0:T(8,128)(2,1)S(1)}, bf16[48,3584]{1,0:T(8,128)(2,1)S(1)}, u32[]{:S(2)}, u32[]{:S(2)}) collective-permute-start(bf16[48,3584]{1,0:T(8,128)(2,1)S(1)} %collective-permute-done.17), channel_id=1, source_target_pairs={{0,8},{1,9},{2,10},{3,11},{4,12},{5,13},{6,14},{7,15},{8,0},{9,1},... | collective-permute-start | bytes 1032200 | tf_op jit(solution)/shard_map/ppermute | solution.py:44
  59.6 10.1 %collective-permute-start.22 = (bf16[48,3584]{1,0:T(8,128)(2,1)S(1)}, bf16[48,3584]{1,0:T(8,128)(2,1)S(1)}, u32[]{:S(2)}, u32[]{:S(2)}) collective-permute-start(bf16[48,3584]{1,0:T(8,128)(2,1)S(1)} %collective-permute-done.20), channel_id=1, source_target_pairs={{0,8},{1,9},{2,10},{3,11},{4,12},{5,13},{6,14},{7,15},{8,0},{9,1},... | collective-permute-start | bytes 1032200 | tf_op jit(solution)/shard_map/ppermute | solution.py:44
  60.1 10.1 %collective-permute-start.23 = (bf16[48,3584]{1,0:T(8,128)(2,1)S(1)}, bf16[48,3584]{1,0:T(8,128)(2,1)S(1)}, u32[]{:S(2)}, u32[]{:S(2)}) collective-permute-start(bf16[48,3584]{1,0:T(8,128)(2,1)S(1)} %collective-permute-done.21), channel_id=1, source_target_pairs={{0,8},{1,9},{2,10},{3,11},{4,12},{5,13},{6,14},{7,15},{8,0},{9,1},... | collective-permute-start | bytes 1032200 | tf_op jit(solution)/shard_map/ppermute | solution.py:44
  66.4 13.1 %collective-permute-start.7 = (bf16[48,4608]{1,0:T(8,128)(2,1)S(1)}, bf16[48,4608]{1,0:T(8,128)(2,1)S(1)}, u32[]{:S(2)}, u32[]{:S(2)}) collective-permute-start(bf16[48,4608]{1,0:T(8,128)(2,1)S(1)} %shard_map.115), channel_id=1, source_target_pairs={{0,1},{1,0},{2,3},{3,2},{4,5},{5,4},{6,7},{7,6},{8,9},{9,8},{10,11... | collective-permute-start | bytes 1327112 | tf_op jit(solution)/shard_map/ppermute | solution.py:44
  67.9 22.7 %collective-permute-start.8 = (bf16[48,4608]{1,0:T(8,128)(2,1)S(1)}, bf16[48,4608]{1,0:T(8,128)(2,1)S(1)}, u32[]{:S(2)}, u32[]{:S(2)}) collective-permute-start(bf16[48,4608]{1,0:T(8,128)(2,1)S(1)} %shard_map.115), channel_id=1, source_target_pairs={{0,8},{1,9},{2,10},{3,11},{4,12},{5,13},{6,14},{7,15},{8,0},{9,1},... | collective-permute-start | bytes 1327112 | tf_op jit(solution)/shard_map/ppermute | solution.py:44
  68.0 22.1 %collective-permute-start.10 = (bf16[48,4608]{1,0:T(8,128)(2,1)S(1)}, bf16[48,4608]{1,0:T(8,128)(2,1)S(1)}, u32[]{:S(2)}, u32[]{:S(2)}) collective-permute-start(bf16[48,4608]{1,0:T(8,128)(2,1)S(1)} %shard_map.115), channel_id=1, source_target_pairs={{0,16},{1,17},{2,18},{3,19},{4,20},{5,21},{6,22},{7,23},{8,24},{9,... | collective-permute-start | bytes 1327112 | tf_op jit(solution)/shard_map/ppermute | solution.py:44
  69.7 20.4 %collective-permute-start.11 = (bf16[48,4608]{1,0:T(8,128)(2,1)S(1)}, bf16[48,4608]{1,0:T(8,128)(2,1)S(1)}, u32[]{:S(2)}, u32[]{:S(2)}) collective-permute-start(bf16[48,4608]{1,0:T(8,128)(2,1)S(1)} %shard_map.115), channel_id=1, source_target_pairs={{0,17},{1,16},{2,19},{3,18},{4,21},{5,20},{6,23},{7,22},{8,25},{9,... | collective-permute-start | bytes 1327112 | tf_op jit(solution)/shard_map/ppermute | solution.py:44
  70.2 22.3 %slice-start = ((s8[9437184]{0:T(1024)(128)(4,1)}), s8[4194304]{0:T(1024)(128)(4,1)S(1)}, s32[]{:S(2)}) async-start(s8[9437184]{0:T(1024)(128)(4,1)} %bitcast.24), calls=%async_computation.1 | async-start | bytes 8388608
  70.3 22.3 %slice-start.1 = ((s8[9437184]{0:T(1024)(128)(4,1)}), s8[4194304]{0:T(1024)(128)(4,1)S(1)}, s32[]{:S(2)}) async-start(s8[9437184]{0:T(1024)(128)(4,1)} %bitcast.24), calls=%async_computation.2 | async-start | bytes 8388608
  70.3 22.3 %slice-start.2 = ((s8[9437184]{0:T(1024)(128)(4,1)}), s8[1048576]{0:T(1024)(128)(4,1)S(1)}, s32[]{:S(2)}) async-start(s8[9437184]{0:T(1024)(128)(4,1)} %bitcast.24), calls=%async_computation.3 | async-start | bytes 2097152
  79.5 11.2 %collective-permute-start.9 = (bf16[48,4608]{1,0:T(8,128)(2,1)S(1)}, bf16[48,4608]{1,0:T(8,128)(2,1)S(1)}, u32[]{:S(2)}, u32[]{:S(2)}) collective-permute-start(bf16[48,4608]{1,0:T(8,128)(2,1)S(1)} %collective-permute-done.7), channel_id=1, source_target_pairs={{0,8},{1,9},{2,10},{3,11},{4,12},{5,13},{6,14},{7,15},{8,0},{9,1},... | collective-permute-start | bytes 1327112 | tf_op jit(solution)/shard_map/ppermute | solution.py:44
  90.1 1.8 %collective-permute-start.12 = (bf16[48,4608]{1,0:T(8,128)(2,1)S(1)}, bf16[48,4608]{1,0:T(8,128)(2,1)S(1)}, u32[]{:S(2)}, u32[]{:S(2)}) collective-permute-start(bf16[48,4608]{1,0:T(8,128)(2,1)S(1)} %collective-permute-done.10), channel_id=1, source_target_pairs={{0,8},{1,9},{2,10},{3,11},{4,12},{5,13},{6,14},{7,15},{8,0},{9,1},... | collective-permute-start | bytes 1327112 | tf_op jit(solution)/shard_map/ppermute | solution.py:44
  90.1 2.4 %collective-permute-start.13 = (bf16[48,4608]{1,0:T(8,128)(2,1)S(1)}, bf16[48,4608]{1,0:T(8,128)(2,1)S(1)}, u32[]{:S(2)}, u32[]{:S(2)}) collective-permute-start(bf16[48,4608]{1,0:T(8,128)(2,1)S(1)} %collective-permute-done.11), channel_id=1, source_target_pairs={{0,8},{1,9},{2,10},{3,11},{4,12},{5,13},{6,14},{7,15},{8,0},{9,1},... | collective-permute-start | bytes 1327112 | tf_op jit(solution)/shard_map/ppermute | solution.py:44
  119.5 2.5 %collective-permute-start.31 = (bf16[192,1792]{1,0:T(8,128)(2,1)S(1)}, bf16[192,1792]{1,0:T(8,128)(2,1)S(1)}, u32[]{:S(2)}, u32[]{:S(2)}) collective-permute-start(bf16[192,1792]{1,0:T(8,128)(2,1)S(1)} %shard_map.124), channel_id=1, source_target_pairs={{0,8},{1,9},{2,10},{3,11},{4,12},{5,13},{6,14},{7,15},{8,0},{9,1},... | collective-permute-start | bytes 2064392 | tf_op jit(solution)/shard_map/ppermute | solution.py:44
  120.0 8.2 %collective-permute-start.27 = (bf16[192,1792]{1,0:T(8,128)(2,1)S(1)}, bf16[192,1792]{1,0:T(8,128)(2,1)S(1)}, u32[]{:S(2)}, u32[]{:S(2)}) collective-permute-start(bf16[192,1792]{1,0:T(8,128)(2,1)S(1)} %get-tuple-element.33), channel_id=1, source_target_pairs={{0,8},{1,9},{2,10},{3,11},{4,12},{5,13},{6,14},{7,15},{8,0},{9,1},... | collective-permute-start | bytes 2064392 | tf_op jit(solution)/shard_map/ppermute | solution.py:44
  122.6 9.8 %copy-start.4 = (f32[3584]{0:T(1024)S(1)}, f32[3584]{0:T(1024)}, u32[]{:S(2)}) copy-start(f32[3584]{0:T(1024)} %param.16) | copy-start | bytes 43012
  122.7 8.8 %collective-permute-start.32 = (bf16[48,1792]{1,0:T(8,128)(2,1)S(1)}, bf16[48,1792]{1,0:T(8,128)(2,1)S(1)}, u32[]{:S(2)}, u32[]{:S(2)}) collective-permute-start(bf16[48,1792]{1,0:T(8,128)(2,1)S(1)} %get-tuple-element.40), channel_id=1, source_target_pairs={{0,1},{1,0},{2,3},{3,2},{4,5},{5,4},{6,7},{7,6},{8,9},{9,8},{10,11... | collective-permute-start | bytes 516104 | tf_op jit(solution)/shard_map/ppermute | solution.py:44
  126.6 33.0 %copy-start.1 = (bf16[16,3584]{1,0:T(8,128)(2,1)S(1)}, bf16[16,3584]{1,0:T(8,128)(2,1)}, u32[]{:S(2)}) copy-start(bf16[16,3584]{1,0:T(8,128)(2,1)} %refs_3_.1) | copy-start | bytes 344068
  126.6 12.2 %collective-permute-start.33 = (bf16[48,1792]{1,0:T(8,128)(2,1)S(1)}, bf16[48,1792]{1,0:T(8,128)(2,1)S(1)}, u32[]{:S(2)}, u32[]{:S(2)}) collective-permute-start(bf16[48,1792]{1,0:T(8,128)(2,1)S(1)} %get-tuple-element.41), channel_id=1, source_target_pairs={{0,16},{1,17},{2,18},{3,19},{4,20},{5,21},{6,22},{7,23},{8,24},{9,... | collective-permute-start | bytes 516104 | tf_op jit(solution)/shard_map/ppermute | solution.py:44
  127.2 11.6 %collective-permute-start.34 = (bf16[48,1792]{1,0:T(8,128)(2,1)S(1)}, bf16[48,1792]{1,0:T(8,128)(2,1)S(1)}, u32[]{:S(2)}, u32[]{:S(2)}) collective-permute-start(bf16[48,1792]{1,0:T(8,128)(2,1)S(1)} %get-tuple-element.42), channel_id=1, source_target_pairs={{0,17},{1,16},{2,19},{3,18},{4,21},{5,20},{6,23},{7,22},{8,25},{9,... | collective-permute-start | bytes 516104 | tf_op jit(solution)/shard_map/ppermute | solution.py:44
  128.8 10.2 %collective-permute-start.28 = (bf16[48,1792]{1,0:T(8,128)(2,1)S(1)}, bf16[48,1792]{1,0:T(8,128)(2,1)S(1)}, u32[]{:S(2)}, u32[]{:S(2)}) collective-permute-start(bf16[48,1792]{1,0:T(8,128)(2,1)S(1)} %get-tuple-element.35), channel_id=1, source_target_pairs={{0,1},{1,0},{2,3},{3,2},{4,5},{5,4},{6,7},{7,6},{8,9},{9,8},{10,11... | collective-permute-start | bytes 516104 | tf_op jit(solution)/shard_map/ppermute | solution.py:44
  130.9 13.0 %collective-permute-start.29 = (bf16[48,1792]{1,0:T(8,128)(2,1)S(1)}, bf16[48,1792]{1,0:T(8,128)(2,1)S(1)}, u32[]{:S(2)}, u32[]{:S(2)}) collective-permute-start(bf16[48,1792]{1,0:T(8,128)(2,1)S(1)} %get-tuple-element.36), channel_id=1, source_target_pairs={{0,16},{1,17},{2,18},{3,19},{4,20},{5,21},{6,22},{7,23},{8,24},{9,... | collective-permute-start | bytes 516104 | tf_op jit(solution)/shard_map/ppermute | solution.py:44
  131.5 12.4 %collective-permute-start.30 = (bf16[48,1792]{1,0:T(8,128)(2,1)S(1)}, bf16[48,1792]{1,0:T(8,128)(2,1)S(1)}, u32[]{:S(2)}, u32[]{:S(2)}) collective-permute-start(bf16[48,1792]{1,0:T(8,128)(2,1)S(1)} %get-tuple-element.37), channel_id=1, source_target_pairs={{0,17},{1,16},{2,19},{3,18},{4,21},{5,20},{6,23},{7,22},{8,25},{9,... | collective-permute-start | bytes 516104 | tf_op jit(solution)/shard_map/ppermute | solution.py:44
  144.6 7.9 %collective-permute-start.35 = (bf16[16,3584]{1,0:T(8,128)(2,1)S(1)}, bf16[16,3584]{1,0:T(8,128)(2,1)S(1)}, u32[]{:S(2)}, u32[]{:S(2)}) collective-permute-start(bf16[16,3584]{1,0:T(8,128)(2,1)S(1)} %get-tuple-element.44), channel_id=1, source_target_pairs={{0,2},{1,3},{2,0},{3,1},{6,4},{7,5},{8,10},{9,11},{10,8},{11,9},{1... | collective-permute-start | bytes 344072 | tf_op jit(solution)/shard_map/ppermute | solution.py:44
  146.9 12.7 %collective-permute-start.36 = (bf16[16,3584]{1,0:T(8,128)(2,1)S(1)}, bf16[16,3584]{1,0:T(8,128)(2,1)S(1)}, u32[]{:S(2)}, u32[]{:S(2)}) collective-permute-start(bf16[16,3584]{1,0:T(8,128)(2,1)S(1)} %get-tuple-element.45), channel_id=1, source_target_pairs={{0,4},{1,5},{4,0},{5,1},{6,2},{7,3},{8,12},{9,13},{12,8},{13,9},{1... | collective-permute-start | bytes 344072 | tf_op jit(solution)/shard_map/ppermute | solution.py:44
  148.8 10.8 %collective-permute-start.37 = (bf16[16,3584]{1,0:T(8,128)(2,1)S(1)}, bf16[16,3584]{1,0:T(8,128)(2,1)S(1)}, u32[]{:S(2)}, u32[]{:S(2)}) collective-permute-start(bf16[16,3584]{1,0:T(8,128)(2,1)S(1)} %get-tuple-element.46), channel_id=1, source_target_pairs={{2,4},{3,5},{4,2},{5,3},{6,0},{7,1},{10,12},{11,13},{12,10},{13,11... | collective-permute-start | bytes 344072 | tf_op jit(solution)/shard_map/ppermute | solution.py:44

commit v3 on v2

--- a/solution.py
+++ b/solution.py
@@ -94,13 +94,10 @@
                 out[j * share : (j + 1) * share, :] = piece[...]
 
 
-def pair_kernel(live, ids, partial, other, own, *lows):
-    share = own.shape[0]
-
+def pair_kernel(live, ids, kept, other, own, *lows):
     def chunk(slot):
         slot = jnp.minimum(slot, live - 1)
-        at = pl.multiple_of((2 * slot + ids[3]) * share, share)
-        return partial[0, pl.ds(at, share), :].astype(F32) + other[slot].astype(F32)
+        return kept[slot].astype(F32) + other[slot].astype(F32)
 
     own[...] = chunk(ids[2])
     for k, low in enumerate(lows, 1):
@@ -208,32 +205,11 @@
     return top + jnp.log(sum([jnp.exp(part - top) for part in every[1:]], jnp.exp(every[0] - top)))
 
 
-def product_kernel(part, ids, grads, head, out):
-    height = out.shape[1] // 2
-    for n in range(2):
-        here = slice(part * out.shape[1] + n * height, part * out.shape[1] + (n + 1) * height)
-        value = lax.dot_general(
-            grads[...], head[here, :], (((1,), (1,)), ((), ())), preferred_element_type=F32
-        )
-        out[:, n * height : (n + 1) * height] = value.astype(out.dtype)
-
-
-def given_kernel(
-    ids, got, labels, scale, t_logits, s_logits, head, given, kept, grads, near, lines, columns, sems
+def logit_kernel(
+    ids, got, labels, scale, t_logits, s_logits, kept, grads, lines, columns
 ):
     vocab = t_logits.shape[1]
     rows = t_logits.shape[0] // 8
-    part = head.shape[0] // 4
-    heads = [
-        pltpu.make_async_copy(
-            head.at[n * part : (n + 1) * part, :],
-            near.at[n * part : (n + 1) * part, :],
-            sems.at[n],
-        )
-        for n in range(4)
-    ]
-    for copy in heads:
-        copy.start()
     total = joined(got, 8 * rows)
     lines[...] = jnp.zeros_like(lines)
     lines[0:1, :] = total[:, : 8 * rows]
@@ -250,13 +226,6 @@
         place = (r // 4) * 2 + r % 2
         into = grads if (r // 2) % 2 else kept
         into[place * rows : (place + 1) * rows, :] = grad.astype(BF16)
-    for n, copy in enumerate(heads):
-        copy.wait()
-        if n < 4 // PARTS:
-            here = slice(n * part, (n + 1) * part)
-            given[:, here] = lax.dot_general(
-                grads[...], near[here, :], (((1,), (1,)), ((), ())), preferred_element_type=F32
-            ).astype(BF16)
 
 
 def prep_kernel(live, share, nseq, ids, *refs):
@@ -354,15 +323,14 @@
     return inverse * scaled - hidden * (inverse * inverse * inverse) * inner
 
 
-def product(grid, grads, head, part, dtype):
-    return call(
-        functools.partial(product_kernel, part),
-        grid.ids,
-        [grads, head],
-        [shape_of((grads.shape[0], head.shape[0] // PARTS), dtype)],
-        [],
-        6,
-    )[0]
+def product(grads, head, part, dtype):
+    width = head.shape[0] // PARTS
+    return lax.dot_general(
+        grads,
+        head[part * width : (part + 1) * width],
+        (((1,), (1,)), ((), ())),
+        preferred_element_type=F32,
+    ).astype(dtype)
 
 
 def reduce_plane(grid, kept, other):
@@ -429,8 +397,16 @@
     grid = Grid(lax.axis_size("dp"), lax.axis_size("tp"), share)
     live = grid.live
 
-    parts = teacher_partial[0, :LIVE].reshape(live, 2, share, width_t)
-    given = lax.dynamic_index_in_dim(parts, 1 - grid.x, 1, keepdims=False)
+    zero = jnp.zeros((), jnp.int32)
+    parts = teacher_partial.reshape(-1, 2, share, width_t)
+
+    def half_of(x):
+        begin = (zero, x, zero, zero)
+        rows = lax.dynamic_slice(parts, begin, (live, 1, share, width_t))
+        return rows.reshape(live, share, width_t)
+
+    given = half_of(1 - grid.x)
+    kept = half_of(grid.x)
     other = grid.send(given, d=1)
     at = jnp.minimum(grid.z, live - 1)
     ks = range(1, grid.depth)
@@ -438,13 +414,12 @@
         own, *lows = call(
             functools.partial(pair_kernel, live),
             grid.ids,
-            [teacher_partial, other],
+            [kept, other],
             [shape_of((share, width_t), F32)] + [shape_of((share, width_t), BF16) for k in ks],
             [],
             4,
         )
     else:
-        kept = lax.dynamic_index_in_dim(parts, grid.x, 1, keepdims=False)
         pair = kept.astype(F32) + other.astype(F32)
         own = lax.dynamic_index_in_dim(pair, at, 0, keepdims=False)
         lows = [
@@ -528,28 +503,21 @@
     got = lax.all_to_all(sent, AXES, 0, 0, tiled=True)
 
     half = rows // 2
-    given, keeps, gives, near = call(
-        given_kernel,
+    keeps, gives = call(
+        logit_kernel,
         grid.ids,
         [got, label_column, scale_column, t_logits, s_logits],
-        [
-            shape_of((half, width_s // PARTS), BF16),
-            shape_of((half, vocab_dev), BF16),
-            shape_of((half, vocab_dev), BF16),
-            shape_of(student_head.shape, BF16),
-        ],
-        [pltpu.VMEM((128, rows), F32), pltpu.VMEM((rows, 128), F32), pltpu.SemaphoreType.DMA((4,))],
-        10,
-        [student_head],
+        [shape_of((half, vocab_dev), BF16), shape_of((half, vocab_dev), BF16)],
+        [pltpu.VMEM((128, rows), F32), pltpu.VMEM((rows, 128), F32)],
+        6,
     )
     others = []
     for part in range(PARTS):
-        if part:
-            given = product(grid, gives, near, part, BF16)
+        given = product(gives, student_head, part, BF16)
         others.append(grid.send(given, b=1))
     parts = []
     for part in range(PARTS):
-        kept = product(grid, keeps, near, part, F32)
+        kept = product(keeps, student_head, part, F32)
         parts.append(reduce_plane(grid, kept, others[part]))
     sums = reduce_depth(grid, parts, share)
     row_loss = call(

time: 162 us -> 159 us (0.981)
  Pallas kernels: 21.9 us -> 13.5 us
  matrix products: 6.8 us -> 12.2 us
    pallas_call x16 -> x13, Pallas kernels: 21.9 us -> 13.5 us  [call(): pl.pallas_call(kernel, out_shape=outs, in_specs=[SMEM] + [VMEM] * len(arg...]
    dot_general x0 -> x4, matrix products: none -> 5.43 us  [product(): lax.dot_general(grads, head[part * width:(part + 1) * width], (((1,), (1,...]
  transfers between devices with their start and end apart: 38 -> 38, of which waited for: 16 -> 16; matrix products, arithmetic and copies ran while one was open for 5% -> 7% of each run, Pallas kernels for 8% -> 5%
where the time goes in v3:
time: 159 us; the launch traced here: 158 us
  waiting for transfers between devices  57.4 us (36%)
  starting transfers between devices  51.5 us (32%)
  blocking collectives  15.5 us (10%)
  Pallas kernels  13.5 us (8%)
  matrix products  12.2 us (8%)
  local copies, waits for them, and re-layouts  3.78 us (2%)
  other arithmetic  2.77 us (2%)
    ppermute x38, waiting for transfers between devices, send(): return lax.ppermute(value, AXES, pairs)  57.4 us
    ppermute x38, starting transfers between devices, send(): return lax.ppermute(value, AXES, pairs)  51.5 us
    all_to_all x1, blocking collectives, shards(): got = lax.all_to_all(sent, AXES, 0, 0, tiled=True)  15.5 us
    pallas_call x13, Pallas kernels, call(): pl.pallas_call(kernel, out_shape=outs, in_specs=[SMEM] + [VMEM] * len(arg...  13.5 us
    dot_general x4, matrix products, product(): lax.dot_general(grads, head[part * width:(part + 1) * width], (((1,), (1,...  5.43 us
    dot_general x1, matrix products, shards(): t_logits = jnp.dot(whole_t, teacher_head, preferred_element_type=F32)  3.8 us
  transfers between devices with their start and end apart: 38, of which 16 were waited for; matrix products, arithmetic and copies ran while one was open for 7% of the time, Pallas kernels for 5%

profile of v3, /device:TPU:0, one launch (start us, length us, event | category | flops | bytes accessed | tf_op | source)
XLA Modules:
  0.0 157.9 jit_solution(14636087567230962845)
XLA Ops:
  0.6 1.1 fusion.14
  1.7 1.0 fusion.16.refs_0_
  2.7 5.0 %collective-permute-start.14 = (bf16[16,3584]{1,0:T(8,128)(2,1)S(1)}, bf16[16,3584]{1,0:T(8,128)(2,1)S(1)}, u32[]{:S(2)}, u32[]{:S(2)}) collective-permute-start(bf16[16,3584]{1,0:T(8,128)(2,1)S(1)} %fusion.16.refs_0_), channel_id=1, source_target_pairs={{0,2},{1,3},{2,0},{3,1},{4,6},{5,7},{8,10},{9,11},{10,8},{11,9},{1... | collective-permute-start | bytes 344072 | tf_op jit(solution)/shard_map/ppermute | solution.py:44
  7.7 4.5 %collective-permute-start.15 = (bf16[16,3584]{1,0:T(8,128)(2,1)S(1)}, bf16[16,3584]{1,0:T(8,128)(2,1)S(1)}, u32[]{:S(2)}, u32[]{:S(2)}) collective-permute-start(bf16[16,3584]{1,0:T(8,128)(2,1)S(1)} %fusion.16.refs_0_), channel_id=1, source_target_pairs={{0,4},{1,5},{2,6},{3,7},{4,0},{5,1},{8,12},{9,13},{10,14},{11,15},... | collective-permute-start | bytes 344072 | tf_op jit(solution)/shard_map/ppermute | solution.py:44
  12.2 1.3 collective-permute-start.16
  13.5 0.7 pad_add_fusion
  14.2 1.6 %collective-permute-start.25 = (s32[1,136]{1,0:T(1,128)S(1)}, s32[1,136]{1,0:T(1,128)S(1)}, u32[]{:S(2)}, u32[]{:S(2)}) collective-permute-start(s32[1,136]{1,0:T(1,128)S(1)} %bitcast.27), channel_id=1, source_target_pairs={{0,16},{1,17},{2,18},{3,19},{4,20},{5,21},{6,22},{7,23},{8,24},{9,... | collective-permute-start | bytes 1640 | tf_op jit(solution)/shard_map/ppermute | solution.py:44
  15.8 1.2 dynamic-slice_bitcast_fusion
  17.0 0.7 broadcast_in_dim.14.refs_5_
  17.8 0.7 broadcast_in_dim.15.refs_6_
  19.0 1.5 collective-permute-start
  20.5 1.1 collective-permute-done.26.refs_3_
  21.6 1.1 shard_map.117
  22.8 0.7 shard_map.116
  23.4 1.6 collective-permute-start.17
  25.5 6.5 %collective-permute-done.other = bf16[3,16,4608]{2,1,0:T(8,128)(2,1)S(1)} collective-permute-done((bf16[3,16,4608]{2,1,0:T(8,128)(2,1)S(1)}, bf16[3,16,4608]{2,1,0:T(8,128)(2,1)S(1)}, u32[]{:S(2)}, u32[]{:S(2)}) %collective-permute-start) | collective-permute-done | bytes 442400 | tf_op jit(solution)/shard_map/ppermute | solution.py:44
  32.0 0.7 shard_map.113
  32.7 3.4 %collective-permute-start.1 = (bf16[16,4608]{1,0:T(8,128)(2,1)S(1)}, bf16[16,4608]{1,0:T(8,128)(2,1)S(1)}, u32[]{:S(2)}, u32[]{:S(2)}) collective-permute-start(bf16[16,4608]{1,0:T(8,128)(2,1)S(1)} %get-tuple-element.24), channel_id=1, source_target_pairs={{0,2},{1,3},{2,0},{3,1},{6,4},{7,5},{8,10},{9,11},{10,8},{11,9},{1... | collective-permute-start | bytes 442376 | tf_op jit(solution)/shard_map/ppermute | solution.py:44
  36.1 1.9 %collective-permute-start.2 = (bf16[16,4608]{1,0:T(8,128)(2,1)S(1)}, bf16[16,4608]{1,0:T(8,128)(2,1)S(1)}, u32[]{:S(2)}, u32[]{:S(2)}) collective-permute-start(bf16[16,4608]{1,0:T(8,128)(2,1)S(1)} %get-tuple-element.25), channel_id=1, source_target_pairs={{0,4},{1,5},{4,0},{5,1},{6,2},{7,3},{8,12},{9,13},{12,8},{13,9},{1... | collective-permute-start | bytes 442376 | tf_op jit(solution)/shard_map/ppermute | solution.py:44
  38.1 0.7 collective-permute-done.17
  38.8 1.3 collective-permute-start.3
  40.2 2.4 %collective-permute-start.21 = (bf16[48,3584]{1,0:T(8,128)(2,1)S(1)}, bf16[48,3584]{1,0:T(8,128)(2,1)S(1)}, u32[]{:S(2)}, u32[]{:S(2)}) collective-permute-start(bf16[48,3584]{1,0:T(8,128)(2,1)S(1)} %shard_map.116), channel_id=1, source_target_pairs={{0,17},{1,16},{2,19},{3,18},{4,21},{5,20},{6,23},{7,22},{8,25},{9,... | collective-permute-start | bytes 1032200 | tf_op jit(solution)/shard_map/ppermute | solution.py:44
  42.6 7.7 %collective-permute-done.2.refs_2_ = bf16[16,4608]{1,0:T(8,128)(2,1)S(1)} collective-permute-done((bf16[16,4608]{1,0:T(8,128)(2,1)S(1)}, bf16[16,4608]{1,0:T(8,128)(2,1)S(1)}, u32[]{:S(2)}, u32[]{:S(2)}) %collective-permute-start.2) | collective-permute-done | bytes 147488 | tf_op jit(solution)/shard_map/ppermute | solution.py:44
  50.3 0.9 shard_map.114.refs_0_
  51.2 4.9 %collective-permute-start.4 = (bf16[16,4608]{1,0:T(8,128)(2,1)S(1)}, bf16[16,4608]{1,0:T(8,128)(2,1)S(1)}, u32[]{:S(2)}, u32[]{:S(2)}) collective-permute-start(bf16[16,4608]{1,0:T(8,128)(2,1)S(1)} %shard_map.114.refs_0_), channel_id=1, source_target_pairs={{0,2},{1,3},{2,0},{3,1},{4,6},{5,7},{8,10},{9,11},{10,8},{11,9},{1... | collective-permute-start | bytes 442376 | tf_op jit(solution)/shard_map/ppermute | solution.py:44
  56.1 1.9 %collective-permute-start.5 = (bf16[16,4608]{1,0:T(8,128)(2,1)S(1)}, bf16[16,4608]{1,0:T(8,128)(2,1)S(1)}, u32[]{:S(2)}, u32[]{:S(2)}) collective-permute-start(bf16[16,4608]{1,0:T(8,128)(2,1)S(1)} %shard_map.114.refs_0_), channel_id=1, source_target_pairs={{0,4},{1,5},{2,6},{3,7},{4,0},{5,1},{8,12},{9,13},{10,14},{11,15},... | collective-permute-start | bytes 442376 | tf_op jit(solution)/shard_map/ppermute | solution.py:44
  58.0 1.3 collective-permute-start.6
  60.0 5.5 %collective-permute-done.5.refs_2_ = bf16[16,4608]{1,0:T(8,128)(2,1)S(1)} collective-permute-done((bf16[16,4608]{1,0:T(8,128)(2,1)S(1)}, bf16[16,4608]{1,0:T(8,128)(2,1)S(1)}, u32[]{:S(2)}, u32[]{:S(2)}) %collective-permute-start.5) | collective-permute-done | bytes 147488 | tf_op jit(solution)/shard_map/ppermute | solution.py:44
  65.6 0.7 shard_map.115
  66.2 1.6 collective-permute-start.7
  67.8 1.6 %collective-permute-start.10 = (bf16[48,4608]{1,0:T(8,128)(2,1)S(1)}, bf16[48,4608]{1,0:T(8,128)(2,1)S(1)}, u32[]{:S(2)}, u32[]{:S(2)}) collective-permute-start(bf16[48,4608]{1,0:T(8,128)(2,1)S(1)} %shard_map.115), channel_id=1, source_target_pairs={{0,16},{1,17},{2,18},{3,19},{4,20},{5,21},{6,22},{7,23},{8,24},{9,... | collective-permute-start | bytes 1327112 | tf_op jit(solution)/shard_map/ppermute | solution.py:44
  69.5 0.5 collective-permute-start.11
  70.2 3.0 %fusion.18.logits.s_logits = f32[384,1024]{1,0:T(8,128)S(1)} fusion(bf16[384,3584]{1,0:T(8,128)(2,1)S(1)} %constant_dynamic-update-slice_fusion.8, bf16[3584,1024]{1,0:T(8,128)(2,1)S(1)} %copy-done.3), kind=kOutput, calls=%fused_computation.37 | convolution fusion | flops 2818572288 | bytes 11665408 | tf_op jit(solution)/shard_map/dot_general | solution.py:489
  73.2 2.3 %shard_map.118.s_cols = f32[384,128]{1,0:T(8,128)S(1)} custom-call(s32[5]{0:T(128)S(1)} %stack.23.ids, f32[384,1024]{1,0:T(8,128)S(1)} %fusion.18.logits.s_logits, s32[384,1]{1,0:T(8,128)S(1)} %get-tuple-element.27.labels), custom_call_target="tpu_custom_call" | custom-call | tf_op jit(solution)/shard_map/pallas_call | solution.py:76
  75.5 3.8 %collective-permute-done.7 = bf16[48,4608]{1,0:T(8,128)(2,1)S(1)} collective-permute-done((bf16[48,4608]{1,0:T(8,128)(2,1)S(1)}, bf16[48,4608]{1,0:T(8,128)(2,1)S(1)}, u32[]{:S(2)}, u32[]{:S(2)}) %collective-permute-start.7) | collective-permute-done | bytes 442400 | tf_op jit(solution)/shard_map/ppermute | solution.py:44
  79.3 10.6 %collective-permute-done.10 = bf16[48,4608]{1,0:T(8,128)(2,1)S(1)} collective-permute-done((bf16[48,4608]{1,0:T(8,128)(2,1)S(1)}, bf16[48,4608]{1,0:T(8,128)(2,1)S(1)}, u32[]{:S(2)}, u32[]{:S(2)}) %collective-permute-start.10) | collective-permute-done | bytes 442400 | tf_op jit(solution)/shard_map/ppermute | solution.py:44
  90.7 1.1 collective-permute-done.12
  91.8 0.6 collective-permute-done.13
  92.5 3.8 %fusion.17.logits.t_logits = f32[384,1024]{1,0:T(8,128)S(1)} fusion(bf16[384,4608]{1,0:T(8,128)(2,1)S(1)} %constant_dynamic-update-slice_fusion, bf16[4608,1024]{1,0:T(8,128)(2,1)S(1)} %bitcast.33), kind=kOutput, calls=%fused_computation.36 | convolution fusion | flops 3623878656 | bytes 14548992 | tf_op jit(solution)/shard_map/dot_general | solution.py:493
  96.3 1.4 shard_map.119
  97.6 15.5 %all_to_all.5.got = f32[32,1,1536]{2,1,0:T(1,128)S(1)} all-to-all(f32[32,1,1536]{2,1,0:T(1,128)S(1)} %shard_map.119), channel_id=1, replica_groups=mesh['dp'=4,'tp'=8] {'dp','tp'}, dimensions={0} | all-to-all | bytes 393216 | tf_op jit(solution)/shard_map/all_to_all | solution.py:503
  113.1 1.6 shard_map.120
  114.7 1.4 fusion.8
  116.5 1.4 fusion.11
  118.1 1.4 fusion.6.kept
  119.4 0.7 shard_map.121
  120.1 2.1 %collective-permute-start.28 = (bf16[48,1792]{1,0:T(8,128)(2,1)S(1)}, bf16[48,1792]{1,0:T(8,128)(2,1)S(1)}, u32[]{:S(2)}, u32[]{:S(2)}) collective-permute-start(bf16[48,1792]{1,0:T(8,128)(2,1)S(1)} %get-tuple-element.32), channel_id=1, source_target_pairs={{0,1},{1,0},{2,3},{3,2},{4,5},{5,4},{6,7},{7,6},{8,9},{9,8},{10,11... | collective-permute-start | bytes 516104 | tf_op jit(solution)/shard_map/ppermute | solution.py:44
  122.2 1.4 fusion.2.kept
  123.6 0.6 collective-permute-start.29
  124.2 0.9 collective-permute-start.30
  125.1 0.7 shard_map.122
  125.8 2.1 %collective-permute-start.32 = (bf16[48,1792]{1,0:T(8,128)(2,1)S(1)}, bf16[48,1792]{1,0:T(8,128)(2,1)S(1)}, u32[]{:S(2)}, u32[]{:S(2)}) collective-permute-start(bf16[48,1792]{1,0:T(8,128)(2,1)S(1)} %get-tuple-element.36), channel_id=1, source_target_pairs={{0,1},{1,0},{2,3},{3,2},{4,5},{5,4},{6,7},{7,6},{8,9},{9,8},{10,11... | collective-permute-start | bytes 516104 | tf_op jit(solution)/shard_map/ppermute | solution.py:44
  128.4 1.0 collective-permute-start.34
  129.4 0.7 shard_map.125
  130.1 4.6 %collective-permute-done.29.refs_2_ = bf16[48,1792]{1,0:T(8,128)(2,1)S(1)} collective-permute-done((bf16[48,1792]{1,0:T(8,128)(2,1)S(1)}, bf16[48,1792]{1,0:T(8,128)(2,1)S(1)}, u32[]{:S(2)}, u32[]{:S(2)}) %collective-permute-start.29) | collective-permute-done | bytes 172064 | tf_op jit(solution)/shard_map/ppermute | solution.py:44
  134.7 1.3 collective-permute-done.32.refs_5_
  136.0 4.8 %collective-permute-done.33.refs_6_ = bf16[48,1792]{1,0:T(8,128)(2,1)S(1)} collective-permute-done((bf16[48,1792]{1,0:T(8,128)(2,1)S(1)}, bf16[48,1792]{1,0:T(8,128)(2,1)S(1)}, u32[]{:S(2)}, u32[]{:S(2)}) %collective-permute-start.33) | collective-permute-done | bytes 172064 | tf_op jit(solution)/shard_map/ppermute | solution.py:44
  140.8 0.7 shard_map.123
  141.5 2.3 %collective-permute-start.35 = (bf16[16,3584]{1,0:T(8,128)(2,1)S(1)}, bf16[16,3584]{1,0:T(8,128)(2,1)S(1)}, u32[]{:S(2)}, u32[]{:S(2)}) collective-permute-start(bf16[16,3584]{1,0:T(8,128)(2,1)S(1)} %get-tuple-element.40), channel_id=1, source_target_pairs={{0,2},{1,3},{2,0},{3,1},{6,4},{7,5},{8,10},{9,11},{10,8},{11,9},{1... | collective-permute-start | bytes 344072 | tf_op jit(solution)/shard_map/ppermute | solution.py:44
  143.8 1.9 %collective-permute-start.36 = (bf16[16,3584]{1,0:T(8,128)(2,1)S(1)}, bf16[16,3584]{1,0:T(8,128)(2,1)S(1)}, u32[]{:S(2)}, u32[]{:S(2)}) collective-permute-start(bf16[16,3584]{1,0:T(8,128)(2,1)S(1)} %get-tuple-element.41), channel_id=1, source_target_pairs={{0,4},{1,5},{4,0},{5,1},{6,2},{7,3},{8,12},{9,13},{12,8},{13,9},{1... | collective-permute-start | bytes 344072 | tf_op jit(solution)/shard_map/ppermute | solution.py:44
  145.7 1.3 collective-permute-start.37
  147.6 1.8 %collective-permute-done.35.refs_0_ = bf16[16,3584]{1,0:T(8,128)(2,1)S(1)} collective-permute-done((bf16[16,3584]{1,0:T(8,128)(2,1)S(1)}, bf16[16,3584]{1,0:T(8,128)(2,1)S(1)}, u32[]{:S(2)}, u32[]{:S(2)}) %collective-permute-start.35) | collective-permute-done | bytes 114720 | tf_op jit(solution)/shard_map/ppermute | solution.py:44
  149.4 7.1 %collective-permute-done.36.refs_1_ = bf16[16,3584]{1,0:T(8,128)(2,1)S(1)} collective-permute-done((bf16[16,3584]{1,0:T(8,128)(2,1)S(1)}, bf16[16,3584]{1,0:T(8,128)(2,1)S(1)}, u32[]{:S(2)}, u32[]{:S(2)}) %collective-permute-start.36) | collective-permute-done | bytes 114720 | tf_op jit(solution)/shard_map/ppermute | solution.py:44
  156.5 1.4 shard_map.124
  (73 shorter events, 4.4 us)
Async XLA Ops:
  0.6 49.7 %copy-start.1 = (bf16[16,4608]{1,0:T(8,128)(2,1)S(1)}, bf16[16,4608]{1,0:T(8,128)(2,1)}, u32[]{:S(2)}) copy-start(bf16[16,4608]{1,0:T(8,128)(2,1)} %refs_4_.1) | copy-start | bytes 442372
  2.7 20.0 %collective-permute-start.14 = (bf16[16,3584]{1,0:T(8,128)(2,1)S(1)}, bf16[16,3584]{1,0:T(8,128)(2,1)S(1)}, u32[]{:S(2)}, u32[]{:S(2)}) collective-permute-start(bf16[16,3584]{1,0:T(8,128)(2,1)S(1)} %fusion.16.refs_0_), channel_id=1, source_target_pairs={{0,2},{1,3},{2,0},{3,1},{4,6},{5,7},{8,10},{9,11},{10,8},{11,9},{1... | collective-permute-start | bytes 344072 | tf_op jit(solution)/shard_map/ppermute | solution.py:44
  7.7 15.0 %collective-permute-start.15 = (bf16[16,3584]{1,0:T(8,128)(2,1)S(1)}, bf16[16,3584]{1,0:T(8,128)(2,1)S(1)}, u32[]{:S(2)}, u32[]{:S(2)}) collective-permute-start(bf16[16,3584]{1,0:T(8,128)(2,1)S(1)} %fusion.16.refs_0_), channel_id=1, source_target_pairs={{0,4},{1,5},{2,6},{3,7},{4,0},{5,1},{8,12},{9,13},{10,14},{11,15},... | collective-permute-start | bytes 344072 | tf_op jit(solution)/shard_map/ppermute | solution.py:44
  12.2 10.6 %collective-permute-start.16 = (bf16[16,3584]{1,0:T(8,128)(2,1)S(1)}, bf16[16,3584]{1,0:T(8,128)(2,1)S(1)}, u32[]{:S(2)}, u32[]{:S(2)}) collective-permute-start(bf16[16,3584]{1,0:T(8,128)(2,1)S(1)} %fusion.16.refs_0_), channel_id=1, source_target_pairs={{0,6},{1,7},{2,4},{3,5},{4,2},{5,3},{8,14},{9,15},{10,12},{11,13},... | collective-permute-start | bytes 344072 | tf_op jit(solution)/shard_map/ppermute | solution.py:44
  14.2 4.3 %collective-permute-start.24 = (s32[1,136]{1,0:T(1,128)S(1)}, s32[1,136]{1,0:T(1,128)S(1)}, u32[]{:S(2)}, u32[]{:S(2)}) collective-permute-start(s32[1,136]{1,0:T(1,128)S(1)} %bitcast.26), channel_id=1, source_target_pairs={{0,8},{1,9},{2,10},{3,11},{4,12},{5,13},{6,14},{7,15},{8,0},{9,1},... | collective-permute-start | bytes 1640 | tf_op jit(solution)/shard_map/ppermute | solution.py:44
  14.2 4.8 %collective-permute-start.25 = (s32[1,136]{1,0:T(1,128)S(1)}, s32[1,136]{1,0:T(1,128)S(1)}, u32[]{:S(2)}, u32[]{:S(2)}) collective-permute-start(s32[1,136]{1,0:T(1,128)S(1)} %bitcast.27), channel_id=1, source_target_pairs={{0,16},{1,17},{2,18},{3,19},{4,20},{5,21},{6,22},{7,23},{8,24},{9,... | collective-permute-start | bytes 1640 | tf_op jit(solution)/shard_map/ppermute | solution.py:44
  18.5 3.1 %collective-permute-start.26 = (s32[1,136]{1,0:T(1,128)S(1)}, s32[1,136]{1,0:T(1,128)S(1)}, u32[]{:S(2)}, u32[]{:S(2)}) collective-permute-start(s32[1,136]{1,0:T(1,128)S(1)} %bitcast.28), channel_id=1, source_target_pairs={{0,24},{1,25},{2,26},{3,27},{4,28},{5,29},{6,30},{7,31},{8,16},{9,... | collective-permute-start | bytes 1640 | tf_op jit(solution)/shard_map/ppermute | solution.py:44
  19.0 13.0 %collective-permute-start = (bf16[3,16,4608]{2,1,0:T(8,128)(2,1)S(1)}, bf16[3,16,4608]{2,1,0:T(8,128)(2,1)S(1)}, u32[]{:S(2)}, u32[]{:S(2)}) collective-permute-start(bf16[3,16,4608]{2,1,0:T(8,128)(2,1)S(1)} %get-tuple-element.44), channel_id=1, source_target_pairs={{0,1},{1,0},{2,3},{3,2},{4,5},{5,4},{6,7},{7,6},{8,9},{9,8},{10,11... | collective-permute-start | bytes 1327112 | tf_op jit(solution)/shard_map/ppermute | solution.py:44
  23.4 15.3 %collective-permute-start.17 = (bf16[48,3584]{1,0:T(8,128)(2,1)S(1)}, bf16[48,3584]{1,0:T(8,128)(2,1)S(1)}, u32[]{:S(2)}, u32[]{:S(2)}) collective-permute-start(bf16[48,3584]{1,0:T(8,128)(2,1)S(1)} %shard_map.116), channel_id=1, source_target_pairs={{0,1},{1,0},{2,3},{3,2},{4,5},{5,4},{6,7},{7,6},{8,9},{9,8},{10,11... | collective-permute-start | bytes 1032200 | tf_op jit(solution)/shard_map/ppermute | solution.py:44
  25.0 33.0 %collective-permute-start.18 = (bf16[48,3584]{1,0:T(8,128)(2,1)S(1)}, bf16[48,3584]{1,0:T(8,128)(2,1)S(1)}, u32[]{:S(2)}, u32[]{:S(2)}) collective-permute-start(bf16[48,3584]{1,0:T(8,128)(2,1)S(1)} %shard_map.116), channel_id=1, source_target_pairs={{0,8},{1,9},{2,10},{3,11},{4,12},{5,13},{6,14},{7,15},{8,0},{9,1},... | collective-permute-start | bytes 1032200 | tf_op jit(solution)/shard_map/ppermute | solution.py:44
  25.0 34.4 %collective-permute-start.20 = (bf16[48,3584]{1,0:T(8,128)(2,1)S(1)}, bf16[48,3584]{1,0:T(8,128)(2,1)S(1)}, u32[]{:S(2)}, u32[]{:S(2)}) collective-permute-start(bf16[48,3584]{1,0:T(8,128)(2,1)S(1)} %shard_map.116), channel_id=1, source_target_pairs={{0,16},{1,17},{2,18},{3,19},{4,20},{5,21},{6,22},{7,23},{8,24},{9,... | collective-permute-start | bytes 1032200 | tf_op jit(solution)/shard_map/ppermute | solution.py:44
  32.7 7.5 %collective-permute-start.1 = (bf16[16,4608]{1,0:T(8,128)(2,1)S(1)}, bf16[16,4608]{1,0:T(8,128)(2,1)S(1)}, u32[]{:S(2)}, u32[]{:S(2)}) collective-permute-start(bf16[16,4608]{1,0:T(8,128)(2,1)S(1)} %get-tuple-element.24), channel_id=1, source_target_pairs={{0,2},{1,3},{2,0},{3,1},{6,4},{7,5},{8,10},{9,11},{10,8},{11,9},{1... | collective-permute-start | bytes 442376 | tf_op jit(solution)/shard_map/ppermute | solution.py:44
  36.1 14.2 %collective-permute-start.2 = (bf16[16,4608]{1,0:T(8,128)(2,1)S(1)}, bf16[16,4608]{1,0:T(8,128)(2,1)S(1)}, u32[]{:S(2)}, u32[]{:S(2)}) collective-permute-start(bf16[16,4608]{1,0:T(8,128)(2,1)S(1)} %get-tuple-element.25), channel_id=1, source_target_pairs={{0,4},{1,5},{4,0},{5,1},{6,2},{7,3},{8,12},{9,13},{12,8},{13,9},{1... | collective-permute-start | bytes 442376 | tf_op jit(solution)/shard_map/ppermute | solution.py:44
  38.8 11.6 %collective-permute-start.3 = (bf16[16,4608]{1,0:T(8,128)(2,1)S(1)}, bf16[16,4608]{1,0:T(8,128)(2,1)S(1)}, u32[]{:S(2)}, u32[]{:S(2)}) collective-permute-start(bf16[16,4608]{1,0:T(8,128)(2,1)S(1)} %get-tuple-element.26), channel_id=1, source_target_pairs={{2,4},{3,5},{4,2},{5,3},{6,0},{7,1},{10,12},{11,13},{12,10},{13,11... | collective-permute-start | bytes 442376 | tf_op jit(solution)/shard_map/ppermute | solution.py:44
  40.0 30.1 %copy-start.3 = (bf16[3584,1024]{1,0:T(8,128)(2,1)S(1)}, bf16[3584,1024]{1,0:T(8,128)(2,1)}, u32[]{:S(2)}) copy-start(bf16[3584,1024]{1,0:T(8,128)(2,1)} %param.17) | copy-start | bytes 22020100
  40.2 19.3 %collective-permute-start.21 = (bf16[48,3584]{1,0:T(8,128)(2,1)S(1)}, bf16[48,3584]{1,0:T(8,128)(2,1)S(1)}, u32[]{:S(2)}, u32[]{:S(2)}) collective-permute-start(bf16[48,3584]{1,0:T(8,128)(2,1)S(1)} %shard_map.116), channel_id=1, source_target_pairs={{0,17},{1,16},{2,19},{3,18},{4,21},{5,20},{6,23},{7,22},{8,25},{9,... | collective-permute-start | bytes 1032200 | tf_op jit(solution)/shard_map/ppermute | solution.py:44
  51.2 8.8 %collective-permute-start.4 = (bf16[16,4608]{1,0:T(8,128)(2,1)S(1)}, bf16[16,4608]{1,0:T(8,128)(2,1)S(1)}, u32[]{:S(2)}, u32[]{:S(2)}) collective-permute-start(bf16[16,4608]{1,0:T(8,128)(2,1)S(1)} %shard_map.114.refs_0_), channel_id=1, source_target_pairs={{0,2},{1,3},{2,0},{3,1},{4,6},{5,7},{8,10},{9,11},{10,8},{11,9},{1... | collective-permute-start | bytes 442376 | tf_op jit(solution)/shard_map/ppermute | solution.py:44
  56.1 9.5 %collective-permute-start.5 = (bf16[16,4608]{1,0:T(8,128)(2,1)S(1)}, bf16[16,4608]{1,0:T(8,128)(2,1)S(1)}, u32[]{:S(2)}, u32[]{:S(2)}) collective-permute-start(bf16[16,4608]{1,0:T(8,128)(2,1)S(1)} %shard_map.114.refs_0_), channel_id=1, source_target_pairs={{0,4},{1,5},{2,6},{3,7},{4,0},{5,1},{8,12},{9,13},{10,14},{11,15},... | collective-permute-start | bytes 442376 | tf_op jit(solution)/shard_map/ppermute | solution.py:44
  58.0 7.6 %collective-permute-start.6 = (bf16[16,4608]{1,0:T(8,128)(2,1)S(1)}, bf16[16,4608]{1,0:T(8,128)(2,1)S(1)}, u32[]{:S(2)}, u32[]{:S(2)}) collective-permute-start(bf16[16,4608]{1,0:T(8,128)(2,1)S(1)} %shard_map.114.refs_0_), channel_id=1, source_target_pairs={{0,6},{1,7},{2,4},{3,5},{4,2},{5,3},{8,14},{9,15},{10,12},{11,13},... | collective-permute-start | bytes 442376 | tf_op jit(solution)/shard_map/ppermute | solution.py:44
  59.4 8.5 %collective-permute-start.19 = (bf16[48,3584]{1,0:T(8,128)(2,1)S(1)}, bf16[48,3584]{1,0:T(8,128)(2,1)S(1)}, u32[]{:S(2)}, u32[]{:S(2)}) collective-permute-start(bf16[48,3584]{1,0:T(8,128)(2,1)S(1)} %collective-permute-done.17), channel_id=1, source_target_pairs={{0,8},{1,9},{2,10},{3,11},{4,12},{5,13},{6,14},{7,15},{8,0},{9,1},... | collective-permute-start | bytes 1032200 | tf_op jit(solution)/shard_map/ppermute | solution.py:44
  59.4 10.1 %collective-permute-start.22 = (bf16[48,3584]{1,0:T(8,128)(2,1)S(1)}, bf16[48,3584]{1,0:T(8,128)(2,1)S(1)}, u32[]{:S(2)}, u32[]{:S(2)}) collective-permute-start(bf16[48,3584]{1,0:T(8,128)(2,1)S(1)} %collective-permute-done.20), channel_id=1, source_target_pairs={{0,8},{1,9},{2,10},{3,11},{4,12},{5,13},{6,14},{7,15},{8,0},{9,1},... | collective-permute-start | bytes 1032200 | tf_op jit(solution)/shard_map/ppermute | solution.py:44
  60.0 10.1 %collective-permute-start.23 = (bf16[48,3584]{1,0:T(8,128)(2,1)S(1)}, bf16[48,3584]{1,0:T(8,128)(2,1)S(1)}, u32[]{:S(2)}, u32[]{:S(2)}) collective-permute-start(bf16[48,3584]{1,0:T(8,128)(2,1)S(1)} %collective-permute-done.21), channel_id=1, source_target_pairs={{0,8},{1,9},{2,10},{3,11},{4,12},{5,13},{6,14},{7,15},{8,0},{9,1},... | collective-permute-start | bytes 1032200 | tf_op jit(solution)/shard_map/ppermute | solution.py:44
  66.2 13.1 %collective-permute-start.7 = (bf16[48,4608]{1,0:T(8,128)(2,1)S(1)}, bf16[48,4608]{1,0:T(8,128)(2,1)S(1)}, u32[]{:S(2)}, u32[]{:S(2)}) collective-permute-start(bf16[48,4608]{1,0:T(8,128)(2,1)S(1)} %shard_map.115), channel_id=1, source_target_pairs={{0,1},{1,0},{2,3},{3,2},{4,5},{5,4},{6,7},{7,6},{8,9},{9,8},{10,11... | collective-permute-start | bytes 1327112 | tf_op jit(solution)/shard_map/ppermute | solution.py:44
  67.8 22.7 %collective-permute-start.8 = (bf16[48,4608]{1,0:T(8,128)(2,1)S(1)}, bf16[48,4608]{1,0:T(8,128)(2,1)S(1)}, u32[]{:S(2)}, u32[]{:S(2)}) collective-permute-start(bf16[48,4608]{1,0:T(8,128)(2,1)S(1)} %shard_map.115), channel_id=1, source_target_pairs={{0,8},{1,9},{2,10},{3,11},{4,12},{5,13},{6,14},{7,15},{8,0},{9,1},... | collective-permute-start | bytes 1327112 | tf_op jit(solution)/shard_map/ppermute | solution.py:44
  67.8 22.1 %collective-permute-start.10 = (bf16[48,4608]{1,0:T(8,128)(2,1)S(1)}, bf16[48,4608]{1,0:T(8,128)(2,1)S(1)}, u32[]{:S(2)}, u32[]{:S(2)}) collective-permute-start(bf16[48,4608]{1,0:T(8,128)(2,1)S(1)} %shard_map.115), channel_id=1, source_target_pairs={{0,16},{1,17},{2,18},{3,19},{4,20},{5,21},{6,22},{7,23},{8,24},{9,... | collective-permute-start | bytes 1327112 | tf_op jit(solution)/shard_map/ppermute | solution.py:44
  69.5 20.4 %collective-permute-start.11 = (bf16[48,4608]{1,0:T(8,128)(2,1)S(1)}, bf16[48,4608]{1,0:T(8,128)(2,1)S(1)}, u32[]{:S(2)}, u32[]{:S(2)}) collective-permute-start(bf16[48,4608]{1,0:T(8,128)(2,1)S(1)} %shard_map.115), channel_id=1, source_target_pairs={{0,17},{1,16},{2,19},{3,18},{4,21},{5,20},{6,23},{7,22},{8,25},{9,... | collective-permute-start | bytes 1327112 | tf_op jit(solution)/shard_map/ppermute | solution.py:44
  70.1 22.3 %slice-start = ((s8[9437184]{0:T(1024)(128)(4,1)}), s8[4194304]{0:T(1024)(128)(4,1)S(1)}, s32[]{:S(2)}) async-start(s8[9437184]{0:T(1024)(128)(4,1)} %bitcast.32), calls=%async_computation.1 | async-start | bytes 8388608
  70.2 22.3 %slice-start.1 = ((s8[9437184]{0:T(1024)(128)(4,1)}), s8[4194304]{0:T(1024)(128)(4,1)S(1)}, s32[]{:S(2)}) async-start(s8[9437184]{0:T(1024)(128)(4,1)} %bitcast.32), calls=%async_computation.2 | async-start | bytes 8388608
  70.2 22.3 %slice-start.2 = ((s8[9437184]{0:T(1024)(128)(4,1)}), s8[1048576]{0:T(1024)(128)(4,1)S(1)}, s32[]{:S(2)}) async-start(s8[9437184]{0:T(1024)(128)(4,1)} %bitcast.32), calls=%async_computation.3 | async-start | bytes 2097152
  79.3 11.2 %collective-permute-start.9 = (bf16[48,4608]{1,0:T(8,128)(2,1)S(1)}, bf16[48,4608]{1,0:T(8,128)(2,1)S(1)}, u32[]{:S(2)}, u32[]{:S(2)}) collective-permute-start(bf16[48,4608]{1,0:T(8,128)(2,1)S(1)} %collective-permute-done.7), channel_id=1, source_target_pairs={{0,8},{1,9},{2,10},{3,11},{4,12},{5,13},{6,14},{7,15},{8,0},{9,1},... | collective-permute-start | bytes 1327112 | tf_op jit(solution)/shard_map/ppermute | solution.py:44
  90.0 1.8 %collective-permute-start.12 = (bf16[48,4608]{1,0:T(8,128)(2,1)S(1)}, bf16[48,4608]{1,0:T(8,128)(2,1)S(1)}, u32[]{:S(2)}, u32[]{:S(2)}) collective-permute-start(bf16[48,4608]{1,0:T(8,128)(2,1)S(1)} %collective-permute-done.10), channel_id=1, source_target_pairs={{0,8},{1,9},{2,10},{3,11},{4,12},{5,13},{6,14},{7,15},{8,0},{9,1},... | collective-permute-start | bytes 1327112 | tf_op jit(solution)/shard_map/ppermute | solution.py:44
  90.0 2.4 %collective-permute-start.13 = (bf16[48,4608]{1,0:T(8,128)(2,1)S(1)}, bf16[48,4608]{1,0:T(8,128)(2,1)S(1)}, u32[]{:S(2)}, u32[]{:S(2)}) collective-permute-start(bf16[48,4608]{1,0:T(8,128)(2,1)S(1)} %collective-permute-done.11), channel_id=1, source_target_pairs={{0,8},{1,9},{2,10},{3,11},{4,12},{5,13},{6,14},{7,15},{8,0},{9,1},... | collective-permute-start | bytes 1327112 | tf_op jit(solution)/shard_map/ppermute | solution.py:44
  116.1 3.4 %collective-permute-start.27 = (bf16[192,1792]{1,0:T(8,128)(2,1)S(1)}, bf16[192,1792]{1,0:T(8,128)(2,1)S(1)}, u32[]{:S(2)}, u32[]{:S(2)}) collective-permute-start(bf16[192,1792]{1,0:T(8,128)(2,1)S(1)} %fusion.8), channel_id=1, source_target_pairs={{0,8},{1,9},{2,10},{3,11},{4,12},{5,13},{6,14},{7,15},{8,0},{9,1},... | collective-permute-start | bytes 2064392 | tf_op jit(solution)/shard_map/ppermute | solution.py:44
  117.9 7.2 %collective-permute-start.31 = (bf16[192,1792]{1,0:T(8,128)(2,1)S(1)}, bf16[192,1792]{1,0:T(8,128)(2,1)S(1)}, u32[]{:S(2)}, u32[]{:S(2)}) collective-permute-start(bf16[192,1792]{1,0:T(8,128)(2,1)S(1)} %fusion.11), channel_id=1, source_target_pairs={{0,8},{1,9},{2,10},{3,11},{4,12},{5,13},{6,14},{7,15},{8,0},{9,1},... | collective-permute-start | bytes 2064392 | tf_op jit(solution)/shard_map/ppermute | solution.py:44
  120.1 9.3 %copy-start.2 = (f32[3584]{0:T(1024)S(1)}, f32[3584]{0:T(1024)}, u32[]{:S(2)}) copy-start(f32[3584]{0:T(1024)} %param.16) | copy-start | bytes 43012
  120.1 36.4 %copy-start = (bf16[16,3584]{1,0:T(8,128)(2,1)S(1)}, bf16[16,3584]{1,0:T(8,128)(2,1)}, u32[]{:S(2)}) copy-start(bf16[16,3584]{1,0:T(8,128)(2,1)} %refs_3_.1) | copy-start | bytes 344068
  120.1 8.3 %collective-permute-start.28 = (bf16[48,1792]{1,0:T(8,128)(2,1)S(1)}, bf16[48,1792]{1,0:T(8,128)(2,1)S(1)}, u32[]{:S(2)}, u32[]{:S(2)}) collective-permute-start(bf16[48,1792]{1,0:T(8,128)(2,1)S(1)} %get-tuple-element.32), channel_id=1, source_target_pairs={{0,1},{1,0},{2,3},{3,2},{4,5},{5,4},{6,7},{7,6},{8,9},{9,8},{10,11... | collective-permute-start | bytes 516104 | tf_op jit(solution)/shard_map/ppermute | solution.py:44
  123.6 11.1 %collective-permute-start.29 = (bf16[48,1792]{1,0:T(8,128)(2,1)S(1)}, bf16[48,1792]{1,0:T(8,128)(2,1)S(1)}, u32[]{:S(2)}, u32[]{:S(2)}) collective-permute-start(bf16[48,1792]{1,0:T(8,128)(2,1)S(1)} %get-tuple-element.33), channel_id=1, source_target_pairs={{0,16},{1,17},{2,18},{3,19},{4,20},{5,21},{6,22},{7,23},{8,24},{9,... | collective-permute-start | bytes 516104 | tf_op jit(solution)/shard_map/ppermute | solution.py:44
  124.2 10.5 %collective-permute-start.30 = (bf16[48,1792]{1,0:T(8,128)(2,1)S(1)}, bf16[48,1792]{1,0:T(8,128)(2,1)S(1)}, u32[]{:S(2)}, u32[]{:S(2)}) collective-permute-start(bf16[48,1792]{1,0:T(8,128)(2,1)S(1)} %get-tuple-element.34), channel_id=1, source_target_pairs={{0,17},{1,16},{2,19},{3,18},{4,21},{5,20},{6,23},{7,22},{8,25},{9,... | collective-permute-start | bytes 516104 | tf_op jit(solution)/shard_map/ppermute | solution.py:44
  125.8 10.2 %collective-permute-start.32 = (bf16[48,1792]{1,0:T(8,128)(2,1)S(1)}, bf16[48,1792]{1,0:T(8,128)(2,1)S(1)}, u32[]{:S(2)}, u32[]{:S(2)}) collective-permute-start(bf16[48,1792]{1,0:T(8,128)(2,1)S(1)} %get-tuple-element.36), channel_id=1, source_target_pairs={{0,1},{1,0},{2,3},{3,2},{4,5},{5,4},{6,7},{7,6},{8,9},{9,8},{10,11... | collective-permute-start | bytes 516104 | tf_op jit(solution)/shard_map/ppermute | solution.py:44
  127.8 13.0 %collective-permute-start.33 = (bf16[48,1792]{1,0:T(8,128)(2,1)S(1)}, bf16[48,1792]{1,0:T(8,128)(2,1)S(1)}, u32[]{:S(2)}, u32[]{:S(2)}) collective-permute-start(bf16[48,1792]{1,0:T(8,128)(2,1)S(1)} %get-tuple-element.37), channel_id=1, source_target_pairs={{0,16},{1,17},{2,18},{3,19},{4,20},{5,21},{6,22},{7,23},{8,24},{9,... | collective-permute-start | bytes 516104 | tf_op jit(solution)/shard_map/ppermute | solution.py:44
  128.4 12.4 %collective-permute-start.34 = (bf16[48,1792]{1,0:T(8,128)(2,1)S(1)}, bf16[48,1792]{1,0:T(8,128)(2,1)S(1)}, u32[]{:S(2)}, u32[]{:S(2)}) collective-permute-start(bf16[48,1792]{1,0:T(8,128)(2,1)S(1)} %get-tuple-element.38), channel_id=1, source_target_pairs={{0,17},{1,16},{2,19},{3,18},{4,21},{5,20},{6,23},{7,22},{8,25},{9,... | collective-permute-start | bytes 516104 | tf_op jit(solution)/shard_map/ppermute | solution.py:44
  141.5 7.8 %collective-permute-start.35 = (bf16[16,3584]{1,0:T(8,128)(2,1)S(1)}, bf16[16,3584]{1,0:T(8,128)(2,1)S(1)}, u32[]{:S(2)}, u32[]{:S(2)}) collective-permute-start(bf16[16,3584]{1,0:T(8,128)(2,1)S(1)} %get-tuple-element.40), channel_id=1, source_target_pairs={{0,2},{1,3},{2,0},{3,1},{6,4},{7,5},{8,10},{9,11},{10,8},{11,9},{1... | collective-permute-start | bytes 344072 | tf_op jit(solution)/shard_map/ppermute | solution.py:44
  143.8 12.7 %collective-permute-start.36 = (bf16[16,3584]{1,0:T(8,128)(2,1)S(1)}, bf16[16,3584]{1,0:T(8,128)(2,1)S(1)}, u32[]{:S(2)}, u32[]{:S(2)}) collective-permute-start(bf16[16,3584]{1,0:T(8,128)(2,1)S(1)} %get-tuple-element.41), channel_id=1, source_target_pairs={{0,4},{1,5},{4,0},{5,1},{6,2},{7,3},{8,12},{9,13},{12,8},{13,9},{1... | collective-permute-start | bytes 344072 | tf_op jit(solution)/shard_map/ppermute | solution.py:44
  145.7 10.7 %collective-permute-start.37 = (bf16[16,3584]{1,0:T(8,128)(2,1)S(1)}, bf16[16,3584]{1,0:T(8,128)(2,1)S(1)}, u32[]{:S(2)}, u32[]{:S(2)}) collective-permute-start(bf16[16,3584]{1,0:T(8,128)(2,1)S(1)} %get-tuple-element.42), channel_id=1, source_target_pairs={{2,4},{3,5},{4,2},{5,3},{6,0},{7,1},{10,12},{11,13},{12,10},{13,11... | collective-permute-start | bytes 344072 | tf_op jit(solution)/shard_map/ppermute | solution.py:44

commit v4 on v3

--- a/solution.py
+++ b/solution.py
@@ -83,15 +83,17 @@
     )(ids, *args, *far)
 
 
-def pick_kernel(live, ids, *refs):
-    pieces, out = refs[:-1], refs[-1]
-    share = pieces[0].shape[0]
+def pick_kernel(live, count, ids, *refs):
+    pieces, outs = refs[:-count], refs[-count:]
+    share, width = pieces[0].shape[0], outs[0].shape[1]
     for j in range(live):
         for k, piece in enumerate(pieces):
 
             @pl.when((ids[2] ^ j) == k)
             def _(j=j, piece=piece):
-                out[j * share : (j + 1) * share, :] = piece[...]
+                for part, out in enumerate(outs):
+                    there = slice(part * width, (part + 1) * width)
+                    out[j * share : (j + 1) * share, :] = piece[:, there]
 
 
 def pair_kernel(live, ids, kept, other, own, *lows):
@@ -115,18 +117,20 @@
     out[...] = norm_rows(final, final_gain[...])[0].astype(BF16)
 
 
-def gather_depth(grid, rows):
+def gather_depth(grid, rows, count):
+    share, width = rows.shape[0], rows.shape[1] // count
     pieces = [rows] + grid.send_depth([rows] * (grid.depth - 1), source=grid.live)
     if not grid.tiled:
-        return jnp.concatenate([pick(pieces, grid.z ^ j) for j in range(grid.live)], axis=0)
+        whole = [pick(pieces, grid.z ^ j) for j in range(grid.live)]
+        return jnp.split(jnp.concatenate(whole, axis=0), count, axis=1)
     return call(
-        functools.partial(pick_kernel, grid.live),
+        functools.partial(pick_kernel, grid.live, count),
         grid.ids,
         pieces,
-        [shape_of((grid.live * rows.shape[0], rows.shape[1]), rows.dtype)],
+        [shape_of((grid.live * share, width), rows.dtype)] * count,
         [],
         4,
-    )[0]
+    )
 
 
 def gather_plane(grid, own):
@@ -432,7 +436,7 @@
 
     student_f = student_hidden.astype(F32)
     student_norm = norm_rows(student_f, student_gain)[0].astype(BF16)
-    own_s = gather_depth(grid, student_norm)
+    own_s = gather_depth(grid, student_norm, 1)[0]
     whole_s = gather_plane(grid, own_s)
 
     ints = jnp.concatenate([labels, lengths[0]])[None]
@@ -481,8 +485,8 @@
         post, _ = norm_rows(mlp_sum, post_gain)
         final = teacher_residual.astype(F32) + post
         teacher_norm = norm_rows(final, final_gain)[0].astype(BF16)
-    own_t = gather_depth(grid, teacher_norm)
-    whole_t = gather_plane(grid, own_t)
+    own_t = gather_depth(grid, teacher_norm, PARTS)
+    whole_t = [gather_plane(grid, part) for part in own_t]
 
     vocab_dev = student_head.shape[1]
 
@@ -490,7 +494,14 @@
     s_cols = call(
         student_kernel, grid.ids, [s_logits, label_column], [shape_of((rows, 128), F32)], [], 4
     )[0]
-    t_logits = jnp.dot(whole_t, teacher_head, preferred_element_type=F32)
+    t_logits = 0.0
+    for i, part in enumerate(whole_t):
+        width = part.shape[1]
+        t_logits = t_logits + jnp.dot(
+            part, teacher_head[i * width : (i + 1) * width], preferred_element_type=F32
+        )
+        if i < PARTS - 1:
+            t_logits = lax.optimization_barrier(t_logits)
     devices = 4 * grid.tp
     sent = call(
         teacher_kernel,

time: 159 us -> 157 us (0.987)
  waiting for transfers between devices: 57.4 us -> 50 us
  starting transfers between devices: 51.5 us -> 57.2 us
    ppermute x38 -> x45, waiting for transfers between devices: 57.4 us -> 50 us  [send(): return lax.ppermute(value, AXES, pairs)]
    ppermute x38 -> x45, starting transfers between devices: 51.5 us -> 57.2 us  [send(): return lax.ppermute(value, AXES, pairs)]
    dot_general x1 -> x2, matrix products: 3.8 us -> 3.97 us  [shards(): jnp.dot(part, teacher_head[i * width:(i + 1) * width], preferred_element_...]
  transfers between devices with their start and end apart: 38 -> 45, of which waited for: 16 -> 16; matrix products, arithmetic and copies ran while one was open for 7% -> 8% of each run, Pallas kernels for 5% -> 5%
where the time goes in v4:
time: 157 us; the launch traced here: 156 us
  starting transfers between devices  57.2 us (36%)
  waiting for transfers between devices  50 us (32%)
  blocking collectives  16.4 us (10%)
  Pallas kernels  13.6 us (9%)
  matrix products  12.4 us (8%)
  other arithmetic  3.03 us (2%)
  local copies, waits for them, and re-layouts  2.34 us (1%)
    ppermute x45, starting transfers between devices, send(): return lax.ppermute(value, AXES, pairs)  57.2 us
    ppermute x45, waiting for transfers between devices, send(): return lax.ppermute(value, AXES, pairs)  50 us
    all_to_all x1, blocking collectives, shards(): got = lax.all_to_all(sent, AXES, 0, 0, tiled=True)  16.4 us
    pallas_call x13, Pallas kernels, call(): pl.pallas_call(kernel, out_shape=outs, in_specs=[SMEM] + [VMEM] * len(arg...  13.6 us
    dot_general x4, matrix products, product(): lax.dot_general(grads, head[part * width:(part + 1) * width], (((1,), (1,...  5.43 us
    dot_general x2, matrix products, shards(): jnp.dot(part, teacher_head[i * width:(i + 1) * width], preferred_element_...  3.97 us
  transfers between devices with their start and end apart: 45, of which 16 were waited for; matrix products, arithmetic and copies ran while one was open for 8% of the time, Pallas kernels for 5%

profile of v4, /device:TPU:0, one launch (start us, length us, event | category | flops | bytes accessed | tf_op | source)
XLA Modules:
  0.0 156.4 jit_solution(13445985903494951799)
XLA Ops:
  0.6 1.1 fusion.18
  1.7 1.0 fusion.20.refs_0_
  2.7 5.0 %collective-permute-start.21 = (bf16[16,3584]{1,0:T(8,128)(2,1)S(1)}, bf16[16,3584]{1,0:T(8,128)(2,1)S(1)}, u32[]{:S(2)}, u32[]{:S(2)}) collective-permute-start(bf16[16,3584]{1,0:T(8,128)(2,1)S(1)} %fusion.20.refs_0_), channel_id=1, source_target_pairs={{0,2},{1,3},{2,0},{3,1},{4,6},{5,7},{8,10},{9,11},{10,8},{11,9},{1... | collective-permute-start | bytes 344072 | tf_op jit(solution)/shard_map/ppermute | solution.py:44
  7.7 4.5 %collective-permute-start.22 = (bf16[16,3584]{1,0:T(8,128)(2,1)S(1)}, bf16[16,3584]{1,0:T(8,128)(2,1)S(1)}, u32[]{:S(2)}, u32[]{:S(2)}) collective-permute-start(bf16[16,3584]{1,0:T(8,128)(2,1)S(1)} %fusion.20.refs_0_), channel_id=1, source_target_pairs={{0,4},{1,5},{2,6},{3,7},{4,0},{5,1},{8,12},{9,13},{10,14},{11,15},... | collective-permute-start | bytes 344072 | tf_op jit(solution)/shard_map/ppermute | solution.py:44
  12.2 1.3 collective-permute-start.23
  13.5 0.7 pad_add_fusion
  14.2 1.6 %collective-permute-start.32 = (s32[1,136]{1,0:T(1,128)S(1)}, s32[1,136]{1,0:T(1,128)S(1)}, u32[]{:S(2)}, u32[]{:S(2)}) collective-permute-start(s32[1,136]{1,0:T(1,128)S(1)} %bitcast.27), channel_id=1, source_target_pairs={{0,16},{1,17},{2,18},{3,19},{4,20},{5,21},{6,22},{7,23},{8,24},{9,... | collective-permute-start | bytes 1640 | tf_op jit(solution)/shard_map/ppermute | solution.py:44
  15.8 1.2 dynamic-slice_bitcast_fusion
  17.8 1.5 collective-permute-start
  19.3 0.9 collective-permute-done.33.refs_3_
  20.2 1.1 shard_map.117
  21.3 0.7 shard_map.116
  22.0 1.6 collective-permute-start.24
  24.1 6.8 %collective-permute-done.other = bf16[3,16,4608]{2,1,0:T(8,128)(2,1)S(1)} collective-permute-done((bf16[3,16,4608]{2,1,0:T(8,128)(2,1)S(1)}, bf16[3,16,4608]{2,1,0:T(8,128)(2,1)S(1)}, u32[]{:S(2)}, u32[]{:S(2)}) %collective-permute-start) | collective-permute-done | bytes 442400 | tf_op jit(solution)/shard_map/ppermute | solution.py:44
  30.9 0.7 shard_map.113
  31.6 3.4 %collective-permute-start.1 = (bf16[16,4608]{1,0:T(8,128)(2,1)S(1)}, bf16[16,4608]{1,0:T(8,128)(2,1)S(1)}, u32[]{:S(2)}, u32[]{:S(2)}) collective-permute-start(bf16[16,4608]{1,0:T(8,128)(2,1)S(1)} %get-tuple-element.26), channel_id=1, source_target_pairs={{0,2},{1,3},{2,0},{3,1},{6,4},{7,5},{8,10},{9,11},{10,8},{11,9},{1... | collective-permute-start | bytes 442376 | tf_op jit(solution)/shard_map/ppermute | solution.py:44
  35.0 1.9 %collective-permute-start.2 = (bf16[16,4608]{1,0:T(8,128)(2,1)S(1)}, bf16[16,4608]{1,0:T(8,128)(2,1)S(1)}, u32[]{:S(2)}, u32[]{:S(2)}) collective-permute-start(bf16[16,4608]{1,0:T(8,128)(2,1)S(1)} %get-tuple-element.27), channel_id=1, source_target_pairs={{0,4},{1,5},{4,0},{5,1},{6,2},{7,3},{8,12},{9,13},{12,8},{13,9},{1... | collective-permute-start | bytes 442376 | tf_op jit(solution)/shard_map/ppermute | solution.py:44
  37.3 1.3 collective-permute-start.3
  38.8 2.4 %collective-permute-start.28 = (bf16[48,3584]{1,0:T(8,128)(2,1)S(1)}, bf16[48,3584]{1,0:T(8,128)(2,1)S(1)}, u32[]{:S(2)}, u32[]{:S(2)}) collective-permute-start(bf16[48,3584]{1,0:T(8,128)(2,1)S(1)} %shard_map.116), channel_id=1, source_target_pairs={{0,17},{1,16},{2,19},{3,18},{4,21},{5,20},{6,23},{7,22},{8,25},{9,... | collective-permute-start | bytes 1032200 | tf_op jit(solution)/shard_map/ppermute | solution.py:44
  41.3 7.9 %collective-permute-done.2.refs_2_ = bf16[16,4608]{1,0:T(8,128)(2,1)S(1)} collective-permute-done((bf16[16,4608]{1,0:T(8,128)(2,1)S(1)}, bf16[16,4608]{1,0:T(8,128)(2,1)S(1)}, u32[]{:S(2)}, u32[]{:S(2)}) %collective-permute-start.2) | collective-permute-done | bytes 147488 | tf_op jit(solution)/shard_map/ppermute | solution.py:44
  49.2 0.8 shard_map.114.refs_0_
  50.1 4.3 %collective-permute-start.4 = (bf16[16,4608]{1,0:T(8,128)(2,1)S(1)}, bf16[16,4608]{1,0:T(8,128)(2,1)S(1)}, u32[]{:S(2)}, u32[]{:S(2)}) collective-permute-start(bf16[16,4608]{1,0:T(8,128)(2,1)S(1)} %shard_map.114.refs_0_), channel_id=1, source_target_pairs={{0,2},{1,3},{2,0},{3,1},{4,6},{5,7},{8,10},{9,11},{10,8},{11,9},{1... | collective-permute-start | bytes 442376 | tf_op jit(solution)/shard_map/ppermute | solution.py:44
  54.3 1.9 %collective-permute-start.5 = (bf16[16,4608]{1,0:T(8,128)(2,1)S(1)}, bf16[16,4608]{1,0:T(8,128)(2,1)S(1)}, u32[]{:S(2)}, u32[]{:S(2)}) collective-permute-start(bf16[16,4608]{1,0:T(8,128)(2,1)S(1)} %shard_map.114.refs_0_), channel_id=1, source_target_pairs={{0,4},{1,5},{2,6},{3,7},{4,0},{5,1},{8,12},{9,13},{10,14},{11,15},... | collective-permute-start | bytes 442376 | tf_op jit(solution)/shard_map/ppermute | solution.py:44
  56.3 1.3 collective-permute-start.6
  58.6 4.7 %collective-permute-done.5.refs_2_ = bf16[16,4608]{1,0:T(8,128)(2,1)S(1)} collective-permute-done((bf16[16,4608]{1,0:T(8,128)(2,1)S(1)}, bf16[16,4608]{1,0:T(8,128)(2,1)S(1)}, u32[]{:S(2)}, u32[]{:S(2)}) %collective-permute-start.5) | collective-permute-done | bytes 147488 | tf_op jit(solution)/shard_map/ppermute | solution.py:44
  63.3 0.7 shard_map.115
  64.0 1.6 collective-permute-start.14
  65.6 1.6 %collective-permute-start.17 = (bf16[48,2304]{1,0:T(8,128)(2,1)S(1)}, bf16[48,2304]{1,0:T(8,128)(2,1)S(1)}, u32[]{:S(2)}, u32[]{:S(2)}) collective-permute-start(bf16[48,2304]{1,0:T(8,128)(2,1)S(1)} %get-tuple-element.30), channel_id=1, source_target_pairs={{0,16},{1,17},{2,18},{3,19},{4,20},{5,21},{6,22},{7,23},{8,24},{9,... | collective-permute-start | bytes 663560 | tf_op jit(solution)/shard_map/ppermute | solution.py:44
  67.8 1.6 collective-permute-start.7
  69.5 3.0 %fusion.21.logits.s_logits = f32[384,1024]{1,0:T(8,128)S(1)} fusion(bf16[384,3584]{1,0:T(8,128)(2,1)S(1)} %constant_dynamic-update-slice_fusion.16, bf16[3584,1024]{1,0:T(8,128)(2,1)S(1)} %copy-done.5), kind=kOutput, calls=%fused_computation.48 | convolution fusion | flops 2818572288 | bytes 11665408 | tf_op jit(solution)/shard_map/dot_general | solution.py:493
  72.5 2.3 %shard_map.118.s_cols = f32[384,128]{1,0:T(8,128)S(1)} custom-call(s32[5]{0:T(128)S(1)} %stack.23.ids, f32[384,1024]{1,0:T(8,128)S(1)} %fusion.21.logits.s_logits, s32[384,1]{1,0:T(8,128)S(1)} %get-tuple-element.31.labels), custom_call_target="tpu_custom_call" | custom-call | tf_op jit(solution)/shard_map/pallas_call | solution.py:76
  74.9 1.6 %collective-permute-start.10 = (bf16[48,2304]{1,0:T(8,128)(2,1)S(1)}, bf16[48,2304]{1,0:T(8,128)(2,1)S(1)}, u32[]{:S(2)}, u32[]{:S(2)}) collective-permute-start(bf16[48,2304]{1,0:T(8,128)(2,1)S(1)} %get-tuple-element.29), channel_id=1, source_target_pairs={{0,16},{1,17},{2,18},{3,19},{4,20},{5,21},{6,22},{7,23},{8,24},{9,... | collective-permute-start | bytes 663560 | tf_op jit(solution)/shard_map/ppermute | solution.py:44
  76.5 3.1 %collective-permute-done.7 = bf16[48,2304]{1,0:T(8,128)(2,1)S(1)} collective-permute-done((bf16[48,2304]{1,0:T(8,128)(2,1)S(1)}, bf16[48,2304]{1,0:T(8,128)(2,1)S(1)}, u32[]{:S(2)}, u32[]{:S(2)}) %collective-permute-start.7) | collective-permute-done | bytes 221216 | tf_op jit(solution)/shard_map/ppermute | solution.py:44
  79.6 2.3 %collective-permute-start.11 = (bf16[48,2304]{1,0:T(8,128)(2,1)S(1)}, bf16[48,2304]{1,0:T(8,128)(2,1)S(1)}, u32[]{:S(2)}, u32[]{:S(2)}) collective-permute-start(bf16[48,2304]{1,0:T(8,128)(2,1)S(1)} %get-tuple-element.29), channel_id=1, source_target_pairs={{0,17},{1,16},{2,19},{3,18},{4,21},{5,20},{6,23},{7,22},{8,25},{9,... | collective-permute-start | bytes 663560 | tf_op jit(solution)/shard_map/ppermute | solution.py:44
  82.1 0.6 collective-permute-start.9
  82.7 5.0 %collective-permute-done.10 = bf16[48,2304]{1,0:T(8,128)(2,1)S(1)} collective-permute-done((bf16[48,2304]{1,0:T(8,128)(2,1)S(1)}, bf16[48,2304]{1,0:T(8,128)(2,1)S(1)}, u32[]{:S(2)}, u32[]{:S(2)}) %collective-permute-start.10) | collective-permute-done | bytes 221216 | tf_op jit(solution)/shard_map/ppermute | solution.py:44
  88.4 0.8 collective-permute-done.20
  89.2 2.0 %fusion = f32[384,1024]{1,0:T(8,128)S(1)} fusion(bf16[384,2304]{1,0:T(8,128)(2,1)S(1)} %constant_dynamic-update-slice_fusion.8, bf16[4608,1024]{1,0:T(8,128)(2,1)S(1)} %bitcast.33), kind=kOutput, calls=%fused_computation | convolution fusion | flops 1811939328 | bytes 8060928 | tf_op jit(solution)/shard_map/dot_general | solution.py:500
  91.4 2.0 %fusion.2 = f32[384,1024]{1,0:T(8,128)S(1)} fusion(bf16[384,2304]{1,0:T(8,128)(2,1)S(1)} %constant_dynamic-update-slice_fusion, bf16[4608,1024]{1,0:T(8,128)(2,1)S(1)} %bitcast.33), kind=kOutput, calls=%fused_computation.2 | convolution fusion | flops 1811939328 | bytes 8060928 | tf_op jit(solution)/shard_map/dot_general | solution.py:500
  93.7 1.5 shard_map.119
  95.1 16.4 %all_to_all.5.got = f32[32,1,1536]{2,1,0:T(1,128)S(1)} all-to-all(f32[32,1,1536]{2,1,0:T(1,128)S(1)} %shard_map.119), channel_id=1, replica_groups=mesh['dp'=4,'tp'=8] {'dp','tp'}, dimensions={0} | all-to-all | bytes 393216 | tf_op jit(solution)/shard_map/all_to_all | solution.py:514
  111.6 1.6 %shard_map.120 = (bf16[192,1024]{1,0:T(8,128)(2,1)S(1)}, bf16[192,1024]{1,0:T(8,128)(2,1)S(1)}) custom-call(s32[5]{0:T(128)S(1)} %stack.23.ids, f32[32,1,1536]{2,1,0:T(1,128)S(1)} %all_to_all.5.got, s32[384,1]{1,0:T(8,128)S(1)} %get-tuple-element.31.labels, f32[384,1]{1,0:T(8,128)S(1)} %get-tuple-element.32.scale, f32[384,1024]{1,0:T(8,128)S(1)} %add.35.logits.t_logits, ...), custom_call_target="tpu_custom_call" | custom-call | tf_op jit(solution)/shard_map/pallas_call | solution.py:76
  113.2 1.4 fusion.15
  115.0 1.4 fusion.12
  116.6 1.4 fusion.6.kept
  117.9 0.7 shard_map.122
  118.6 2.1 %collective-permute-start.39 = (bf16[48,1792]{1,0:T(8,128)(2,1)S(1)}, bf16[48,1792]{1,0:T(8,128)(2,1)S(1)}, u32[]{:S(2)}, u32[]{:S(2)}) collective-permute-start(bf16[48,1792]{1,0:T(8,128)(2,1)S(1)} %get-tuple-element.40), channel_id=1, source_target_pairs={{0,1},{1,0},{2,3},{3,2},{4,5},{5,4},{6,7},{7,6},{8,9},{9,8},{10,11... | collective-permute-start | bytes 516104 | tf_op jit(solution)/shard_map/ppermute | solution.py:44
  120.7 1.4 fusion.10.kept
  122.0 0.6 collective-permute-start.40
  122.6 0.9 collective-permute-start.41
  123.6 0.7 shard_map.121
  124.2 2.1 %collective-permute-start.35 = (bf16[48,1792]{1,0:T(8,128)(2,1)S(1)}, bf16[48,1792]{1,0:T(8,128)(2,1)S(1)}, u32[]{:S(2)}, u32[]{:S(2)}) collective-permute-start(bf16[48,1792]{1,0:T(8,128)(2,1)S(1)} %get-tuple-element.36), channel_id=1, source_target_pairs={{0,1},{1,0},{2,3},{3,2},{4,5},{5,4},{6,7},{7,6},{8,9},{9,8},{10,11... | collective-permute-start | bytes 516104 | tf_op jit(solution)/shard_map/ppermute | solution.py:44
  126.9 1.0 collective-permute-start.37
  127.9 0.7 shard_map.125
  128.6 4.6 %collective-permute-done.40.refs_6_ = bf16[48,1792]{1,0:T(8,128)(2,1)S(1)} collective-permute-done((bf16[48,1792]{1,0:T(8,128)(2,1)S(1)}, bf16[48,1792]{1,0:T(8,128)(2,1)S(1)}, u32[]{:S(2)}, u32[]{:S(2)}) %collective-permute-start.40) | collective-permute-done | bytes 172064 | tf_op jit(solution)/shard_map/ppermute | solution.py:44
  133.2 1.3 collective-permute-done.35.refs_1_
  134.5 4.8 %collective-permute-done.36.refs_2_ = bf16[48,1792]{1,0:T(8,128)(2,1)S(1)} collective-permute-done((bf16[48,1792]{1,0:T(8,128)(2,1)S(1)}, bf16[48,1792]{1,0:T(8,128)(2,1)S(1)}, u32[]{:S(2)}, u32[]{:S(2)}) %collective-permute-start.36) | collective-permute-done | bytes 172064 | tf_op jit(solution)/shard_map/ppermute | solution.py:44
  139.3 0.7 shard_map.123
  140.0 2.3 %collective-permute-start.42 = (bf16[16,3584]{1,0:T(8,128)(2,1)S(1)}, bf16[16,3584]{1,0:T(8,128)(2,1)S(1)}, u32[]{:S(2)}, u32[]{:S(2)}) collective-permute-start(bf16[16,3584]{1,0:T(8,128)(2,1)S(1)} %get-tuple-element.44), channel_id=1, source_target_pairs={{0,2},{1,3},{2,0},{3,1},{6,4},{7,5},{8,10},{9,11},{10,8},{11,9},{1... | collective-permute-start | bytes 344072 | tf_op jit(solution)/shard_map/ppermute | solution.py:44
  142.3 1.9 %collective-permute-start.43 = (bf16[16,3584]{1,0:T(8,128)(2,1)S(1)}, bf16[16,3584]{1,0:T(8,128)(2,1)S(1)}, u32[]{:S(2)}, u32[]{:S(2)}) collective-permute-start(bf16[16,3584]{1,0:T(8,128)(2,1)S(1)} %get-tuple-element.45), channel_id=1, source_target_pairs={{0,4},{1,5},{4,0},{5,1},{6,2},{7,3},{8,12},{9,13},{12,8},{13,9},{1... | collective-permute-start | bytes 344072 | tf_op jit(solution)/shard_map/ppermute | solution.py:44
  144.2 1.3 collective-permute-start.44
  146.0 1.8 %collective-permute-done.42.refs_0_ = bf16[16,3584]{1,0:T(8,128)(2,1)S(1)} collective-permute-done((bf16[16,3584]{1,0:T(8,128)(2,1)S(1)}, bf16[16,3584]{1,0:T(8,128)(2,1)S(1)}, u32[]{:S(2)}, u32[]{:S(2)}) %collective-permute-start.42) | collective-permute-done | bytes 114720 | tf_op jit(solution)/shard_map/ppermute | solution.py:44
  147.9 7.1 %collective-permute-done.43.refs_1_ = bf16[16,3584]{1,0:T(8,128)(2,1)S(1)} collective-permute-done((bf16[16,3584]{1,0:T(8,128)(2,1)S(1)}, bf16[16,3584]{1,0:T(8,128)(2,1)S(1)}, u32[]{:S(2)}, u32[]{:S(2)}) %collective-permute-start.43) | collective-permute-done | bytes 114720 | tf_op jit(solution)/shard_map/ppermute | solution.py:44
  155.0 1.4 shard_map.124
  (100 shorter events, 6.7 us)
Async XLA Ops:
  0.6 16.4 %copy-start.3 = (f32[4608]{0:T(1024)S(1)}, f32[4608]{0:T(1024)}, u32[]{:S(2)}) copy-start(f32[4608]{0:T(1024)} %param.12) | copy-start | bytes 55300
  0.6 16.4 %copy-start.4 = (f32[4608]{0:T(1024)S(1)}, f32[4608]{0:T(1024)}, u32[]{:S(2)}) copy-start(f32[4608]{0:T(1024)} %param.13) | copy-start | bytes 55300
  2.7 18.6 %collective-permute-start.21 = (bf16[16,3584]{1,0:T(8,128)(2,1)S(1)}, bf16[16,3584]{1,0:T(8,128)(2,1)S(1)}, u32[]{:S(2)}, u32[]{:S(2)}) collective-permute-start(bf16[16,3584]{1,0:T(8,128)(2,1)S(1)} %fusion.20.refs_0_), channel_id=1, source_target_pairs={{0,2},{1,3},{2,0},{3,1},{4,6},{5,7},{8,10},{9,11},{10,8},{11,9},{1... | collective-permute-start | bytes 344072 | tf_op jit(solution)/shard_map/ppermute | solution.py:44
  7.7 13.6 %collective-permute-start.22 = (bf16[16,3584]{1,0:T(8,128)(2,1)S(1)}, bf16[16,3584]{1,0:T(8,128)(2,1)S(1)}, u32[]{:S(2)}, u32[]{:S(2)}) collective-permute-start(bf16[16,3584]{1,0:T(8,128)(2,1)S(1)} %fusion.20.refs_0_), channel_id=1, source_target_pairs={{0,4},{1,5},{2,6},{3,7},{4,0},{5,1},{8,12},{9,13},{10,14},{11,15},... | collective-permute-start | bytes 344072 | tf_op jit(solution)/shard_map/ppermute | solution.py:44
  12.2 9.1 %collective-permute-start.23 = (bf16[16,3584]{1,0:T(8,128)(2,1)S(1)}, bf16[16,3584]{1,0:T(8,128)(2,1)S(1)}, u32[]{:S(2)}, u32[]{:S(2)}) collective-permute-start(bf16[16,3584]{1,0:T(8,128)(2,1)S(1)} %fusion.20.refs_0_), channel_id=1, source_target_pairs={{0,6},{1,7},{2,4},{3,5},{4,2},{5,3},{8,14},{9,15},{10,12},{11,13},... | collective-permute-start | bytes 344072 | tf_op jit(solution)/shard_map/ppermute | solution.py:44
  14.2 2.9 %collective-permute-start.31 = (s32[1,136]{1,0:T(1,128)S(1)}, s32[1,136]{1,0:T(1,128)S(1)}, u32[]{:S(2)}, u32[]{:S(2)}) collective-permute-start(s32[1,136]{1,0:T(1,128)S(1)} %bitcast.26), channel_id=1, source_target_pairs={{0,8},{1,9},{2,10},{3,11},{4,12},{5,13},{6,14},{7,15},{8,0},{9,1},... | collective-permute-start | bytes 1640 | tf_op jit(solution)/shard_map/ppermute | solution.py:44
  14.2 3.6 %collective-permute-start.32 = (s32[1,136]{1,0:T(1,128)S(1)}, s32[1,136]{1,0:T(1,128)S(1)}, u32[]{:S(2)}, u32[]{:S(2)}) collective-permute-start(s32[1,136]{1,0:T(1,128)S(1)} %bitcast.27), channel_id=1, source_target_pairs={{0,16},{1,17},{2,18},{3,19},{4,20},{5,21},{6,22},{7,23},{8,24},{9,... | collective-permute-start | bytes 1640 | tf_op jit(solution)/shard_map/ppermute | solution.py:44
  17.0 32.2 %copy-start.1 = (bf16[16,4608]{1,0:T(8,128)(2,1)S(1)}, bf16[16,4608]{1,0:T(8,128)(2,1)}, u32[]{:S(2)}) copy-start(bf16[16,4608]{1,0:T(8,128)(2,1)} %refs_4_.1) | copy-start | bytes 442372
  17.1 3.1 %collective-permute-start.33 = (s32[1,136]{1,0:T(1,128)S(1)}, s32[1,136]{1,0:T(1,128)S(1)}, u32[]{:S(2)}, u32[]{:S(2)}) collective-permute-start(s32[1,136]{1,0:T(1,128)S(1)} %bitcast.28), channel_id=1, source_target_pairs={{0,24},{1,25},{2,26},{3,27},{4,28},{5,29},{6,30},{7,31},{8,16},{9,... | collective-permute-start | bytes 1640 | tf_op jit(solution)/shard_map/ppermute | solution.py:44
  17.8 13.0 %collective-permute-start = (bf16[3,16,4608]{2,1,0:T(8,128)(2,1)S(1)}, bf16[3,16,4608]{2,1,0:T(8,128)(2,1)S(1)}, u32[]{:S(2)}, u32[]{:S(2)}) collective-permute-start(bf16[3,16,4608]{2,1,0:T(8,128)(2,1)S(1)} %get-tuple-element.48), channel_id=1, source_target_pairs={{0,1},{1,0},{2,3},{3,2},{4,5},{5,4},{6,7},{7,6},{8,9},{9,8},{10,11... | collective-permute-start | bytes 1327112 | tf_op jit(solution)/shard_map/ppermute | solution.py:44
  22.0 15.3 %collective-permute-start.24 = (bf16[48,3584]{1,0:T(8,128)(2,1)S(1)}, bf16[48,3584]{1,0:T(8,128)(2,1)S(1)}, u32[]{:S(2)}, u32[]{:S(2)}) collective-permute-start(bf16[48,3584]{1,0:T(8,128)(2,1)S(1)} %shard_map.116), channel_id=1, source_target_pairs={{0,1},{1,0},{2,3},{3,2},{4,5},{5,4},{6,7},{7,6},{8,9},{9,8},{10,11... | collective-permute-start | bytes 1032200 | tf_op jit(solution)/shard_map/ppermute | solution.py:44
  23.5 32.7 %collective-permute-start.25 = (bf16[48,3584]{1,0:T(8,128)(2,1)S(1)}, bf16[48,3584]{1,0:T(8,128)(2,1)S(1)}, u32[]{:S(2)}, u32[]{:S(2)}) collective-permute-start(bf16[48,3584]{1,0:T(8,128)(2,1)S(1)} %shard_map.116), channel_id=1, source_target_pairs={{0,8},{1,9},{2,10},{3,11},{4,12},{5,13},{6,14},{7,15},{8,0},{9,1},... | collective-permute-start | bytes 1032200 | tf_op jit(solution)/shard_map/ppermute | solution.py:44
  23.6 34.1 %collective-permute-start.27 = (bf16[48,3584]{1,0:T(8,128)(2,1)S(1)}, bf16[48,3584]{1,0:T(8,128)(2,1)S(1)}, u32[]{:S(2)}, u32[]{:S(2)}) collective-permute-start(bf16[48,3584]{1,0:T(8,128)(2,1)S(1)} %shard_map.116), channel_id=1, source_target_pairs={{0,16},{1,17},{2,18},{3,19},{4,20},{5,21},{6,22},{7,23},{8,24},{9,... | collective-permute-start | bytes 1032200 | tf_op jit(solution)/shard_map/ppermute | solution.py:44
  31.6 7.3 %collective-permute-start.1 = (bf16[16,4608]{1,0:T(8,128)(2,1)S(1)}, bf16[16,4608]{1,0:T(8,128)(2,1)S(1)}, u32[]{:S(2)}, u32[]{:S(2)}) collective-permute-start(bf16[16,4608]{1,0:T(8,128)(2,1)S(1)} %get-tuple-element.26), channel_id=1, source_target_pairs={{0,2},{1,3},{2,0},{3,1},{6,4},{7,5},{8,10},{9,11},{10,8},{11,9},{1... | collective-permute-start | bytes 442376 | tf_op jit(solution)/shard_map/ppermute | solution.py:44
  35.0 14.2 %collective-permute-start.2 = (bf16[16,4608]{1,0:T(8,128)(2,1)S(1)}, bf16[16,4608]{1,0:T(8,128)(2,1)S(1)}, u32[]{:S(2)}, u32[]{:S(2)}) collective-permute-start(bf16[16,4608]{1,0:T(8,128)(2,1)S(1)} %get-tuple-element.27), channel_id=1, source_target_pairs={{0,4},{1,5},{4,0},{5,1},{6,2},{7,3},{8,12},{9,13},{12,8},{13,9},{1... | collective-permute-start | bytes 442376 | tf_op jit(solution)/shard_map/ppermute | solution.py:44
  37.3 11.9 %collective-permute-start.3 = (bf16[16,4608]{1,0:T(8,128)(2,1)S(1)}, bf16[16,4608]{1,0:T(8,128)(2,1)S(1)}, u32[]{:S(2)}, u32[]{:S(2)}) collective-permute-start(bf16[16,4608]{1,0:T(8,128)(2,1)S(1)} %get-tuple-element.28), channel_id=1, source_target_pairs={{2,4},{3,5},{4,2},{5,3},{6,0},{7,1},{10,12},{11,13},{12,10},{13,11... | collective-permute-start | bytes 442376 | tf_op jit(solution)/shard_map/ppermute | solution.py:44
  38.6 30.8 %copy-start.5 = (bf16[3584,1024]{1,0:T(8,128)(2,1)S(1)}, bf16[3584,1024]{1,0:T(8,128)(2,1)}, u32[]{:S(2)}) copy-start(bf16[3584,1024]{1,0:T(8,128)(2,1)} %param.17) | copy-start | bytes 22020100
  38.8 18.9 %collective-permute-start.28 = (bf16[48,3584]{1,0:T(8,128)(2,1)S(1)}, bf16[48,3584]{1,0:T(8,128)(2,1)S(1)}, u32[]{:S(2)}, u32[]{:S(2)}) collective-permute-start(bf16[48,3584]{1,0:T(8,128)(2,1)S(1)} %shard_map.116), channel_id=1, source_target_pairs={{0,17},{1,16},{2,19},{3,18},{4,21},{5,20},{6,23},{7,22},{8,25},{9,... | collective-permute-start | bytes 1032200 | tf_op jit(solution)/shard_map/ppermute | solution.py:44
  50.1 8.5 %collective-permute-start.4 = (bf16[16,4608]{1,0:T(8,128)(2,1)S(1)}, bf16[16,4608]{1,0:T(8,128)(2,1)S(1)}, u32[]{:S(2)}, u32[]{:S(2)}) collective-permute-start(bf16[16,4608]{1,0:T(8,128)(2,1)S(1)} %shard_map.114.refs_0_), channel_id=1, source_target_pairs={{0,2},{1,3},{2,0},{3,1},{4,6},{5,7},{8,10},{9,11},{10,8},{11,9},{1... | collective-permute-start | bytes 442376 | tf_op jit(solution)/shard_map/ppermute | solution.py:44
  54.3 9.0 %collective-permute-start.5 = (bf16[16,4608]{1,0:T(8,128)(2,1)S(1)}, bf16[16,4608]{1,0:T(8,128)(2,1)S(1)}, u32[]{:S(2)}, u32[]{:S(2)}) collective-permute-start(bf16[16,4608]{1,0:T(8,128)(2,1)S(1)} %shard_map.114.refs_0_), channel_id=1, source_target_pairs={{0,4},{1,5},{2,6},{3,7},{4,0},{5,1},{8,12},{9,13},{10,14},{11,15},... | collective-permute-start | bytes 442376 | tf_op jit(solution)/shard_map/ppermute | solution.py:44
  56.3 7.0 %collective-permute-start.6 = (bf16[16,4608]{1,0:T(8,128)(2,1)S(1)}, bf16[16,4608]{1,0:T(8,128)(2,1)S(1)}, u32[]{:S(2)}, u32[]{:S(2)}) collective-permute-start(bf16[16,4608]{1,0:T(8,128)(2,1)S(1)} %shard_map.114.refs_0_), channel_id=1, source_target_pairs={{0,6},{1,7},{2,4},{3,5},{4,2},{5,3},{8,14},{9,15},{10,12},{11,13},... | collective-permute-start | bytes 442376 | tf_op jit(solution)/shard_map/ppermute | solution.py:44
  57.6 7.9 %collective-permute-start.26 = (bf16[48,3584]{1,0:T(8,128)(2,1)S(1)}, bf16[48,3584]{1,0:T(8,128)(2,1)S(1)}, u32[]{:S(2)}, u32[]{:S(2)}) collective-permute-start(bf16[48,3584]{1,0:T(8,128)(2,1)S(1)} %collective-permute-done.24), channel_id=1, source_target_pairs={{0,8},{1,9},{2,10},{3,11},{4,12},{5,13},{6,14},{7,15},{8,0},{9,1},... | collective-permute-start | bytes 1032200 | tf_op jit(solution)/shard_map/ppermute | solution.py:44
  57.7 9.5 %collective-permute-start.29 = (bf16[48,3584]{1,0:T(8,128)(2,1)S(1)}, bf16[48,3584]{1,0:T(8,128)(2,1)S(1)}, u32[]{:S(2)}, u32[]{:S(2)}) collective-permute-start(bf16[48,3584]{1,0:T(8,128)(2,1)S(1)} %collective-permute-done.27), channel_id=1, source_target_pairs={{0,8},{1,9},{2,10},{3,11},{4,12},{5,13},{6,14},{7,15},{8,0},{9,1},... | collective-permute-start | bytes 1032200 | tf_op jit(solution)/shard_map/ppermute | solution.py:44
  58.6 9.3 %collective-permute-start.30 = (bf16[48,3584]{1,0:T(8,128)(2,1)S(1)}, bf16[48,3584]{1,0:T(8,128)(2,1)S(1)}, u32[]{:S(2)}, u32[]{:S(2)}) collective-permute-start(bf16[48,3584]{1,0:T(8,128)(2,1)S(1)} %collective-permute-done.28), channel_id=1, source_target_pairs={{0,8},{1,9},{2,10},{3,11},{4,12},{5,13},{6,14},{7,15},{8,0},{9,1},... | collective-permute-start | bytes 1032200 | tf_op jit(solution)/shard_map/ppermute | solution.py:44
  64.0 10.8 %collective-permute-start.14 = (bf16[48,2304]{1,0:T(8,128)(2,1)S(1)}, bf16[48,2304]{1,0:T(8,128)(2,1)S(1)}, u32[]{:S(2)}, u32[]{:S(2)}) collective-permute-start(bf16[48,2304]{1,0:T(8,128)(2,1)S(1)} %get-tuple-element.30), channel_id=1, source_target_pairs={{0,1},{1,0},{2,3},{3,2},{4,5},{5,4},{6,7},{7,6},{8,9},{9,8},{10,11... | collective-permute-start | bytes 663560 | tf_op jit(solution)/shard_map/ppermute | solution.py:44
  65.5 9.4 %collective-permute-start.15 = (bf16[48,2304]{1,0:T(8,128)(2,1)S(1)}, bf16[48,2304]{1,0:T(8,128)(2,1)S(1)}, u32[]{:S(2)}, u32[]{:S(2)}) collective-permute-start(bf16[48,2304]{1,0:T(8,128)(2,1)S(1)} %get-tuple-element.30), channel_id=1, source_target_pairs={{0,8},{1,9},{2,10},{3,11},{4,12},{5,13},{6,14},{7,15},{8,0},{9,1},... | collective-permute-start | bytes 663560 | tf_op jit(solution)/shard_map/ppermute | solution.py:44
  65.6 16.5 %collective-permute-start.17 = (bf16[48,2304]{1,0:T(8,128)(2,1)S(1)}, bf16[48,2304]{1,0:T(8,128)(2,1)S(1)}, u32[]{:S(2)}, u32[]{:S(2)}) collective-permute-start(bf16[48,2304]{1,0:T(8,128)(2,1)S(1)} %get-tuple-element.30), channel_id=1, source_target_pairs={{0,16},{1,17},{2,18},{3,19},{4,20},{5,21},{6,22},{7,23},{8,24},{9,... | collective-permute-start | bytes 663560 | tf_op jit(solution)/shard_map/ppermute | solution.py:44
  67.3 15.4 %collective-permute-start.18 = (bf16[48,2304]{1,0:T(8,128)(2,1)S(1)}, bf16[48,2304]{1,0:T(8,128)(2,1)S(1)}, u32[]{:S(2)}, u32[]{:S(2)}) collective-permute-start(bf16[48,2304]{1,0:T(8,128)(2,1)S(1)} %get-tuple-element.30), channel_id=1, source_target_pairs={{0,17},{1,16},{2,19},{3,18},{4,21},{5,20},{6,23},{7,22},{8,25},{9,... | collective-permute-start | bytes 663560 | tf_op jit(solution)/shard_map/ppermute | solution.py:44
  67.8 11.8 %collective-permute-start.7 = (bf16[48,2304]{1,0:T(8,128)(2,1)S(1)}, bf16[48,2304]{1,0:T(8,128)(2,1)S(1)}, u32[]{:S(2)}, u32[]{:S(2)}) collective-permute-start(bf16[48,2304]{1,0:T(8,128)(2,1)S(1)} %get-tuple-element.29), channel_id=1, source_target_pairs={{0,1},{1,0},{2,3},{3,2},{4,5},{5,4},{6,7},{7,6},{8,9},{9,8},{10,11... | collective-permute-start | bytes 663560 | tf_op jit(solution)/shard_map/ppermute | solution.py:44
  69.4 19.8 %slice-start = ((s8[9437184]{0:T(1024)(128)(4,1)}), s8[4194304]{0:T(1024)(128)(4,1)S(1)}, s32[]{:S(2)}) async-start(s8[9437184]{0:T(1024)(128)(4,1)} %bitcast.32), calls=%async_computation.1 | async-start | bytes 8388608
  69.4 19.8 %slice-start.1 = ((s8[9437184]{0:T(1024)(128)(4,1)}), s8[4194304]{0:T(1024)(128)(4,1)S(1)}, s32[]{:S(2)}) async-start(s8[9437184]{0:T(1024)(128)(4,1)} %bitcast.32), calls=%async_computation.2 | async-start | bytes 8388608
  69.4 19.8 %slice-start.2 = ((s8[9437184]{0:T(1024)(128)(4,1)}), s8[1048576]{0:T(1024)(128)(4,1)S(1)}, s32[]{:S(2)}) async-start(s8[9437184]{0:T(1024)(128)(4,1)} %bitcast.32), calls=%async_computation.3 | async-start | bytes 2097152
  74.8 7.2 %collective-permute-start.8 = (bf16[48,2304]{1,0:T(8,128)(2,1)S(1)}, bf16[48,2304]{1,0:T(8,128)(2,1)S(1)}, u32[]{:S(2)}, u32[]{:S(2)}) collective-permute-start(bf16[48,2304]{1,0:T(8,128)(2,1)S(1)} %get-tuple-element.29), channel_id=1, source_target_pairs={{0,8},{1,9},{2,10},{3,11},{4,12},{5,13},{6,14},{7,15},{8,0},{9,1},... | collective-permute-start | bytes 663560 | tf_op jit(solution)/shard_map/ppermute | solution.py:44
  74.9 12.8 %collective-permute-start.10 = (bf16[48,2304]{1,0:T(8,128)(2,1)S(1)}, bf16[48,2304]{1,0:T(8,128)(2,1)S(1)}, u32[]{:S(2)}, u32[]{:S(2)}) collective-permute-start(bf16[48,2304]{1,0:T(8,128)(2,1)S(1)} %get-tuple-element.29), channel_id=1, source_target_pairs={{0,16},{1,17},{2,18},{3,19},{4,20},{5,21},{6,22},{7,23},{8,24},{9,... | collective-permute-start | bytes 663560 | tf_op jit(solution)/shard_map/ppermute | solution.py:44
  79.6 8.1 %collective-permute-start.11 = (bf16[48,2304]{1,0:T(8,128)(2,1)S(1)}, bf16[48,2304]{1,0:T(8,128)(2,1)S(1)}, u32[]{:S(2)}, u32[]{:S(2)}) collective-permute-start(bf16[48,2304]{1,0:T(8,128)(2,1)S(1)} %get-tuple-element.29), channel_id=1, source_target_pairs={{0,17},{1,16},{2,19},{3,18},{4,21},{5,20},{6,23},{7,22},{8,25},{9,... | collective-permute-start | bytes 663560 | tf_op jit(solution)/shard_map/ppermute | solution.py:44
  82.0 6.2 %collective-permute-start.16 = (bf16[48,2304]{1,0:T(8,128)(2,1)S(1)}, bf16[48,2304]{1,0:T(8,128)(2,1)S(1)}, u32[]{:S(2)}, u32[]{:S(2)}) collective-permute-start(bf16[48,2304]{1,0:T(8,128)(2,1)S(1)} %collective-permute-done.14), channel_id=1, source_target_pairs={{0,8},{1,9},{2,10},{3,11},{4,12},{5,13},{6,14},{7,15},{8,0},{9,1},... | collective-permute-start | bytes 663560 | tf_op jit(solution)/shard_map/ppermute | solution.py:44
  82.1 9.1 %collective-permute-start.9 = (bf16[48,2304]{1,0:T(8,128)(2,1)S(1)}, bf16[48,2304]{1,0:T(8,128)(2,1)S(1)}, u32[]{:S(2)}, u32[]{:S(2)}) collective-permute-start(bf16[48,2304]{1,0:T(8,128)(2,1)S(1)} %collective-permute-done.7), channel_id=1, source_target_pairs={{0,8},{1,9},{2,10},{3,11},{4,12},{5,13},{6,14},{7,15},{8,0},{9,1},... | collective-permute-start | bytes 663560 | tf_op jit(solution)/shard_map/ppermute | solution.py:44
  82.6 5.7 %collective-permute-start.19 = (bf16[48,2304]{1,0:T(8,128)(2,1)S(1)}, bf16[48,2304]{1,0:T(8,128)(2,1)S(1)}, u32[]{:S(2)}, u32[]{:S(2)}) collective-permute-start(bf16[48,2304]{1,0:T(8,128)(2,1)S(1)} %collective-permute-done.17), channel_id=1, source_target_pairs={{0,8},{1,9},{2,10},{3,11},{4,12},{5,13},{6,14},{7,15},{8,0},{9,1},... | collective-permute-start | bytes 663560 | tf_op jit(solution)/shard_map/ppermute | solution.py:44
  87.7 1.5 collective-permute-start.20
  87.7 3.6 %collective-permute-start.12 = (bf16[48,2304]{1,0:T(8,128)(2,1)S(1)}, bf16[48,2304]{1,0:T(8,128)(2,1)S(1)}, u32[]{:S(2)}, u32[]{:S(2)}) collective-permute-start(bf16[48,2304]{1,0:T(8,128)(2,1)S(1)} %collective-permute-done.10), channel_id=1, source_target_pairs={{0,8},{1,9},{2,10},{3,11},{4,12},{5,13},{6,14},{7,15},{8,0},{9,1},... | collective-permute-start | bytes 663560 | tf_op jit(solution)/shard_map/ppermute | solution.py:44
  88.2 3.1 %collective-permute-start.13 = (bf16[48,2304]{1,0:T(8,128)(2,1)S(1)}, bf16[48,2304]{1,0:T(8,128)(2,1)S(1)}, u32[]{:S(2)}, u32[]{:S(2)}) collective-permute-start(bf16[48,2304]{1,0:T(8,128)(2,1)S(1)} %collective-permute-done.11), channel_id=1, source_target_pairs={{0,8},{1,9},{2,10},{3,11},{4,12},{5,13},{6,14},{7,15},{8,0},{9,1},... | collective-permute-start | bytes 663560 | tf_op jit(solution)/shard_map/ppermute | solution.py:44
  114.5 3.4 %collective-permute-start.38 = (bf16[192,1792]{1,0:T(8,128)(2,1)S(1)}, bf16[192,1792]{1,0:T(8,128)(2,1)S(1)}, u32[]{:S(2)}, u32[]{:S(2)}) collective-permute-start(bf16[192,1792]{1,0:T(8,128)(2,1)S(1)} %fusion.15), channel_id=1, source_target_pairs={{0,8},{1,9},{2,10},{3,11},{4,12},{5,13},{6,14},{7,15},{8,0},{9,1},... | collective-permute-start | bytes 2064392 | tf_op jit(solution)/shard_map/ppermute | solution.py:44
  116.4 7.2 %collective-permute-start.34 = (bf16[192,1792]{1,0:T(8,128)(2,1)S(1)}, bf16[192,1792]{1,0:T(8,128)(2,1)S(1)}, u32[]{:S(2)}, u32[]{:S(2)}) collective-permute-start(bf16[192,1792]{1,0:T(8,128)(2,1)S(1)} %fusion.12), channel_id=1, source_target_pairs={{0,8},{1,9},{2,10},{3,11},{4,12},{5,13},{6,14},{7,15},{8,0},{9,1},... | collective-permute-start | bytes 2064392 | tf_op jit(solution)/shard_map/ppermute | solution.py:44
  118.6 8.3 %collective-permute-start.39 = (bf16[48,1792]{1,0:T(8,128)(2,1)S(1)}, bf16[48,1792]{1,0:T(8,128)(2,1)S(1)}, u32[]{:S(2)}, u32[]{:S(2)}) collective-permute-start(bf16[48,1792]{1,0:T(8,128)(2,1)S(1)} %get-tuple-element.40), channel_id=1, source_target_pairs={{0,1},{1,0},{2,3},{3,2},{4,5},{5,4},{6,7},{7,6},{8,9},{9,8},{10,11... | collective-permute-start | bytes 516104 | tf_op jit(solution)/shard_map/ppermute | solution.py:44
  122.0 5.8 %copy-start.2 = (f32[3584]{0:T(1024)S(1)}, f32[3584]{0:T(1024)}, u32[]{:S(2)}) copy-start(f32[3584]{0:T(1024)} %param.16) | copy-start | bytes 43012
  122.0 11.2 %collective-permute-start.40 = (bf16[48,1792]{1,0:T(8,128)(2,1)S(1)}, bf16[48,1792]{1,0:T(8,128)(2,1)S(1)}, u32[]{:S(2)}, u32[]{:S(2)}) collective-permute-start(bf16[48,1792]{1,0:T(8,128)(2,1)S(1)} %get-tuple-element.41), channel_id=1, source_target_pairs={{0,16},{1,17},{2,18},{3,19},{4,20},{5,21},{6,22},{7,23},{8,24},{9,... | collective-permute-start | bytes 516104 | tf_op jit(solution)/shard_map/ppermute | solution.py:44
  122.6 32.3 %copy-start = (bf16[16,3584]{1,0:T(8,128)(2,1)S(1)}, bf16[16,3584]{1,0:T(8,128)(2,1)}, u32[]{:S(2)}) copy-start(bf16[16,3584]{1,0:T(8,128)(2,1)} %refs_3_.1) | copy-start | bytes 344068
  122.6 10.5 %collective-permute-start.41 = (bf16[48,1792]{1,0:T(8,128)(2,1)S(1)}, bf16[48,1792]{1,0:T(8,128)(2,1)S(1)}, u32[]{:S(2)}, u32[]{:S(2)}) collective-permute-start(bf16[48,1792]{1,0:T(8,128)(2,1)S(1)} %get-tuple-element.42), channel_id=1, source_target_pairs={{0,17},{1,16},{2,19},{3,18},{4,21},{5,20},{6,23},{7,22},{8,25},{9,... | collective-permute-start | bytes 516104 | tf_op jit(solution)/shard_map/ppermute | solution.py:44
  124.2 10.2 %collective-permute-start.35 = (bf16[48,1792]{1,0:T(8,128)(2,1)S(1)}, bf16[48,1792]{1,0:T(8,128)(2,1)S(1)}, u32[]{:S(2)}, u32[]{:S(2)}) collective-permute-start(bf16[48,1792]{1,0:T(8,128)(2,1)S(1)} %get-tuple-element.36), channel_id=1, source_target_pairs={{0,1},{1,0},{2,3},{3,2},{4,5},{5,4},{6,7},{7,6},{8,9},{9,8},{10,11... | collective-permute-start | bytes 516104 | tf_op jit(solution)/shard_map/ppermute | solution.py:44
  126.3 13.0 %collective-permute-start.36 = (bf16[48,1792]{1,0:T(8,128)(2,1)S(1)}, bf16[48,1792]{1,0:T(8,128)(2,1)S(1)}, u32[]{:S(2)}, u32[]{:S(2)}) collective-permute-start(bf16[48,1792]{1,0:T(8,128)(2,1)S(1)} %get-tuple-element.37), channel_id=1, source_target_pairs={{0,16},{1,17},{2,18},{3,19},{4,20},{5,21},{6,22},{7,23},{8,24},{9,... | collective-permute-start | bytes 516104 | tf_op jit(solution)/shard_map/ppermute | solution.py:44
  126.9 12.4 %collective-permute-start.37 = (bf16[48,1792]{1,0:T(8,128)(2,1)S(1)}, bf16[48,1792]{1,0:T(8,128)(2,1)S(1)}, u32[]{:S(2)}, u32[]{:S(2)}) collective-permute-start(bf16[48,1792]{1,0:T(8,128)(2,1)S(1)} %get-tuple-element.38), channel_id=1, source_target_pairs={{0,17},{1,16},{2,19},{3,18},{4,21},{5,20},{6,23},{7,22},{8,25},{9,... | collective-permute-start | bytes 516104 | tf_op jit(solution)/shard_map/ppermute | solution.py:44
  140.0 7.8 %collective-permute-start.42 = (bf16[16,3584]{1,0:T(8,128)(2,1)S(1)}, bf16[16,3584]{1,0:T(8,128)(2,1)S(1)}, u32[]{:S(2)}, u32[]{:S(2)}) collective-permute-start(bf16[16,3584]{1,0:T(8,128)(2,1)S(1)} %get-tuple-element.44), channel_id=1, source_target_pairs={{0,2},{1,3},{2,0},{3,1},{6,4},{7,5},{8,10},{9,11},{10,8},{11,9},{1... | collective-permute-start | bytes 344072 | tf_op jit(solution)/shard_map/ppermute | solution.py:44
  142.3 12.7 %collective-permute-start.43 = (bf16[16,3584]{1,0:T(8,128)(2,1)S(1)}, bf16[16,3584]{1,0:T(8,128)(2,1)S(1)}, u32[]{:S(2)}, u32[]{:S(2)}) collective-permute-start(bf16[16,3584]{1,0:T(8,128)(2,1)S(1)} %get-tuple-element.45), channel_id=1, source_target_pairs={{0,4},{1,5},{4,0},{5,1},{6,2},{7,3},{8,12},{9,13},{12,8},{13,9},{1... | collective-permute-start | bytes 344072 | tf_op jit(solution)/shard_map/ppermute | solution.py:44
  144.2 10.7 %collective-permute-start.44 = (bf16[16,3584]{1,0:T(8,128)(2,1)S(1)}, bf16[16,3584]{1,0:T(8,128)(2,1)S(1)}, u32[]{:S(2)}, u32[]{:S(2)}) collective-permute-start(bf16[16,3584]{1,0:T(8,128)(2,1)S(1)} %get-tuple-element.46), channel_id=1, source_target_pairs={{2,4},{3,5},{4,2},{5,3},{6,0},{7,1},{10,12},{11,13},{12,10},{13,11... | collective-permute-start | bytes 344072 | tf_op jit(solution)/shard_map/ppermute | solution.py:44

commit v5 on v4

--- a/solution.py
+++ b/solution.py
@@ -293,15 +293,18 @@
 
 def chunk_kernel(live, ids, *refs):
     parts, (own, *lows) = refs[: 4 * PARTS], refs[4 * PARTS :]
-    share, width = own.shape[0], own.shape[1] // PARTS
+    share = own.shape[0]
 
     def chunk(out, slot):
         here = block_rows(jnp.minimum(slot, live - 1), share)
+        begin = 0
         for part in range(PARTS):
             base, by_x, by_y, far = parts[4 * part : 4 * part + 4]
             total = base[here, :] + by_x[here, :].astype(F32)
             total = total + by_y[here, :].astype(F32) + far[here, :].astype(F32)
-            out[:, part * width : (part + 1) * width] = total.astype(out.dtype)
+            end = begin + base.shape[1]
+            out[:, begin:end] = total.astype(out.dtype)
+            begin = end
 
     chunk(own, ids[2])
     for k, low in enumerate(lows, 1):
@@ -328,10 +331,10 @@
 
 
 def product(grads, head, part, dtype):
-    width = head.shape[0] // PARTS
+    cut = head.shape[0] * 4 // 7 // 128 * 128
     return lax.dot_general(
         grads,
-        head[part * width : (part + 1) * width],
+        head[cut:] if part else head[:cut],
         (((1,), (1,)), ((), ())),
         preferred_element_type=F32,
     ).astype(dtype)
@@ -351,7 +354,7 @@
 
 
 def reduce_depth(grid, parts, share):
-    width = PARTS * parts[0][0].shape[1]
+    width = sum([part[0].shape[1] for part in parts])
     if grid.tiled:
         summed, *lows = call(
             functools.partial(chunk_kernel, grid.live),

time: 157 us -> 159 us (1.013)
  transfers between devices with their start and end apart: 45 -> 45, of which waited for: 16 -> 13; matrix products, arithmetic and copies ran while one was open for 8% -> 8% of each run, Pallas kernels for 5% -> 5%
where the time goes in v5:
time: 159 us; the launch traced here: 158 us
  starting transfers between devices  58.4 us (37%)
  waiting for transfers between devices  50.5 us (32%)
  blocking collectives  16.4 us (10%)
  Pallas kernels  13.6 us (9%)
  matrix products  12.4 us (8%)
  other arithmetic  3 us (2%)
  local copies, waits for them, and re-layouts  2.35 us (1%)
    ppermute x45, starting transfers between devices, send(): return lax.ppermute(value, AXES, pairs)  58.4 us
    ppermute x45, waiting for transfers between devices, send(): return lax.ppermute(value, AXES, pairs)  50.5 us
    all_to_all x1, blocking collectives, shards(): got = lax.all_to_all(sent, AXES, 0, 0, tiled=True)  16.4 us
    pallas_call x13, Pallas kernels, call(): pl.pallas_call(kernel, out_shape=outs, in_specs=[SMEM] + [VMEM] * len(arg...  13.6 us
    dot_general x4, matrix products, product(): lax.dot_general(grads, head[cut:] if part else head[:cut], (((1,), (1,)),...  5.41 us
    dot_general x2, matrix products, shards(): jnp.dot(part, teacher_head[i * width:(i + 1) * width], preferred_element_...  3.97 us
  transfers between devices with their start and end apart: 45, of which 13 were waited for; matrix products, arithmetic and copies ran while one was open for 8% of the time, Pallas kernels for 5%

profile of v5, /device:TPU:0, one launch (start us, length us, event | category | flops | bytes accessed | tf_op | source)
XLA Modules:
  0.0 158.1 jit_solution(8003740049610719690)
XLA Ops:
  0.6 1.1 fusion.18
  1.7 1.0 fusion.20.refs_0_
  2.7 5.0 %collective-permute-start.21 = (bf16[16,3584]{1,0:T(8,128)(2,1)S(1)}, bf16[16,3584]{1,0:T(8,128)(2,1)S(1)}, u32[]{:S(2)}, u32[]{:S(2)}) collective-permute-start(bf16[16,3584]{1,0:T(8,128)(2,1)S(1)} %fusion.20.refs_0_), channel_id=1, source_target_pairs={{0,2},{1,3},{2,0},{3,1},{4,6},{5,7},{8,10},{9,11},{10,8},{11,9},{1... | collective-permute-start | bytes 344072 | tf_op jit(solution)/shard_map/ppermute | solution.py:44
  7.7 4.5 %collective-permute-start.22 = (bf16[16,3584]{1,0:T(8,128)(2,1)S(1)}, bf16[16,3584]{1,0:T(8,128)(2,1)S(1)}, u32[]{:S(2)}, u32[]{:S(2)}) collective-permute-start(bf16[16,3584]{1,0:T(8,128)(2,1)S(1)} %fusion.20.refs_0_), channel_id=1, source_target_pairs={{0,4},{1,5},{2,6},{3,7},{4,0},{5,1},{8,12},{9,13},{10,14},{11,15},... | collective-permute-start | bytes 344072 | tf_op jit(solution)/shard_map/ppermute | solution.py:44
  12.2 1.3 collective-permute-start.23
  13.5 0.7 pad_add_fusion
  14.2 1.6 %collective-permute-start.32 = (s32[1,136]{1,0:T(1,128)S(1)}, s32[1,136]{1,0:T(1,128)S(1)}, u32[]{:S(2)}, u32[]{:S(2)}) collective-permute-start(s32[1,136]{1,0:T(1,128)S(1)} %bitcast.27), channel_id=1, source_target_pairs={{0,16},{1,17},{2,18},{3,19},{4,20},{5,21},{6,22},{7,23},{8,24},{9,... | collective-permute-start | bytes 1640 | tf_op jit(solution)/shard_map/ppermute | solution.py:44
  15.8 1.2 dynamic-slice_bitcast_fusion
  17.8 1.5 collective-permute-start
  19.3 0.9 collective-permute-done.33.refs_3_
  20.2 1.1 shard_map.117
  21.3 0.7 shard_map.116
  22.0 1.6 collective-permute-start.24
  24.1 6.8 %collective-permute-done.other = bf16[3,16,4608]{2,1,0:T(8,128)(2,1)S(1)} collective-permute-done((bf16[3,16,4608]{2,1,0:T(8,128)(2,1)S(1)}, bf16[3,16,4608]{2,1,0:T(8,128)(2,1)S(1)}, u32[]{:S(2)}, u32[]{:S(2)}) %collective-permute-start) | collective-permute-done | bytes 442400 | tf_op jit(solution)/shard_map/ppermute | solution.py:44
  30.9 0.7 shard_map.113
  31.6 3.4 %collective-permute-start.1 = (bf16[16,4608]{1,0:T(8,128)(2,1)S(1)}, bf16[16,4608]{1,0:T(8,128)(2,1)S(1)}, u32[]{:S(2)}, u32[]{:S(2)}) collective-permute-start(bf16[16,4608]{1,0:T(8,128)(2,1)S(1)} %get-tuple-element.26), channel_id=1, source_target_pairs={{0,2},{1,3},{2,0},{3,1},{6,4},{7,5},{8,10},{9,11},{10,8},{11,9},{1... | collective-permute-start | bytes 442376 | tf_op jit(solution)/shard_map/ppermute | solution.py:44
  35.0 1.9 %collective-permute-start.2 = (bf16[16,4608]{1,0:T(8,128)(2,1)S(1)}, bf16[16,4608]{1,0:T(8,128)(2,1)S(1)}, u32[]{:S(2)}, u32[]{:S(2)}) collective-permute-start(bf16[16,4608]{1,0:T(8,128)(2,1)S(1)} %get-tuple-element.27), channel_id=1, source_target_pairs={{0,4},{1,5},{4,0},{5,1},{6,2},{7,3},{8,12},{9,13},{12,8},{13,9},{1... | collective-permute-start | bytes 442376 | tf_op jit(solution)/shard_map/ppermute | solution.py:44
  37.3 1.3 collective-permute-start.3
  38.8 2.4 %collective-permute-start.28 = (bf16[48,3584]{1,0:T(8,128)(2,1)S(1)}, bf16[48,3584]{1,0:T(8,128)(2,1)S(1)}, u32[]{:S(2)}, u32[]{:S(2)}) collective-permute-start(bf16[48,3584]{1,0:T(8,128)(2,1)S(1)} %shard_map.116), channel_id=1, source_target_pairs={{0,17},{1,16},{2,19},{3,18},{4,21},{5,20},{6,23},{7,22},{8,25},{9,... | collective-permute-start | bytes 1032200 | tf_op jit(solution)/shard_map/ppermute | solution.py:44
  41.3 7.9 %collective-permute-done.2.refs_2_ = bf16[16,4608]{1,0:T(8,128)(2,1)S(1)} collective-permute-done((bf16[16,4608]{1,0:T(8,128)(2,1)S(1)}, bf16[16,4608]{1,0:T(8,128)(2,1)S(1)}, u32[]{:S(2)}, u32[]{:S(2)}) %collective-permute-start.2) | collective-permute-done | bytes 147488 | tf_op jit(solution)/shard_map/ppermute | solution.py:44
  49.2 0.8 shard_map.114.refs_0_
  50.1 4.3 %collective-permute-start.4 = (bf16[16,4608]{1,0:T(8,128)(2,1)S(1)}, bf16[16,4608]{1,0:T(8,128)(2,1)S(1)}, u32[]{:S(2)}, u32[]{:S(2)}) collective-permute-start(bf16[16,4608]{1,0:T(8,128)(2,1)S(1)} %shard_map.114.refs_0_), channel_id=1, source_target_pairs={{0,2},{1,3},{2,0},{3,1},{4,6},{5,7},{8,10},{9,11},{10,8},{11,9},{1... | collective-permute-start | bytes 442376 | tf_op jit(solution)/shard_map/ppermute | solution.py:44
  54.3 1.9 %collective-permute-start.5 = (bf16[16,4608]{1,0:T(8,128)(2,1)S(1)}, bf16[16,4608]{1,0:T(8,128)(2,1)S(1)}, u32[]{:S(2)}, u32[]{:S(2)}) collective-permute-start(bf16[16,4608]{1,0:T(8,128)(2,1)S(1)} %shard_map.114.refs_0_), channel_id=1, source_target_pairs={{0,4},{1,5},{2,6},{3,7},{4,0},{5,1},{8,12},{9,13},{10,14},{11,15},... | collective-permute-start | bytes 442376 | tf_op jit(solution)/shard_map/ppermute | solution.py:44
  56.3 1.3 collective-permute-start.6
  58.6 4.7 %collective-permute-done.5.refs_2_ = bf16[16,4608]{1,0:T(8,128)(2,1)S(1)} collective-permute-done((bf16[16,4608]{1,0:T(8,128)(2,1)S(1)}, bf16[16,4608]{1,0:T(8,128)(2,1)S(1)}, u32[]{:S(2)}, u32[]{:S(2)}) %collective-permute-start.5) | collective-permute-done | bytes 147488 | tf_op jit(solution)/shard_map/ppermute | solution.py:44
  63.3 0.7 shard_map.115
  64.0 1.6 collective-permute-start.14
  65.6 1.6 %collective-permute-start.17 = (bf16[48,2304]{1,0:T(8,128)(2,1)S(1)}, bf16[48,2304]{1,0:T(8,128)(2,1)S(1)}, u32[]{:S(2)}, u32[]{:S(2)}) collective-permute-start(bf16[48,2304]{1,0:T(8,128)(2,1)S(1)} %get-tuple-element.30), channel_id=1, source_target_pairs={{0,16},{1,17},{2,18},{3,19},{4,20},{5,21},{6,22},{7,23},{8,24},{9,... | collective-permute-start | bytes 663560 | tf_op jit(solution)/shard_map/ppermute | solution.py:44
  67.3 0.5 collective-permute-start.18
  67.8 1.6 collective-permute-start.7
  69.5 3.0 %fusion.21.logits.s_logits = f32[384,1024]{1,0:T(8,128)S(1)} fusion(bf16[384,3584]{1,0:T(8,128)(2,1)S(1)} %constant_dynamic-update-slice_fusion.16, bf16[3584,1024]{1,0:T(8,128)(2,1)S(1)} %copy-done.5), kind=kOutput, calls=%fused_computation.48 | convolution fusion | flops 2818572288 | bytes 11665408 | tf_op jit(solution)/shard_map/dot_general | solution.py:496
  72.5 2.3 %shard_map.118.s_cols = f32[384,128]{1,0:T(8,128)S(1)} custom-call(s32[5]{0:T(128)S(1)} %stack.23.ids, f32[384,1024]{1,0:T(8,128)S(1)} %fusion.21.logits.s_logits, s32[384,1]{1,0:T(8,128)S(1)} %get-tuple-element.31.labels), custom_call_target="tpu_custom_call" | custom-call | tf_op jit(solution)/shard_map/pallas_call | solution.py:76
  74.9 1.6 %collective-permute-start.10 = (bf16[48,2304]{1,0:T(8,128)(2,1)S(1)}, bf16[48,2304]{1,0:T(8,128)(2,1)S(1)}, u32[]{:S(2)}, u32[]{:S(2)}) collective-permute-start(bf16[48,2304]{1,0:T(8,128)(2,1)S(1)} %get-tuple-element.29), channel_id=1, source_target_pairs={{0,16},{1,17},{2,18},{3,19},{4,20},{5,21},{6,22},{7,23},{8,24},{9,... | collective-permute-start | bytes 663560 | tf_op jit(solution)/shard_map/ppermute | solution.py:44
  76.5 3.1 %collective-permute-done.7 = bf16[48,2304]{1,0:T(8,128)(2,1)S(1)} collective-permute-done((bf16[48,2304]{1,0:T(8,128)(2,1)S(1)}, bf16[48,2304]{1,0:T(8,128)(2,1)S(1)}, u32[]{:S(2)}, u32[]{:S(2)}) %collective-permute-start.7) | collective-permute-done | bytes 221216 | tf_op jit(solution)/shard_map/ppermute | solution.py:44
  79.6 2.3 %collective-permute-start.11 = (bf16[48,2304]{1,0:T(8,128)(2,1)S(1)}, bf16[48,2304]{1,0:T(8,128)(2,1)S(1)}, u32[]{:S(2)}, u32[]{:S(2)}) collective-permute-start(bf16[48,2304]{1,0:T(8,128)(2,1)S(1)} %get-tuple-element.29), channel_id=1, source_target_pairs={{0,17},{1,16},{2,19},{3,18},{4,21},{5,20},{6,23},{7,22},{8,25},{9,... | collective-permute-start | bytes 663560 | tf_op jit(solution)/shard_map/ppermute | solution.py:44
  82.1 0.6 collective-permute-start.9
  82.7 5.0 %collective-permute-done.10 = bf16[48,2304]{1,0:T(8,128)(2,1)S(1)} collective-permute-done((bf16[48,2304]{1,0:T(8,128)(2,1)S(1)}, bf16[48,2304]{1,0:T(8,128)(2,1)S(1)}, u32[]{:S(2)}, u32[]{:S(2)}) %collective-permute-start.10) | collective-permute-done | bytes 221216 | tf_op jit(solution)/shard_map/ppermute | solution.py:44
  87.7 0.5 collective-permute-start.12
  88.4 0.8 collective-permute-done.20
  89.2 2.0 %fusion = f32[384,1024]{1,0:T(8,128)S(1)} fusion(bf16[384,2304]{1,0:T(8,128)(2,1)S(1)} %constant_dynamic-update-slice_fusion.8, bf16[4608,1024]{1,0:T(8,128)(2,1)S(1)} %bitcast.33), kind=kOutput, calls=%fused_computation | convolution fusion | flops 1811939328 | bytes 8060928 | tf_op jit(solution)/shard_map/dot_general | solution.py:503
  91.4 2.0 %fusion.2 = f32[384,1024]{1,0:T(8,128)S(1)} fusion(bf16[384,2304]{1,0:T(8,128)(2,1)S(1)} %constant_dynamic-update-slice_fusion, bf16[4608,1024]{1,0:T(8,128)(2,1)S(1)} %bitcast.33), kind=kOutput, calls=%fused_computation.2 | convolution fusion | flops 1811939328 | bytes 8060928 | tf_op jit(solution)/shard_map/dot_general | solution.py:503
  93.6 1.5 shard_map.119
  95.1 16.4 %all_to_all.5.got = f32[32,1,1536]{2,1,0:T(1,128)S(1)} all-to-all(f32[32,1,1536]{2,1,0:T(1,128)S(1)} %shard_map.119), channel_id=1, replica_groups=mesh['dp'=4,'tp'=8] {'dp','tp'}, dimensions={0} | all-to-all | bytes 393216 | tf_op jit(solution)/shard_map/all_to_all | solution.py:517
  111.6 1.6 shard_map.120
  113.1 1.2 fusion.12
  114.8 1.5 fusion.15
  116.5 1.2 fusion.10.kept
  117.7 0.7 shard_map.122
  118.4 2.1 %collective-permute-start.39 = (bf16[48,1536]{1,0:T(8,128)(2,1)S(1)}, bf16[48,1536]{1,0:T(8,128)(2,1)S(1)}, u32[]{:S(2)}, u32[]{:S(2)}) collective-permute-start(bf16[48,1536]{1,0:T(8,128)(2,1)S(1)} %get-tuple-element.40), channel_id=1, source_target_pairs={{0,1},{1,0},{2,3},{3,2},{4,5},{5,4},{6,7},{7,6},{8,9},{9,8},{10,11... | collective-permute-start | bytes 442376 | tf_op jit(solution)/shard_map/ppermute | solution.py:44
  120.5 1.5 fusion.6.kept
  122.0 0.7 shard_map.121
  122.8 1.4 collective-permute-start.36
  124.2 2.1 %collective-permute-start.37 = (bf16[48,2048]{1,0:T(8,128)(2,1)S(1)}, bf16[48,2048]{1,0:T(8,128)(2,1)S(1)}, u32[]{:S(2)}, u32[]{:S(2)}) collective-permute-start(bf16[48,2048]{1,0:T(8,128)(2,1)S(1)} %get-tuple-element.38), channel_id=1, source_target_pairs={{0,17},{1,16},{2,19},{3,18},{4,21},{5,20},{6,23},{7,22},{8,25},{9,... | collective-permute-start | bytes 589832 | tf_op jit(solution)/shard_map/ppermute | solution.py:44
  126.3 0.5 collective-permute-start.40
  126.8 1.0 collective-permute-start.41
  127.8 0.7 shard_map.125
  128.6 11.5 %collective-permute-done.40.refs_6_ = bf16[48,1536]{1,0:T(8,128)(2,1)S(1)} collective-permute-done((bf16[48,1536]{1,0:T(8,128)(2,1)S(1)}, bf16[48,1536]{1,0:T(8,128)(2,1)S(1)}, u32[]{:S(2)}, u32[]{:S(2)}) %collective-permute-start.40) | collective-permute-done | bytes 147488 | tf_op jit(solution)/shard_map/ppermute | solution.py:44
  140.0 0.7 shard_map.123
  140.8 3.5 %collective-permute-start.42 = (bf16[16,3584]{1,0:T(8,128)(2,1)S(1)}, bf16[16,3584]{1,0:T(8,128)(2,1)S(1)}, u32[]{:S(2)}, u32[]{:S(2)}) collective-permute-start(bf16[16,3584]{1,0:T(8,128)(2,1)S(1)} %get-tuple-element.44), channel_id=1, source_target_pairs={{0,2},{1,3},{2,0},{3,1},{6,4},{7,5},{8,10},{9,11},{10,8},{11,9},{1... | collective-permute-start | bytes 344072 | tf_op jit(solution)/shard_map/ppermute | solution.py:44
  144.3 1.9 %collective-permute-start.43 = (bf16[16,3584]{1,0:T(8,128)(2,1)S(1)}, bf16[16,3584]{1,0:T(8,128)(2,1)S(1)}, u32[]{:S(2)}, u32[]{:S(2)}) collective-permute-start(bf16[16,3584]{1,0:T(8,128)(2,1)S(1)} %get-tuple-element.45), channel_id=1, source_target_pairs={{0,4},{1,5},{4,0},{5,1},{6,2},{7,3},{8,12},{9,13},{12,8},{13,9},{1... | collective-permute-start | bytes 344072 | tf_op jit(solution)/shard_map/ppermute | solution.py:44
  146.2 1.3 collective-permute-start.44
  147.5 0.5 slice_bitcast_fusion
  148.0 8.7 %collective-permute-done.43.refs_1_ = bf16[16,3584]{1,0:T(8,128)(2,1)S(1)} collective-permute-done((bf16[16,3584]{1,0:T(8,128)(2,1)S(1)}, bf16[16,3584]{1,0:T(8,128)(2,1)S(1)}, u32[]{:S(2)}, u32[]{:S(2)}) %collective-permute-start.43) | collective-permute-done | bytes 114720 | tf_op jit(solution)/shard_map/ppermute | solution.py:44
  156.7 1.4 shard_map.124
  (100 shorter events, 4.6 us)
Async XLA Ops:
  0.6 16.4 %copy-start.3 = (f32[4608]{0:T(1024)S(1)}, f32[4608]{0:T(1024)}, u32[]{:S(2)}) copy-start(f32[4608]{0:T(1024)} %param.12) | copy-start | bytes 55300
  0.6 16.4 %copy-start.4 = (f32[4608]{0:T(1024)S(1)}, f32[4608]{0:T(1024)}, u32[]{:S(2)}) copy-start(f32[4608]{0:T(1024)} %param.13) | copy-start | bytes 55300
  2.7 18.6 %collective-permute-start.21 = (bf16[16,3584]{1,0:T(8,128)(2,1)S(1)}, bf16[16,3584]{1,0:T(8,128)(2,1)S(1)}, u32[]{:S(2)}, u32[]{:S(2)}) collective-permute-start(bf16[16,3584]{1,0:T(8,128)(2,1)S(1)} %fusion.20.refs_0_), channel_id=1, source_target_pairs={{0,2},{1,3},{2,0},{3,1},{4,6},{5,7},{8,10},{9,11},{10,8},{11,9},{1... | collective-permute-start | bytes 344072 | tf_op jit(solution)/shard_map/ppermute | solution.py:44
  7.7 13.6 %collective-permute-start.22 = (bf16[16,3584]{1,0:T(8,128)(2,1)S(1)}, bf16[16,3584]{1,0:T(8,128)(2,1)S(1)}, u32[]{:S(2)}, u32[]{:S(2)}) collective-permute-start(bf16[16,3584]{1,0:T(8,128)(2,1)S(1)} %fusion.20.refs_0_), channel_id=1, source_target_pairs={{0,4},{1,5},{2,6},{3,7},{4,0},{5,1},{8,12},{9,13},{10,14},{11,15},... | collective-permute-start | bytes 344072 | tf_op jit(solution)/shard_map/ppermute | solution.py:44
  12.2 9.1 %collective-permute-start.23 = (bf16[16,3584]{1,0:T(8,128)(2,1)S(1)}, bf16[16,3584]{1,0:T(8,128)(2,1)S(1)}, u32[]{:S(2)}, u32[]{:S(2)}) collective-permute-start(bf16[16,3584]{1,0:T(8,128)(2,1)S(1)} %fusion.20.refs_0_), channel_id=1, source_target_pairs={{0,6},{1,7},{2,4},{3,5},{4,2},{5,3},{8,14},{9,15},{10,12},{11,13},... | collective-permute-start | bytes 344072 | tf_op jit(solution)/shard_map/ppermute | solution.py:44
  14.2 2.9 %collective-permute-start.31 = (s32[1,136]{1,0:T(1,128)S(1)}, s32[1,136]{1,0:T(1,128)S(1)}, u32[]{:S(2)}, u32[]{:S(2)}) collective-permute-start(s32[1,136]{1,0:T(1,128)S(1)} %bitcast.26), channel_id=1, source_target_pairs={{0,8},{1,9},{2,10},{3,11},{4,12},{5,13},{6,14},{7,15},{8,0},{9,1},... | collective-permute-start | bytes 1640 | tf_op jit(solution)/shard_map/ppermute | solution.py:44
  14.2 3.6 %collective-permute-start.32 = (s32[1,136]{1,0:T(1,128)S(1)}, s32[1,136]{1,0:T(1,128)S(1)}, u32[]{:S(2)}, u32[]{:S(2)}) collective-permute-start(s32[1,136]{1,0:T(1,128)S(1)} %bitcast.27), channel_id=1, source_target_pairs={{0,16},{1,17},{2,18},{3,19},{4,20},{5,21},{6,22},{7,23},{8,24},{9,... | collective-permute-start | bytes 1640 | tf_op jit(solution)/shard_map/ppermute | solution.py:44
  17.0 32.2 %copy-start.1 = (bf16[16,4608]{1,0:T(8,128)(2,1)S(1)}, bf16[16,4608]{1,0:T(8,128)(2,1)}, u32[]{:S(2)}) copy-start(bf16[16,4608]{1,0:T(8,128)(2,1)} %refs_4_.1) | copy-start | bytes 442372
  17.1 3.1 %collective-permute-start.33 = (s32[1,136]{1,0:T(1,128)S(1)}, s32[1,136]{1,0:T(1,128)S(1)}, u32[]{:S(2)}, u32[]{:S(2)}) collective-permute-start(s32[1,136]{1,0:T(1,128)S(1)} %bitcast.28), channel_id=1, source_target_pairs={{0,24},{1,25},{2,26},{3,27},{4,28},{5,29},{6,30},{7,31},{8,16},{9,... | collective-permute-start | bytes 1640 | tf_op jit(solution)/shard_map/ppermute | solution.py:44
  17.8 13.0 %collective-permute-start = (bf16[3,16,4608]{2,1,0:T(8,128)(2,1)S(1)}, bf16[3,16,4608]{2,1,0:T(8,128)(2,1)S(1)}, u32[]{:S(2)}, u32[]{:S(2)}) collective-permute-start(bf16[3,16,4608]{2,1,0:T(8,128)(2,1)S(1)} %get-tuple-element.48), channel_id=1, source_target_pairs={{0,1},{1,0},{2,3},{3,2},{4,5},{5,4},{6,7},{7,6},{8,9},{9,8},{10,11... | collective-permute-start | bytes 1327112 | tf_op jit(solution)/shard_map/ppermute | solution.py:44
  22.0 15.3 %collective-permute-start.24 = (bf16[48,3584]{1,0:T(8,128)(2,1)S(1)}, bf16[48,3584]{1,0:T(8,128)(2,1)S(1)}, u32[]{:S(2)}, u32[]{:S(2)}) collective-permute-start(bf16[48,3584]{1,0:T(8,128)(2,1)S(1)} %shard_map.116), channel_id=1, source_target_pairs={{0,1},{1,0},{2,3},{3,2},{4,5},{5,4},{6,7},{7,6},{8,9},{9,8},{10,11... | collective-permute-start | bytes 1032200 | tf_op jit(solution)/shard_map/ppermute | solution.py:44
  23.5 32.7 %collective-permute-start.25 = (bf16[48,3584]{1,0:T(8,128)(2,1)S(1)}, bf16[48,3584]{1,0:T(8,128)(2,1)S(1)}, u32[]{:S(2)}, u32[]{:S(2)}) collective-permute-start(bf16[48,3584]{1,0:T(8,128)(2,1)S(1)} %shard_map.116), channel_id=1, source_target_pairs={{0,8},{1,9},{2,10},{3,11},{4,12},{5,13},{6,14},{7,15},{8,0},{9,1},... | collective-permute-start | bytes 1032200 | tf_op jit(solution)/shard_map/ppermute | solution.py:44
  23.6 34.1 %collective-permute-start.27 = (bf16[48,3584]{1,0:T(8,128)(2,1)S(1)}, bf16[48,3584]{1,0:T(8,128)(2,1)S(1)}, u32[]{:S(2)}, u32[]{:S(2)}) collective-permute-start(bf16[48,3584]{1,0:T(8,128)(2,1)S(1)} %shard_map.116), channel_id=1, source_target_pairs={{0,16},{1,17},{2,18},{3,19},{4,20},{5,21},{6,22},{7,23},{8,24},{9,... | collective-permute-start | bytes 1032200 | tf_op jit(solution)/shard_map/ppermute | solution.py:44
  31.6 7.3 %collective-permute-start.1 = (bf16[16,4608]{1,0:T(8,128)(2,1)S(1)}, bf16[16,4608]{1,0:T(8,128)(2,1)S(1)}, u32[]{:S(2)}, u32[]{:S(2)}) collective-permute-start(bf16[16,4608]{1,0:T(8,128)(2,1)S(1)} %get-tuple-element.26), channel_id=1, source_target_pairs={{0,2},{1,3},{2,0},{3,1},{6,4},{7,5},{8,10},{9,11},{10,8},{11,9},{1... | collective-permute-start | bytes 442376 | tf_op jit(solution)/shard_map/ppermute | solution.py:44
  35.0 14.2 %collective-permute-start.2 = (bf16[16,4608]{1,0:T(8,128)(2,1)S(1)}, bf16[16,4608]{1,0:T(8,128)(2,1)S(1)}, u32[]{:S(2)}, u32[]{:S(2)}) collective-permute-start(bf16[16,4608]{1,0:T(8,128)(2,1)S(1)} %get-tuple-element.27), channel_id=1, source_target_pairs={{0,4},{1,5},{4,0},{5,1},{6,2},{7,3},{8,12},{9,13},{12,8},{13,9},{1... | collective-permute-start | bytes 442376 | tf_op jit(solution)/shard_map/ppermute | solution.py:44
  37.3 11.9 %collective-permute-start.3 = (bf16[16,4608]{1,0:T(8,128)(2,1)S(1)}, bf16[16,4608]{1,0:T(8,128)(2,1)S(1)}, u32[]{:S(2)}, u32[]{:S(2)}) collective-permute-start(bf16[16,4608]{1,0:T(8,128)(2,1)S(1)} %get-tuple-element.28), channel_id=1, source_target_pairs={{2,4},{3,5},{4,2},{5,3},{6,0},{7,1},{10,12},{11,13},{12,10},{13,11... | collective-permute-start | bytes 442376 | tf_op jit(solution)/shard_map/ppermute | solution.py:44
  38.6 30.8 %copy-start.5 = (bf16[3584,1024]{1,0:T(8,128)(2,1)S(1)}, bf16[3584,1024]{1,0:T(8,128)(2,1)}, u32[]{:S(2)}) copy-start(bf16[3584,1024]{1,0:T(8,128)(2,1)} %param.17) | copy-start | bytes 22020100
  38.8 18.9 %collective-permute-start.28 = (bf16[48,3584]{1,0:T(8,128)(2,1)S(1)}, bf16[48,3584]{1,0:T(8,128)(2,1)S(1)}, u32[]{:S(2)}, u32[]{:S(2)}) collective-permute-start(bf16[48,3584]{1,0:T(8,128)(2,1)S(1)} %shard_map.116), channel_id=1, source_target_pairs={{0,17},{1,16},{2,19},{3,18},{4,21},{5,20},{6,23},{7,22},{8,25},{9,... | collective-permute-start | bytes 1032200 | tf_op jit(solution)/shard_map/ppermute | solution.py:44
  50.1 8.5 %collective-permute-start.4 = (bf16[16,4608]{1,0:T(8,128)(2,1)S(1)}, bf16[16,4608]{1,0:T(8,128)(2,1)S(1)}, u32[]{:S(2)}, u32[]{:S(2)}) collective-permute-start(bf16[16,4608]{1,0:T(8,128)(2,1)S(1)} %shard_map.114.refs_0_), channel_id=1, source_target_pairs={{0,2},{1,3},{2,0},{3,1},{4,6},{5,7},{8,10},{9,11},{10,8},{11,9},{1... | collective-permute-start | bytes 442376 | tf_op jit(solution)/shard_map/ppermute | solution.py:44
  54.3 9.0 %collective-permute-start.5 = (bf16[16,4608]{1,0:T(8,128)(2,1)S(1)}, bf16[16,4608]{1,0:T(8,128)(2,1)S(1)}, u32[]{:S(2)}, u32[]{:S(2)}) collective-permute-start(bf16[16,4608]{1,0:T(8,128)(2,1)S(1)} %shard_map.114.refs_0_), channel_id=1, source_target_pairs={{0,4},{1,5},{2,6},{3,7},{4,0},{5,1},{8,12},{9,13},{10,14},{11,15},... | collective-permute-start | bytes 442376 | tf_op jit(solution)/shard_map/ppermute | solution.py:44
  56.3 7.0 %collective-permute-start.6 = (bf16[16,4608]{1,0:T(8,128)(2,1)S(1)}, bf16[16,4608]{1,0:T(8,128)(2,1)S(1)}, u32[]{:S(2)}, u32[]{:S(2)}) collective-permute-start(bf16[16,4608]{1,0:T(8,128)(2,1)S(1)} %shard_map.114.refs_0_), channel_id=1, source_target_pairs={{0,6},{1,7},{2,4},{3,5},{4,2},{5,3},{8,14},{9,15},{10,12},{11,13},... | collective-permute-start | bytes 442376 | tf_op jit(solution)/shard_map/ppermute | solution.py:44
  57.6 7.9 %collective-permute-start.26 = (bf16[48,3584]{1,0:T(8,128)(2,1)S(1)}, bf16[48,3584]{1,0:T(8,128)(2,1)S(1)}, u32[]{:S(2)}, u32[]{:S(2)}) collective-permute-start(bf16[48,3584]{1,0:T(8,128)(2,1)S(1)} %collective-permute-done.24), channel_id=1, source_target_pairs={{0,8},{1,9},{2,10},{3,11},{4,12},{5,13},{6,14},{7,15},{8,0},{9,1},... | collective-permute-start | bytes 1032200 | tf_op jit(solution)/shard_map/ppermute | solution.py:44
  57.7 9.5 %collective-permute-start.29 = (bf16[48,3584]{1,0:T(8,128)(2,1)S(1)}, bf16[48,3584]{1,0:T(8,128)(2,1)S(1)}, u32[]{:S(2)}, u32[]{:S(2)}) collective-permute-start(bf16[48,3584]{1,0:T(8,128)(2,1)S(1)} %collective-permute-done.27), channel_id=1, source_target_pairs={{0,8},{1,9},{2,10},{3,11},{4,12},{5,13},{6,14},{7,15},{8,0},{9,1},... | collective-permute-start | bytes 1032200 | tf_op jit(solution)/shard_map/ppermute | solution.py:44
  58.6 9.3 %collective-permute-start.30 = (bf16[48,3584]{1,0:T(8,128)(2,1)S(1)}, bf16[48,3584]{1,0:T(8,128)(2,1)S(1)}, u32[]{:S(2)}, u32[]{:S(2)}) collective-permute-start(bf16[48,3584]{1,0:T(8,128)(2,1)S(1)} %collective-permute-done.28), channel_id=1, source_target_pairs={{0,8},{1,9},{2,10},{3,11},{4,12},{5,13},{6,14},{7,15},{8,0},{9,1},... | collective-permute-start | bytes 1032200 | tf_op jit(solution)/shard_map/ppermute | solution.py:44
  64.0 10.8 %collective-permute-start.14 = (bf16[48,2304]{1,0:T(8,128)(2,1)S(1)}, bf16[48,2304]{1,0:T(8,128)(2,1)S(1)}, u32[]{:S(2)}, u32[]{:S(2)}) collective-permute-start(bf16[48,2304]{1,0:T(8,128)(2,1)S(1)} %get-tuple-element.30), channel_id=1, source_target_pairs={{0,1},{1,0},{2,3},{3,2},{4,5},{5,4},{6,7},{7,6},{8,9},{9,8},{10,11... | collective-permute-start | bytes 663560 | tf_op jit(solution)/shard_map/ppermute | solution.py:44
  65.5 9.4 %collective-permute-start.15 = (bf16[48,2304]{1,0:T(8,128)(2,1)S(1)}, bf16[48,2304]{1,0:T(8,128)(2,1)S(1)}, u32[]{:S(2)}, u32[]{:S(2)}) collective-permute-start(bf16[48,2304]{1,0:T(8,128)(2,1)S(1)} %get-tuple-element.30), channel_id=1, source_target_pairs={{0,8},{1,9},{2,10},{3,11},{4,12},{5,13},{6,14},{7,15},{8,0},{9,1},... | collective-permute-start | bytes 663560 | tf_op jit(solution)/shard_map/ppermute | solution.py:44
  65.6 16.5 %collective-permute-start.17 = (bf16[48,2304]{1,0:T(8,128)(2,1)S(1)}, bf16[48,2304]{1,0:T(8,128)(2,1)S(1)}, u32[]{:S(2)}, u32[]{:S(2)}) collective-permute-start(bf16[48,2304]{1,0:T(8,128)(2,1)S(1)} %get-tuple-element.30), channel_id=1, source_target_pairs={{0,16},{1,17},{2,18},{3,19},{4,20},{5,21},{6,22},{7,23},{8,24},{9,... | collective-permute-start | bytes 663560 | tf_op jit(solution)/shard_map/ppermute | solution.py:44
  67.3 15.4 %collective-permute-start.18 = (bf16[48,2304]{1,0:T(8,128)(2,1)S(1)}, bf16[48,2304]{1,0:T(8,128)(2,1)S(1)}, u32[]{:S(2)}, u32[]{:S(2)}) collective-permute-start(bf16[48,2304]{1,0:T(8,128)(2,1)S(1)} %get-tuple-element.30), channel_id=1, source_target_pairs={{0,17},{1,16},{2,19},{3,18},{4,21},{5,20},{6,23},{7,22},{8,25},{9,... | collective-permute-start | bytes 663560 | tf_op jit(solution)/shard_map/ppermute | solution.py:44
  67.8 11.8 %collective-permute-start.7 = (bf16[48,2304]{1,0:T(8,128)(2,1)S(1)}, bf16[48,2304]{1,0:T(8,128)(2,1)S(1)}, u32[]{:S(2)}, u32[]{:S(2)}) collective-permute-start(bf16[48,2304]{1,0:T(8,128)(2,1)S(1)} %get-tuple-element.29), channel_id=1, source_target_pairs={{0,1},{1,0},{2,3},{3,2},{4,5},{5,4},{6,7},{7,6},{8,9},{9,8},{10,11... | collective-permute-start | bytes 663560 | tf_op jit(solution)/shard_map/ppermute | solution.py:44
  69.4 19.8 %slice-start = ((s8[9437184]{0:T(1024)(128)(4,1)}), s8[4194304]{0:T(1024)(128)(4,1)S(1)}, s32[]{:S(2)}) async-start(s8[9437184]{0:T(1024)(128)(4,1)} %bitcast.32), calls=%async_computation.1 | async-start | bytes 8388608
  69.4 19.8 %slice-start.1 = ((s8[9437184]{0:T(1024)(128)(4,1)}), s8[4194304]{0:T(1024)(128)(4,1)S(1)}, s32[]{:S(2)}) async-start(s8[9437184]{0:T(1024)(128)(4,1)} %bitcast.32), calls=%async_computation.2 | async-start | bytes 8388608
  69.4 19.8 %slice-start.2 = ((s8[9437184]{0:T(1024)(128)(4,1)}), s8[1048576]{0:T(1024)(128)(4,1)S(1)}, s32[]{:S(2)}) async-start(s8[9437184]{0:T(1024)(128)(4,1)} %bitcast.32), calls=%async_computation.3 | async-start | bytes 2097152
  74.8 7.2 %collective-permute-start.8 = (bf16[48,2304]{1,0:T(8,128)(2,1)S(1)}, bf16[48,2304]{1,0:T(8,128)(2,1)S(1)}, u32[]{:S(2)}, u32[]{:S(2)}) collective-permute-start(bf16[48,2304]{1,0:T(8,128)(2,1)S(1)} %get-tuple-element.29), channel_id=1, source_target_pairs={{0,8},{1,9},{2,10},{3,11},{4,12},{5,13},{6,14},{7,15},{8,0},{9,1},... | collective-permute-start | bytes 663560 | tf_op jit(solution)/shard_map/ppermute | solution.py:44
  74.9 12.8 %collective-permute-start.10 = (bf16[48,2304]{1,0:T(8,128)(2,1)S(1)}, bf16[48,2304]{1,0:T(8,128)(2,1)S(1)}, u32[]{:S(2)}, u32[]{:S(2)}) collective-permute-start(bf16[48,2304]{1,0:T(8,128)(2,1)S(1)} %get-tuple-element.29), channel_id=1, source_target_pairs={{0,16},{1,17},{2,18},{3,19},{4,20},{5,21},{6,22},{7,23},{8,24},{9,... | collective-permute-start | bytes 663560 | tf_op jit(solution)/shard_map/ppermute | solution.py:44
  79.6 8.1 %collective-permute-start.11 = (bf16[48,2304]{1,0:T(8,128)(2,1)S(1)}, bf16[48,2304]{1,0:T(8,128)(2,1)S(1)}, u32[]{:S(2)}, u32[]{:S(2)}) collective-permute-start(bf16[48,2304]{1,0:T(8,128)(2,1)S(1)} %get-tuple-element.29), channel_id=1, source_target_pairs={{0,17},{1,16},{2,19},{3,18},{4,21},{5,20},{6,23},{7,22},{8,25},{9,... | collective-permute-start | bytes 663560 | tf_op jit(solution)/shard_map/ppermute | solution.py:44
  82.0 6.2 %collective-permute-start.16 = (bf16[48,2304]{1,0:T(8,128)(2,1)S(1)}, bf16[48,2304]{1,0:T(8,128)(2,1)S(1)}, u32[]{:S(2)}, u32[]{:S(2)}) collective-permute-start(bf16[48,2304]{1,0:T(8,128)(2,1)S(1)} %collective-permute-done.14), channel_id=1, source_target_pairs={{0,8},{1,9},{2,10},{3,11},{4,12},{5,13},{6,14},{7,15},{8,0},{9,1},... | collective-permute-start | bytes 663560 | tf_op jit(solution)/shard_map/ppermute | solution.py:44
  82.1 9.1 %collective-permute-start.9 = (bf16[48,2304]{1,0:T(8,128)(2,1)S(1)}, bf16[48,2304]{1,0:T(8,128)(2,1)S(1)}, u32[]{:S(2)}, u32[]{:S(2)}) collective-permute-start(bf16[48,2304]{1,0:T(8,128)(2,1)S(1)} %collective-permute-done.7), channel_id=1, source_target_pairs={{0,8},{1,9},{2,10},{3,11},{4,12},{5,13},{6,14},{7,15},{8,0},{9,1},... | collective-permute-start | bytes 663560 | tf_op jit(solution)/shard_map/ppermute | solution.py:44
  82.6 5.7 %collective-permute-start.19 = (bf16[48,2304]{1,0:T(8,128)(2,1)S(1)}, bf16[48,2304]{1,0:T(8,128)(2,1)S(1)}, u32[]{:S(2)}, u32[]{:S(2)}) collective-permute-start(bf16[48,2304]{1,0:T(8,128)(2,1)S(1)} %collective-permute-done.17), channel_id=1, source_target_pairs={{0,8},{1,9},{2,10},{3,11},{4,12},{5,13},{6,14},{7,15},{8,0},{9,1},... | collective-permute-start | bytes 663560 | tf_op jit(solution)/shard_map/ppermute | solution.py:44
  87.7 1.5 collective-permute-start.20
  87.7 3.6 %collective-permute-start.12 = (bf16[48,2304]{1,0:T(8,128)(2,1)S(1)}, bf16[48,2304]{1,0:T(8,128)(2,1)S(1)}, u32[]{:S(2)}, u32[]{:S(2)}) collective-permute-start(bf16[48,2304]{1,0:T(8,128)(2,1)S(1)} %collective-permute-done.10), channel_id=1, source_target_pairs={{0,8},{1,9},{2,10},{3,11},{4,12},{5,13},{6,14},{7,15},{8,0},{9,1},... | collective-permute-start | bytes 663560 | tf_op jit(solution)/shard_map/ppermute | solution.py:44
  88.2 3.1 %collective-permute-start.13 = (bf16[48,2304]{1,0:T(8,128)(2,1)S(1)}, bf16[48,2304]{1,0:T(8,128)(2,1)S(1)}, u32[]{:S(2)}, u32[]{:S(2)}) collective-permute-start(bf16[48,2304]{1,0:T(8,128)(2,1)S(1)} %collective-permute-done.11), channel_id=1, source_target_pairs={{0,8},{1,9},{2,10},{3,11},{4,12},{5,13},{6,14},{7,15},{8,0},{9,1},... | collective-permute-start | bytes 663560 | tf_op jit(solution)/shard_map/ppermute | solution.py:44
  114.3 3.4 %collective-permute-start.38 = (bf16[192,1536]{1,0:T(8,128)(2,1)S(1)}, bf16[192,1536]{1,0:T(8,128)(2,1)S(1)}, u32[]{:S(2)}, u32[]{:S(2)}) collective-permute-start(bf16[192,1536]{1,0:T(8,128)(2,1)S(1)} %fusion.12), channel_id=1, source_target_pairs={{0,8},{1,9},{2,10},{3,11},{4,12},{5,13},{6,14},{7,15},{8,0},{9,1},... | collective-permute-start | bytes 1769480 | tf_op jit(solution)/shard_map/ppermute | solution.py:44
  116.3 5.7 %collective-permute-start.34 = (bf16[192,2048]{1,0:T(8,128)(2,1)S(1)}, bf16[192,2048]{1,0:T(8,128)(2,1)S(1)}, u32[]{:S(2)}, u32[]{:S(2)}) collective-permute-start(bf16[192,2048]{1,0:T(8,128)(2,1)S(1)} %fusion.15), channel_id=1, source_target_pairs={{0,8},{1,9},{2,10},{3,11},{4,12},{5,13},{6,14},{7,15},{8,0},{9,1},... | collective-permute-start | bytes 2359304 | tf_op jit(solution)/shard_map/ppermute | solution.py:44
  118.4 8.4 %collective-permute-start.39 = (bf16[48,1536]{1,0:T(8,128)(2,1)S(1)}, bf16[48,1536]{1,0:T(8,128)(2,1)S(1)}, u32[]{:S(2)}, u32[]{:S(2)}) collective-permute-start(bf16[48,1536]{1,0:T(8,128)(2,1)S(1)} %get-tuple-element.40), channel_id=1, source_target_pairs={{0,1},{1,0},{2,3},{3,2},{4,5},{5,4},{6,7},{7,6},{8,9},{9,8},{10,11... | collective-permute-start | bytes 442376 | tf_op jit(solution)/shard_map/ppermute | solution.py:44
  122.0 5.8 %copy-start.2 = (f32[3584]{0:T(1024)S(1)}, f32[3584]{0:T(1024)}, u32[]{:S(2)}) copy-start(f32[3584]{0:T(1024)} %param.16) | copy-start | bytes 43012
  122.0 34.7 %copy-start = (bf16[16,3584]{1,0:T(8,128)(2,1)S(1)}, bf16[16,3584]{1,0:T(8,128)(2,1)}, u32[]{:S(2)}) copy-start(bf16[16,3584]{1,0:T(8,128)(2,1)} %refs_3_.1) | copy-start | bytes 344068
  122.7 17.3 %collective-permute-start.35 = (bf16[48,2048]{1,0:T(8,128)(2,1)S(1)}, bf16[48,2048]{1,0:T(8,128)(2,1)S(1)}, u32[]{:S(2)}, u32[]{:S(2)}) collective-permute-start(bf16[48,2048]{1,0:T(8,128)(2,1)S(1)} %get-tuple-element.36), channel_id=1, source_target_pairs={{0,1},{1,0},{2,3},{3,2},{4,5},{5,4},{6,7},{7,6},{8,9},{9,8},{10,11... | collective-permute-start | bytes 589832 | tf_op jit(solution)/shard_map/ppermute | solution.py:44
  122.8 17.2 %collective-permute-start.36 = (bf16[48,2048]{1,0:T(8,128)(2,1)S(1)}, bf16[48,2048]{1,0:T(8,128)(2,1)S(1)}, u32[]{:S(2)}, u32[]{:S(2)}) collective-permute-start(bf16[48,2048]{1,0:T(8,128)(2,1)S(1)} %get-tuple-element.37), channel_id=1, source_target_pairs={{0,16},{1,17},{2,18},{3,19},{4,20},{5,21},{6,22},{7,23},{8,24},{9,... | collective-permute-start | bytes 589832 | tf_op jit(solution)/shard_map/ppermute | solution.py:44
  124.2 15.8 %collective-permute-start.37 = (bf16[48,2048]{1,0:T(8,128)(2,1)S(1)}, bf16[48,2048]{1,0:T(8,128)(2,1)S(1)}, u32[]{:S(2)}, u32[]{:S(2)}) collective-permute-start(bf16[48,2048]{1,0:T(8,128)(2,1)S(1)} %get-tuple-element.38), channel_id=1, source_target_pairs={{0,17},{1,16},{2,19},{3,18},{4,21},{5,20},{6,23},{7,22},{8,25},{9,... | collective-permute-start | bytes 589832 | tf_op jit(solution)/shard_map/ppermute | solution.py:44
  126.3 13.8 %collective-permute-start.40 = (bf16[48,1536]{1,0:T(8,128)(2,1)S(1)}, bf16[48,1536]{1,0:T(8,128)(2,1)S(1)}, u32[]{:S(2)}, u32[]{:S(2)}) collective-permute-start(bf16[48,1536]{1,0:T(8,128)(2,1)S(1)} %get-tuple-element.41), channel_id=1, source_target_pairs={{0,16},{1,17},{2,18},{3,19},{4,20},{5,21},{6,22},{7,23},{8,24},{9,... | collective-permute-start | bytes 442376 | tf_op jit(solution)/shard_map/ppermute | solution.py:44
  126.8 13.2 %collective-permute-start.41 = (bf16[48,1536]{1,0:T(8,128)(2,1)S(1)}, bf16[48,1536]{1,0:T(8,128)(2,1)S(1)}, u32[]{:S(2)}, u32[]{:S(2)}) collective-permute-start(bf16[48,1536]{1,0:T(8,128)(2,1)S(1)} %get-tuple-element.42), channel_id=1, source_target_pairs={{0,17},{1,16},{2,19},{3,18},{4,21},{5,20},{6,23},{7,22},{8,25},{9,... | collective-permute-start | bytes 442376 | tf_op jit(solution)/shard_map/ppermute | solution.py:44
  140.8 7.2 %collective-permute-start.42 = (bf16[16,3584]{1,0:T(8,128)(2,1)S(1)}, bf16[16,3584]{1,0:T(8,128)(2,1)S(1)}, u32[]{:S(2)}, u32[]{:S(2)}) collective-permute-start(bf16[16,3584]{1,0:T(8,128)(2,1)S(1)} %get-tuple-element.44), channel_id=1, source_target_pairs={{0,2},{1,3},{2,0},{3,1},{6,4},{7,5},{8,10},{9,11},{10,8},{11,9},{1... | collective-permute-start | bytes 344072 | tf_op jit(solution)/shard_map/ppermute | solution.py:44
  144.3 12.4 %collective-permute-start.43 = (bf16[16,3584]{1,0:T(8,128)(2,1)S(1)}, bf16[16,3584]{1,0:T(8,128)(2,1)S(1)}, u32[]{:S(2)}, u32[]{:S(2)}) collective-permute-start(bf16[16,3584]{1,0:T(8,128)(2,1)S(1)} %get-tuple-element.45), channel_id=1, source_target_pairs={{0,4},{1,5},{4,0},{5,1},{6,2},{7,3},{8,12},{9,13},{12,8},{13,9},{1... | collective-permute-start | bytes 344072 | tf_op jit(solution)/shard_map/ppermute | solution.py:44
  146.2 10.5 %collective-permute-start.44 = (bf16[16,3584]{1,0:T(8,128)(2,1)S(1)}, bf16[16,3584]{1,0:T(8,128)(2,1)S(1)}, u32[]{:S(2)}, u32[]{:S(2)}) collective-permute-start(bf16[16,3584]{1,0:T(8,128)(2,1)S(1)} %get-tuple-element.46), channel_id=1, source_target_pairs={{2,4},{3,5},{4,2},{5,3},{6,0},{7,1},{10,12},{11,13},{12,10},{13,11... | collective-permute-start | bytes 344072 | tf_op jit(solution)/shard_map/ppermute | solution.py:44
